TPU v7x, 32 devices: a whole 2x2x4 slice. The times are simulated.
32 devices in a mesh: seq: 8 (over z, y), tensor: 4 (over x, core).
Axes of the slice: x: 2, y: 2, z: 4, core: 2. Of those that a mesh axis runs over, the one named last changes fastest.
Arguments:
- inputs: bfloat16 [2, 2048, 1536], P(None, 'seq'), may hold values from -6 to 6
- text_states: bfloat16 [2, 1536, 1536], P(None, 'seq'), may hold values from -6 to 6
- timestep_emb: float32 [2, 3, 6, 1536], replicated, may hold values from -3 to 3
- modulation: float32 [6, 1536], replicated, may hold values from -3 to 3
- attn_in: bfloat16 [3, 1536, 1536], P(None, 'seq', 'tensor'), may hold values from -0.15625 to 0.15625
- in_bias: bfloat16 [2, 3, 1536], P(None, None, 'tensor'), may hold values from -2 to 2
- norm_gains: bfloat16 [4, 1536], P(None, 'tensor'), may hold values from 0.5 to 1.5
- attn_out: bfloat16 [1536, 1536], P('tensor', 'seq'), may hold values from -0.625 to 0.625
- cross_in: bfloat16 [3, 1536, 1536], P(None, 'seq', 'tensor'), may hold values from -0.15625 to 0.15625
- cross_out: bfloat16 [1536, 1536], P('tensor', 'seq'), may hold values from -0.625 to 0.625
- cross_norm_gain: bfloat16 [1536], replicated, may hold values from 0.5 to 1.5
- cross_norm_bias: bfloat16 [1536], replicated, may hold values from -2 to 2
- ffn_in: bfloat16 [1536, 8960], P('seq', 'tensor'), may hold values from -0.15625 to 0.15625
- ffn_bias: bfloat16 [8960], P('tensor'), may hold values from -2 to 2
- ffn_out: bfloat16 [8960, 1536], P('tensor', 'seq'), may hold values from -0.0625 to 0.0625
- out_bias: bfloat16 [3, 1536], replicated, may hold values from -2 to 2
- latent_ids: int32 [2, 2048], P(None, 'seq'), may hold values from 0 to 2, never falling along the last dimension, each value on 1 to 1536 neighbouring positions
- pad_mask: int32 [2, 2048], P(None, 'seq'), may hold values 0 or 1
- frame_pos: int32 [2, 2048], P(None, 'seq'), may hold values from 0 to 7
- row_pos: int32 [2, 2048], P(None, 'seq'), may hold values from 0 to 14
- col_pos: int32 [2, 2048], P(None, 'seq'), may hold values from 0 to 25
- cotangent: bfloat16 [2, 2048, 1536], P(None, 'seq'), may hold values from -6 to 6
Outputs:
- block_out: bfloat16 [2, 2048, 1536], P(None, 'seq')
- grad_inputs: float32 [2, 2048, 1536], P(None, 'seq')
- grad_text: float32 [2, 1536, 1536], P(None, 'seq')
- grad_timestep: float32 [2, 3, 6, 1536], replicated
- grad_modulation: float32 [6, 1536], replicated
- grad_attn_in: float32 [3, 1536, 1536], P(None, 'seq', 'tensor')
- grad_in_bias: float32 [2, 3, 1536], P(None, None, 'tensor')
- grad_norm_gains: float32 [4, 1536], P(None, 'tensor')
- grad_attn_out: float32 [1536, 1536], P('tensor', 'seq')
- grad_cross_in: float32 [3, 1536, 1536], P(None, 'seq', 'tensor')
- grad_cross_out: float32 [1536, 1536], P('tensor', 'seq')
- grad_cross_gain: float32 [1536], replicated
- grad_cross_bias: float32 [1536], replicated
- grad_ffn_in: float32 [1536, 8960], P('seq', 'tensor')
- grad_ffn_bias: float32 [8960], P('tensor')
- grad_ffn_out: float32 [8960, 1536], P('tensor', 'seq')
- grad_out_bias: float32 [3, 1536], replicated
Inputs may be any that keep to these rules, and one draw needn't show every extreme that they name: `latent_ids`: within each micro-batch the latent numbers never fall along the tokens; every latent has 1 to 1536 tokens and one has exactly 1536.
All inputs are finite; a program needn't handle non-finite values. No bound on the sum of `pad_mask` on one device may be relied on, other than what follows from the above.
Results may differ from a plain program's by a relative error of at most 0.025.
Values may be sent and summed in bfloat16 or wider, within the bound.
No kernel may reach another device: no remote copies, remote signals or barrier semaphores. Data moves between devices by JAX's collectives and lax.ppermute only.
A program may use at most 256 MiB of HBM per device.

v0:
```python
from functools import partial
import math

import jax
import jax.numpy as jnp
from jax import lax
from jax.sharding import PartitionSpec as P

HD = 128
TXT = 512


EPS = 1e-06
HIGH = lax.Precision.HIGHEST
NEG = -1e30


def norm_plain(values):
    center = values - jnp.mean(values, -1, keepdims=True)
    return center * lax.rsqrt(jnp.mean(center * center, -1, keepdims=True) + EPS)


def norm_back(values, cotangent):
    center = values - jnp.mean(values, -1, keepdims=True)
    inverse = lax.rsqrt(jnp.mean(center * center, -1, keepdims=True) + EPS)
    normed = center * inverse
    return inverse * (
        cotangent
        - jnp.mean(cotangent, -1, keepdims=True)
        - normed * jnp.mean(cotangent * normed, -1, keepdims=True)
    )


def rope_tables(frames, rows_pos, cols_pos, head_width):
    part_size = head_width // 6
    widths = (head_width - 4 * part_size, 2 * part_size, 2 * part_size)
    angles = []
    for position, group_width in zip((frames, rows_pos, cols_pos), widths):
        exponent = jnp.arange(0, group_width, 2).astype(jnp.float32) / group_width
        angles.append(
            position.astype(jnp.float32)[:, None] * jnp.power(10000.0, -exponent)[None, :]
        )
    joined = jnp.concatenate(angles, -1)
    return (jnp.cos(joined), jnp.sin(joined))


def rotate(values, cosine, sine):
    shape = values.shape
    pairs = values.reshape(shape[:-1] + (shape[-1] // 2, 2))
    first = pairs[..., 0]
    second = pairs[..., 1]
    cosine = cosine[:, None, :]
    sine = sine[:, None, :]
    return jnp.stack((first * cosine - second * sine, first * sine + second * cosine), -1).reshape(
        shape
    )


def keep_state(state):
    return state


def permitted(query_group, query_index, key_group, key_keep, key_index):
    same_latent = query_group[:, None] == key_group[None, :]
    return same_latent & ((key_keep[None, :] == 1) | (query_index[:, None] == key_index[None, :]))


def slice_rows(array, offset, length, axis_num):
    return lax.dynamic_slice_in_dim(array, offset, length, axis_num)


def attend_forward(
    queries, query_group, query_index, key_rows, value_rows, key_group, key_keep, block_rows
):
    factor = 1.0 / math.sqrt(queries.shape[2])
    blocks = key_rows.shape[0] // block_rows

    def fetch(number):
        offset = number * block_rows
        mask_here = permitted(
            query_group,
            query_index,
            slice_rows(key_group, offset, block_rows, 0),
            slice_rows(key_keep, offset, block_rows, 0),
            offset + jnp.arange(block_rows, dtype=jnp.int32),
        )
        return (
            slice_rows(key_rows, offset, block_rows, 0),
            slice_rows(value_rows, offset, block_rows, 0),
            mask_here,
        )

    def first_pass(carry, number):
        key_block, value_block, mask_here = fetch(number)

        def update(state):
            running, totals = state
            scores = jnp.where(
                mask_here[None],
                jnp.einsum("qhd,khd->hqk", queries, key_block, preferred_element_type=jnp.float32)
                * factor,
                NEG,
            )
            newest = jnp.maximum(running, jnp.max(scores, -1))
            weights = jnp.where(mask_here[None], jnp.exp(scores - newest[..., None]), 0.0)
            return (newest, totals * jnp.exp(running - newest) + jnp.sum(weights, -1))

        return (lax.cond(jnp.any(mask_here), update, keep_state, carry), None)

    heads_here = queries.shape[1]
    rows_here = queries.shape[0]
    start_state = (
        jnp.full((heads_here, rows_here), NEG, jnp.float32),
        jnp.zeros((heads_here, rows_here), jnp.float32),
    )
    (running, totals), _ = lax.scan(first_pass, start_state, jnp.arange(blocks))
    log_total = running + jnp.log(totals)

    def second_pass(carry, number):
        key_block, value_block, mask_here = fetch(number)

        def update(output):
            scores = (
                jnp.einsum("qhd,khd->hqk", queries, key_block, preferred_element_type=jnp.float32)
                * factor
            )
            soft_rows = jnp.where(
                mask_here[None], jnp.exp(scores - log_total[..., None]), 0.0
            ).astype(jnp.bfloat16)
            return output + jnp.einsum(
                "hqk,khd->qhd", soft_rows, value_block, preferred_element_type=jnp.float32
            )

        return (lax.cond(jnp.any(mask_here), update, keep_state, carry), None)

    output, _ = lax.scan(second_pass, jnp.zeros(queries.shape, jnp.float32), jnp.arange(blocks))
    return (output, log_total)


def grad_queries(
    queries,
    grad_out,
    log_total,
    delta_rows,
    query_group,
    query_index,
    key_rows,
    value_rows,
    key_group,
    key_keep,
    block_rows,
):
    factor = 1.0 / math.sqrt(queries.shape[2])
    blocks = key_rows.shape[0] // block_rows

    def scan_step(carry, number):
        offset = number * block_rows
        key_block = slice_rows(key_rows, offset, block_rows, 0)
        value_block = slice_rows(value_rows, offset, block_rows, 0)
        mask_here = permitted(
            query_group,
            query_index,
            slice_rows(key_group, offset, block_rows, 0),
            slice_rows(key_keep, offset, block_rows, 0),
            offset + jnp.arange(block_rows, dtype=jnp.int32),
        )

        def update(result):
            scores = (
                jnp.einsum("qhd,khd->hqk", queries, key_block, preferred_element_type=jnp.float32)
                * factor
            )
            soft_rows = jnp.where(mask_here[None], jnp.exp(scores - log_total[..., None]), 0.0)
            dprobs = jnp.einsum(
                "qhd,khd->hqk", grad_out, value_block, preferred_element_type=jnp.float32
            )
            dscore = (soft_rows * (dprobs - delta_rows[..., None])).astype(jnp.bfloat16)
            return result + jnp.einsum(
                "hqk,khd->qhd", dscore, key_block, preferred_element_type=jnp.float32
            )

        return (lax.cond(jnp.any(mask_here), update, keep_state, carry), None)

    result, _ = lax.scan(scan_step, jnp.zeros(queries.shape, jnp.float32), jnp.arange(blocks))
    return result * factor


def grad_keys(
    key_rows,
    value_rows,
    key_group,
    key_keep,
    key_index,
    queries,
    grad_out,
    log_total,
    delta_rows,
    query_group,
    query_index,
    block_rows,
):
    factor = 1.0 / math.sqrt(queries.shape[2])
    blocks = queries.shape[0] // block_rows

    def scan_step(carry, number):
        offset = number * block_rows
        query_block = slice_rows(queries, offset, block_rows, 0)
        grad_block = slice_rows(grad_out, offset, block_rows, 0)
        total_block = slice_rows(log_total, offset, block_rows, 1)
        delta_block = slice_rows(delta_rows, offset, block_rows, 1)
        mask_here = permitted(
            slice_rows(query_group, offset, block_rows, 0),
            slice_rows(query_index, offset, block_rows, 0),
            key_group,
            key_keep,
            key_index,
        )

        def update(state):
            grad_key, grad_value = state
            scores = (
                jnp.einsum(
                    "qhd,khd->hqk", query_block, key_rows, preferred_element_type=jnp.float32
                )
                * factor
            )
            soft_rows = jnp.where(mask_here[None], jnp.exp(scores - total_block[..., None]), 0.0)
            dprobs = jnp.einsum(
                "qhd,khd->hqk", grad_block, value_rows, preferred_element_type=jnp.float32
            )
            dscore = (soft_rows * (dprobs - delta_block[..., None])).astype(jnp.bfloat16)
            return (
                grad_key
                + jnp.einsum(
                    "hqk,qhd->khd", dscore, query_block, preferred_element_type=jnp.float32
                ),
                grad_value
                + jnp.einsum(
                    "hqk,qhd->khd",
                    soft_rows.astype(jnp.bfloat16),
                    grad_block,
                    preferred_element_type=jnp.float32,
                ),
            )

        return (lax.cond(jnp.any(mask_here), update, keep_state, carry), None)

    start_state = (jnp.zeros(key_rows.shape, jnp.float32), jnp.zeros(value_rows.shape, jnp.float32))
    (grad_key, grad_value), _ = lax.scan(scan_step, start_state, jnp.arange(blocks))
    return (grad_key * factor, grad_value)


def sum_heads(partial_rows):
    return lax.psum(partial_rows.astype(jnp.bfloat16), "tensor").astype(jnp.float32)


def head_norms(squares):
    return lax.psum(squares, "tensor")


def sum_features(partial_rows):
    return lax.psum(partial_rows.astype(jnp.bfloat16), "tensor").astype(jnp.float32)


def gather_stats(log_total, delta_rows):
    return (
        lax.all_gather(log_total, "seq", axis=1, tiled=True),
        lax.all_gather(delta_rows, "seq", axis=1, tiled=True),
    )


def gather_weights(attn_in, attn_out, cross_in, cross_out, ffn_in, ffn_out):
    return (
        lax.all_gather(attn_in, "seq", axis=1, tiled=True),
        lax.all_gather(attn_out, "seq", axis=1, tiled=True),
        lax.all_gather(cross_in, "seq", axis=1, tiled=True),
        lax.all_gather(cross_out, "seq", axis=1, tiled=True),
        lax.all_gather(ffn_in, "seq", axis=0, tiled=True),
        lax.all_gather(ffn_out, "seq", axis=1, tiled=True),
    )


def gather_again(attn_in, attn_out, cross_in, cross_out, ffn_in, ffn_out):
    return (
        lax.all_gather(attn_in, "seq", axis=1, tiled=True),
        lax.all_gather(attn_out, "seq", axis=1, tiled=True),
        lax.all_gather(cross_in, "seq", axis=1, tiled=True),
        lax.all_gather(cross_out, "seq", axis=1, tiled=True),
        lax.all_gather(ffn_in, "seq", axis=0, tiled=True),
        lax.all_gather(ffn_out, "seq", axis=1, tiled=True),
    )


def scatter_grads(grad_in, grad_out, grad_cin, grad_cout, grad_up, grad_down):
    return (
        lax.psum_scatter(
            grad_in.astype(jnp.bfloat16), "seq", scatter_dimension=1, tiled=True
        ).astype(jnp.float32),
        lax.psum_scatter(
            grad_out.astype(jnp.bfloat16), "seq", scatter_dimension=1, tiled=True
        ).astype(jnp.float32),
        lax.psum_scatter(
            grad_cin.astype(jnp.bfloat16), "seq", scatter_dimension=1, tiled=True
        ).astype(jnp.float32),
        lax.psum_scatter(
            grad_cout.astype(jnp.bfloat16), "seq", scatter_dimension=1, tiled=True
        ).astype(jnp.float32),
        lax.psum_scatter(
            grad_up.astype(jnp.bfloat16), "seq", scatter_dimension=0, tiled=True
        ).astype(jnp.float32),
        lax.psum_scatter(
            grad_down.astype(jnp.bfloat16), "seq", scatter_dimension=1, tiled=True
        ).astype(jnp.float32),
    )


def rms_backward(pre_rows, inverse, gain, cotangent, summed, width):
    scaled = inverse[:, None]
    return scaled * gain * cotangent - pre_rows * scaled * scaled * scaled * summed[:, None] / width


def shards(
    inputs,
    text_states,
    timestep_emb,
    modulation,
    attn_in,
    in_bias,
    norm_gains,
    attn_out,
    cross_in,
    cross_out,
    cross_norm_gain,
    cross_norm_bias,
    ffn_in,
    ffn_bias,
    ffn_out,
    out_bias,
    latent_ids,
    pad_mask,
    frame_pos,
    row_pos,
    col_pos,
    cotangent,
):
    micro_count, tok_rows, width = inputs.shape
    text_rows = text_states.shape[1]
    latents = timestep_emb.shape[1]
    columns = attn_in.shape[2]
    heads_here = columns // HD
    seq_size = lax.axis_size("seq")
    block_rows = min(512, tok_rows * seq_size)
    seq_place = lax.axis_index("seq")
    tok_index = seq_place * tok_rows + jnp.arange(tok_rows, dtype=jnp.int32)
    text_index = seq_place * text_rows + jnp.arange(text_rows, dtype=jnp.int32)
    text_group = text_index // TXT
    text_keep = jnp.ones((text_rows,), jnp.int32)
    ids_all, pads_all = (
        lax.all_gather(latent_ids, "seq", axis=1, tiled=True),
        lax.all_gather(pad_mask, "seq", axis=1, tiled=True),
    )
    all_index = jnp.arange(ids_all.shape[1], dtype=jnp.int32)
    text_total = text_rows * seq_size
    group_all = jnp.arange(text_total, dtype=jnp.int32) // TXT
    keep_all = jnp.ones((text_total,), jnp.int32)
    bias_in = in_bias.astype(jnp.float32)
    gains = norm_gains.astype(jnp.float32)
    bias_out = out_bias.astype(jnp.float32)
    bias_ffn = ffn_bias.astype(jnp.float32)
    cgain = cross_norm_gain.astype(jnp.float32)
    cbias = cross_norm_bias.astype(jnp.float32)
    latent_range = jnp.arange(latents, dtype=jnp.int32)
    outputs = []
    grad_input_list = []
    grad_text_list = []
    temb_grads = []
    in_bias_grads = []
    gain_grads = []
    cgain_grads = []
    cbias_grads = []
    ffn_bias_grads = []
    out_bias_grads = []
    for micro_step in range(micro_count):
        forward_weights = gather_weights(attn_in, attn_out, cross_in, cross_out, ffn_in, ffn_out)
        w_attn_in, w_attn_out, w_cross_in, w_cross_out, w_ffn_in, w_ffn_out = forward_weights
        state_in = inputs[micro_step].astype(jnp.float32)
        ids_here = latent_ids[micro_step]
        ids_full = ids_all[micro_step]
        pads_full = pads_all[micro_step]
        table = (modulation + timestep_emb[micro_step]).reshape(latents, 6 * width)
        picker = (ids_here[:, None] == latent_range[None, :]).astype(jnp.float32)
        shifts = jnp.dot(picker, table, precision=HIGH, preferred_element_type=jnp.float32).reshape(
            tok_rows, 6, width
        )
        cosine, sine = rope_tables(
            frame_pos[micro_step], row_pos[micro_step], col_pos[micro_step], HD
        )
        normed_one = norm_plain(state_in)
        act_low = (normed_one * (1.0 + shifts[:, 1]) + shifts[:, 0]).astype(jnp.bfloat16)
        projected = (
            jnp.einsum("td,sdc->stc", act_low, w_attn_in, preferred_element_type=jnp.float32)
            + bias_in[0][:, None, :]
        )
        query_pre = projected[0]
        key_pre = projected[1]
        value_low = projected[2].astype(jnp.bfloat16).reshape(tok_rows, heads_here, HD)
        inverse_qk = lax.rsqrt(
            head_norms(
                jnp.stack((jnp.sum(query_pre * query_pre, -1), jnp.sum(key_pre * key_pre, -1)))
            )
            / width
            + EPS
        )
        query_normed = query_pre * inverse_qk[0][:, None] * gains[0]
        key_normed = key_pre * inverse_qk[1][:, None] * gains[1]
        query_low = rotate(query_normed.reshape(tok_rows, heads_here, HD), cosine, sine).astype(
            jnp.bfloat16
        )
        key_low = rotate(key_normed.reshape(tok_rows, heads_here, HD), cosine, sine).astype(
            jnp.bfloat16
        )
        key_all, value_all = (
            lax.all_gather(key_low, "seq", axis=0, tiled=True),
            lax.all_gather(value_low, "seq", axis=0, tiled=True),
        )
        attn_full, total_self = attend_forward(
            query_low, ids_here, tok_index, key_all, value_all, ids_full, pads_full, block_rows
        )
        attn_low = attn_full.reshape(tok_rows, columns).astype(jnp.bfloat16)
        branch_one = (
            sum_heads(jnp.dot(attn_low, w_attn_out, preferred_element_type=jnp.float32))
            + bias_out[0]
        )
        state_one = state_in + branch_one * shifts[:, 2]
        normed_three = norm_plain(state_one)
        cross_act = (normed_three * cgain + cbias).astype(jnp.bfloat16)
        cquery_pre = (
            jnp.dot(cross_act, w_cross_in[0], preferred_element_type=jnp.float32) + bias_in[1, 0]
        )
        text_here = text_states[micro_step]
        ckey_pre = (
            jnp.dot(text_here, w_cross_in[1], preferred_element_type=jnp.float32) + bias_in[1, 1]
        )
        cvalue_low = (
            (jnp.dot(text_here, w_cross_in[2], preferred_element_type=jnp.float32) + bias_in[1, 2])
            .astype(jnp.bfloat16)
            .reshape(text_rows, heads_here, HD)
        )
        inverse_cq = lax.rsqrt(head_norms(jnp.sum(cquery_pre * cquery_pre, -1)) / width + EPS)
        inverse_ck = lax.rsqrt(head_norms(jnp.sum(ckey_pre * ckey_pre, -1)) / width + EPS)
        cquery_low = (
            (cquery_pre * inverse_cq[:, None] * gains[2])
            .astype(jnp.bfloat16)
            .reshape(tok_rows, heads_here, HD)
        )
        ckey_low = (
            (ckey_pre * inverse_ck[:, None] * gains[3])
            .astype(jnp.bfloat16)
            .reshape(text_rows, heads_here, HD)
        )
        ckey_all, cvalue_all = (
            lax.all_gather(ckey_low, "seq", axis=0, tiled=True),
            lax.all_gather(cvalue_low, "seq", axis=0, tiled=True),
        )
        cross_full, total_cross = attend_forward(
            cquery_low, ids_here, tok_index, ckey_all, cvalue_all, group_all, keep_all, TXT
        )
        cross_low = cross_full.reshape(tok_rows, columns).astype(jnp.bfloat16)
        branch_two = (
            sum_heads(jnp.dot(cross_low, w_cross_out, preferred_element_type=jnp.float32))
            + bias_out[1]
        )
        state_two = state_one + branch_two
        normed_two = norm_plain(state_two)
        ffn_act = (normed_two * (1.0 + shifts[:, 4]) + shifts[:, 3]).astype(jnp.bfloat16)
        hidden_pre = jnp.dot(ffn_act, w_ffn_in, preferred_element_type=jnp.float32) + bias_ffn
        hidden_low = jax.nn.gelu(hidden_pre, approximate=True).astype(jnp.bfloat16)
        branch_three = (
            sum_heads(jnp.dot(hidden_low, w_ffn_out, preferred_element_type=jnp.float32))
            + bias_out[2]
        )
        outputs.append((state_two + branch_three * shifts[:, 5]).astype(jnp.bfloat16))
        backward_weights = gather_again(attn_in, attn_out, cross_in, cross_out, ffn_in, ffn_out)
        back_attn_in, back_attn_out, back_cross_in, back_cross_out, back_ffn_in, back_ffn_out = (
            backward_weights
        )
        grad_top = cotangent[micro_step].astype(jnp.float32)
        grad_gate_three = grad_top * branch_three
        grad_branch_three = (grad_top * shifts[:, 5]).astype(jnp.bfloat16)
        grad_hidden = jnp.einsum(
            "td,fd->tf", grad_branch_three, back_ffn_out, preferred_element_type=jnp.float32
        )
        gelu_pull = jax.vjp(partial(jax.nn.gelu, approximate=True), hidden_pre)[1]
        grad_hidden_pre = gelu_pull(grad_hidden)[0].astype(jnp.bfloat16)
        grad_ffn_act = sum_features(
            jnp.einsum(
                "tf,df->td", grad_hidden_pre, back_ffn_in, preferred_element_type=jnp.float32
            )
        )
        grad_state_two = grad_top + norm_back(state_two, grad_ffn_act * (1.0 + shifts[:, 4]))
        grad_branch_two = grad_state_two.astype(jnp.bfloat16)
        grad_cross = (
            jnp.einsum(
                "td,cd->tc", grad_branch_two, back_cross_out, preferred_element_type=jnp.float32
            )
            .astype(jnp.bfloat16)
            .reshape(tok_rows, heads_here, HD)
        )
        delta_cross = jnp.einsum("qhd,qhd->hq", grad_cross.astype(jnp.float32), cross_full)
        cquery_all, gcross_all = (
            lax.all_gather(cquery_low, "seq", axis=0, tiled=True),
            lax.all_gather(grad_cross, "seq", axis=0, tiled=True),
        )
        total_cross_all, delta_cross_all = gather_stats(total_cross, delta_cross)
        grad_cquery = grad_queries(
            cquery_low,
            grad_cross,
            total_cross,
            delta_cross,
            ids_here,
            tok_index,
            ckey_all,
            cvalue_all,
            group_all,
            keep_all,
            TXT,
        ).reshape(tok_rows, columns)
        grad_ckey, grad_cvalue = grad_keys(
            ckey_low,
            cvalue_low,
            text_group,
            text_keep,
            text_index,
            cquery_all,
            gcross_all,
            total_cross_all,
            delta_cross_all,
            ids_full,
            all_index,
            block_rows,
        )
        grad_ckey = grad_ckey.reshape(text_rows, columns)
        sums_cquery = head_norms(jnp.sum(gains[2] * grad_cquery * cquery_pre, -1))
        sums_ckey = head_norms(jnp.sum(gains[3] * grad_ckey * ckey_pre, -1))
        gcq_low = rms_backward(
            cquery_pre, inverse_cq, gains[2], grad_cquery, sums_cquery, width
        ).astype(jnp.bfloat16)
        gck_low = rms_backward(ckey_pre, inverse_ck, gains[3], grad_ckey, sums_ckey, width).astype(
            jnp.bfloat16
        )
        gcv_low = grad_cvalue.reshape(text_rows, columns).astype(jnp.bfloat16)
        part_cross = jnp.einsum(
            "tc,dc->td", gcq_low, back_cross_in[0], preferred_element_type=jnp.float32
        )
        part_text = jnp.einsum(
            "tc,dc->td", gck_low, back_cross_in[1], preferred_element_type=jnp.float32
        ) + jnp.einsum("tc,dc->td", gcv_low, back_cross_in[2], preferred_element_type=jnp.float32)
        joined_sums = sum_features(jnp.concatenate((part_cross, part_text), 0))
        grad_cross_act = joined_sums[:tok_rows]
        grad_text_list.append(joined_sums[tok_rows:])
        grad_state_one = grad_state_two + norm_back(state_one, grad_cross_act * cgain)
        grad_gate_one = grad_state_one * branch_one
        grad_branch_one = (grad_state_one * shifts[:, 2]).astype(jnp.bfloat16)
        grad_attn = (
            jnp.einsum(
                "td,cd->tc", grad_branch_one, back_attn_out, preferred_element_type=jnp.float32
            )
            .astype(jnp.bfloat16)
            .reshape(tok_rows, heads_here, HD)
        )
        delta_self = jnp.einsum("qhd,qhd->hq", grad_attn.astype(jnp.float32), attn_full)
        query_all, gattn_all = (
            lax.all_gather(query_low, "seq", axis=0, tiled=True),
            lax.all_gather(grad_attn, "seq", axis=0, tiled=True),
        )
        total_self_all, delta_self_all = gather_stats(total_self, delta_self)
        grad_query = grad_queries(
            query_low,
            grad_attn,
            total_self,
            delta_self,
            ids_here,
            tok_index,
            key_all,
            value_all,
            ids_full,
            pads_full,
            block_rows,
        )
        grad_key, grad_value = grad_keys(
            key_low,
            value_low,
            ids_here,
            pad_mask[micro_step],
            tok_index,
            query_all,
            gattn_all,
            total_self_all,
            delta_self_all,
            ids_full,
            all_index,
            block_rows,
        )
        grad_qnorm = rotate(grad_query, cosine, -sine).reshape(tok_rows, columns)
        grad_knorm = rotate(grad_key, cosine, -sine).reshape(tok_rows, columns)
        sums_self = head_norms(
            jnp.stack(
                (
                    jnp.sum(gains[0] * grad_qnorm * query_pre, -1),
                    jnp.sum(gains[1] * grad_knorm * key_pre, -1),
                )
            )
        )
        gq_low = rms_backward(
            query_pre, inverse_qk[0], gains[0], grad_qnorm, sums_self[0], width
        ).astype(jnp.bfloat16)
        gk_low = rms_backward(
            key_pre, inverse_qk[1], gains[1], grad_knorm, sums_self[1], width
        ).astype(jnp.bfloat16)
        gv_low = grad_value.reshape(tok_rows, columns).astype(jnp.bfloat16)
        grad_proj = jnp.stack((gq_low, gk_low, gv_low))
        grad_act = sum_features(
            jnp.einsum("stc,sdc->td", grad_proj, back_attn_in, preferred_element_type=jnp.float32)
        )
        grad_input_list.append(
            grad_state_one + norm_back(state_in, grad_act * (1.0 + shifts[:, 1]))
        )
        shift_grads = jnp.stack(
            (
                grad_act,
                grad_act * normed_one,
                grad_gate_one,
                grad_ffn_act,
                grad_ffn_act * normed_two,
                grad_gate_three,
            ),
            1,
        ).reshape(tok_rows, 6 * width)
        temb_grads.append(
            jnp.einsum("tl,te->le", picker, shift_grads, precision=HIGH).reshape(latents, 6, width)
        )
        in_bias_grads.append(
            jnp.stack(
                (
                    jnp.sum(grad_proj.astype(jnp.float32), 1),
                    jnp.stack(
                        (
                            jnp.sum(gcq_low.astype(jnp.float32), 0),
                            jnp.sum(gck_low.astype(jnp.float32), 0),
                            jnp.sum(gcv_low.astype(jnp.float32), 0),
                        )
                    ),
                )
            )
        )
        gain_grads.append(
            jnp.stack(
                (
                    jnp.sum(grad_qnorm * query_pre * inverse_qk[0][:, None], 0),
                    jnp.sum(grad_knorm * key_pre * inverse_qk[1][:, None], 0),
                    jnp.sum(grad_cquery * cquery_pre * inverse_cq[:, None], 0),
                    jnp.sum(grad_ckey * ckey_pre * inverse_ck[:, None], 0),
                )
            )
        )
        cgain_grads.append(jnp.sum(grad_cross_act * normed_three, 0))
        cbias_grads.append(jnp.sum(grad_cross_act, 0))
        ffn_bias_grads.append(jnp.sum(grad_hidden_pre.astype(jnp.float32), 0))
        out_bias_grads.append(
            jnp.stack(
                (
                    jnp.sum(grad_branch_one.astype(jnp.float32), 0),
                    jnp.sum(grad_branch_two.astype(jnp.float32), 0),
                    jnp.sum(grad_branch_three.astype(jnp.float32), 0),
                )
            )
        )
        step_grads = (
            jnp.einsum("td,stc->sdc", act_low, grad_proj, preferred_element_type=jnp.float32),
            jnp.einsum("tc,td->cd", attn_low, grad_branch_one, preferred_element_type=jnp.float32),
            jnp.stack(
                (
                    jnp.einsum("td,tc->dc", cross_act, gcq_low, preferred_element_type=jnp.float32),
                    jnp.einsum("td,tc->dc", text_here, gck_low, preferred_element_type=jnp.float32),
                    jnp.einsum("td,tc->dc", text_here, gcv_low, preferred_element_type=jnp.float32),
                )
            ),
            jnp.einsum("tc,td->cd", cross_low, grad_branch_two, preferred_element_type=jnp.float32),
            jnp.einsum("td,tf->df", ffn_act, grad_hidden_pre, preferred_element_type=jnp.float32),
            jnp.einsum(
                "tf,td->fd", hidden_low, grad_branch_three, preferred_element_type=jnp.float32
            ),
        )
        if micro_step == 0:
            local_grads = step_grads
        else:
            local_grads = jax.tree.map(jnp.add, local_grads, step_grads)
    totals = scatter_grads(*local_grads)
    summed_small = (
        lax.psum(sum(in_bias_grads[1:], in_bias_grads[0]).astype(jnp.bfloat16), "seq").astype(
            jnp.float32
        ),
        lax.psum(sum(gain_grads[1:], gain_grads[0]).astype(jnp.bfloat16), "seq").astype(
            jnp.float32
        ),
        lax.psum(sum(cgain_grads[1:], cgain_grads[0]).astype(jnp.bfloat16), "seq").astype(
            jnp.float32
        ),
        lax.psum(sum(cbias_grads[1:], cbias_grads[0]).astype(jnp.bfloat16), "seq").astype(
            jnp.float32
        ),
        lax.psum(sum(ffn_bias_grads[1:], ffn_bias_grads[0]).astype(jnp.bfloat16), "seq").astype(
            jnp.float32
        ),
        lax.psum(sum(out_bias_grads[1:], out_bias_grads[0]).astype(jnp.bfloat16), "seq").astype(
            jnp.float32
        ),
        lax.psum(jnp.stack(temb_grads).astype(jnp.bfloat16), "seq").astype(jnp.float32),
    )
    grad_in_bias, grad_gains, grad_cgain, grad_cbias, grad_ffn_bias, grad_out_bias, grad_temb = (
        summed_small
    )
    grad_mod = jnp.sum(grad_temb, (0, 1))
    return (
        jnp.stack(outputs),
        jnp.stack(grad_input_list),
        jnp.stack(grad_text_list),
        grad_temb,
        grad_mod,
        totals[0],
        grad_in_bias,
        grad_gains,
        totals[1],
        totals[2],
        totals[3],
        grad_cgain,
        grad_cbias,
        totals[4],
        grad_ffn_bias,
        totals[5],
        grad_out_bias,
    )


def solution(mesh):
    placed = (
        P(None, "seq", None),
        P(None, "seq", None),
        P(),
        P(),
        P(None, "seq", "tensor"),
        P(None, None, "tensor"),
        P(None, "tensor"),
        P("tensor", "seq"),
        P(None, "seq", "tensor"),
        P("tensor", "seq"),
        P(),
        P(),
        P("seq", "tensor"),
        P("tensor"),
        P("tensor", "seq"),
        P(),
        P(None, "seq"),
        P(None, "seq"),
        P(None, "seq"),
        P(None, "seq"),
        P(None, "seq"),
        P(None, "seq", None),
    )
    return jax.shard_map(
        shards,
        mesh=mesh,
        in_specs=placed,
        out_specs=(
            P(None, "seq", None),
            P(None, "seq", None),
            P(None, "seq", None),
            P(),
            P(),
            P(None, "seq", "tensor"),
            P(None, None, "tensor"),
            P(None, "tensor"),
            P("tensor", "seq"),
            P(None, "seq", "tensor"),
            P("tensor", "seq"),
            P(),
            P(),
            P("seq", "tensor"),
            P("tensor"),
            P("tensor", "seq"),
            P(),
        ),
        check_vma=False,
    )
```

profile of v0, /device:TPU:0, one launch (start us, length us, event | category | flops | bytes accessed | tf_op | source)
XLA Modules:
  0.0 2680.0 jit_solution(12762722430975181492)
XLA Ops:
  24.8 53.4 %all-gather.23.cloned.1.call-done = bf16[3,1536,384]{2,1,0:T(8,128)(2,1)} async-done(((bf16[3,192,384]{2,1,0:T(8,128)(2,1)}), bf16[3,1536,384]{2,1,0:T(8,128)(2,1)}) %all-gather.23.cloned.1.call-update) | async-done | bytes 3538960 | tf_op jit(solution)/shard_map/all_gather | solution.py:274
  99.7 26.0 all_gather.114
  125.8 26.5 all_gather.115
  156.8 30.8 %all-gather.45.cloned.1.call-done = bf16[2048,3,128]{0,2,1:T(8,128)(2,1)} async-done(((bf16[256,3,128]{0,2,1:T(8,128)(2,1)}), bf16[2048,3,128]{0,2,1:T(8,128)(2,1)}) %all-gather.45.cloned.1.call-update) | async-done | bytes 1572880 | tf_op jit(solution)/shard_map/all_gather | solution.py:424
  190.2 20.3 while.218
  210.6 21.1 while.219
  236.4 58.6 %all-gather.31.cloned.1.call-done = bf16[3,1536,384]{2,1,0:T(8,128)(2,1)} async-done(((bf16[3,192,384]{2,1,0:T(8,128)(2,1)}), bf16[3,1536,384]{2,1,0:T(8,128)(2,1)}) %all-gather.31.cloned.1.call-update) | async-done | bytes 3538960 | tf_op jit(solution)/shard_map/all_gather | solution.py:276
  297.5 33.5 %all-reduce.22.cloned.1.call-done = bf16[256,1536]{1,0:T(8,128)(2,1)} async-done(((bf16[256,1536]{1,0:T(8,128)(2,1)}), bf16[256,1536]{1,0:T(8,128)(2,1)}) %all-reduce.22.cloned.1.call-update) | async-done | bytes 786448 | tf_op jit(solution)/shard_map/psum | solution.py:254
  348.2 36.4 %all-gather.47.cloned.1.call-done = bf16[1536,3,128]{2,0,1:T(8,128)(2,1)} async-done(((bf16[192,3,128]{2,0,1:T(8,128)(2,1)}), bf16[1536,3,128]{2,0,1:T(8,128)(2,1)}) %all-gather.47.cloned.1.call-update) | async-done | bytes 1179664 | tf_op jit(solution)/shard_map/all_gather | solution.py:462
  394.8 31.7 %all-gather.49.cloned.1.call-done = bf16[1536,3,128]{2,0,1:T(8,128)(2,1)} async-done(((bf16[192,3,128]{2,0,1:T(8,128)(2,1)}), bf16[1536,3,128]{2,0,1:T(8,128)(2,1)}) %all-gather.49.cloned.1.call-update) | async-done | bytes 1179664 | tf_op jit(solution)/shard_map/all_gather | solution.py:463
  437.8 30.8 %all-gather.37.cloned.1.call-done = bf16[384,1536]{0,1:T(8,128)(2,1)} async-done(((bf16[384,192]{0,1:T(8,128)(2,1)}), bf16[384,1536]{0,1:T(8,128)(2,1)}) %all-gather.37.cloned.1.call-update) | async-done | bytes 1179664 | tf_op jit(solution)/shard_map/all_gather | solution.py:277
  473.6 31.4 %all-reduce.24.cloned.1.call-done = bf16[256,1536]{1,0:T(8,128)(2,1)} async-done(((bf16[256,1536]{1,0:T(8,128)(2,1)}), bf16[256,1536]{1,0:T(8,128)(2,1)}) %all-reduce.24.cloned.1.call-update) | async-done | bytes 786448 | tf_op jit(solution)/shard_map/psum | solution.py:254
  513.3 102.7 %all-gather.41.cloned.1.call-done = bf16[2240,1536]{0,1:T(8,128)(2,1)} async-done(((bf16[2240,192]{0,1:T(8,128)(2,1)}), bf16[2240,1536]{0,1:T(8,128)(2,1)}) %all-gather.41.cloned.1.call-update) | async-done | bytes 6881296 | tf_op jit(solution)/shard_map/all_gather | solution.py:279
  623.5 101.5 %all-gather.39.cloned.1.call-done = bf16[1536,2240]{1,0:T(8,128)(2,1)} async-done(((bf16[192,2240]{1,0:T(8,128)(2,1)}), bf16[1536,2240]{1,0:T(8,128)(2,1)}) %all-gather.39.cloned.1.call-update) | async-done | bytes 6881296 | tf_op jit(solution)/shard_map/all_gather | solution.py:278
  740.2 32.1 %all-reduce.30.cloned.1.call-done = bf16[256,1536]{1,0:T(8,128)(2,1)} async-done(((bf16[256,1536]{1,0:T(8,128)(2,1)}), bf16[256,1536]{1,0:T(8,128)(2,1)}) %all-reduce.30.cloned.1.call-update) | async-done | bytes 786448 | tf_op jit(solution)/shard_map/psum | solution.py:262
  780.2 31.9 %all_gather.139 = f32[3,2048]{1,0:T(4,128)} all-gather(f32[3,256]{1,0:T(4,128)S(1)} %copy-done.218), channel_id=1, replica_groups=mesh['seq'=8,'tensor'=4] {'seq'}, dimensions={1}, use_global_device_ids=true | all-gather | bytes 27648 | tf_op jit(solution)/shard_map/all_gather | solution.py:267
  843.9 31.9 %all_gather.141 = f32[3,2048]{1,0:T(4,128)S(1)} all-gather(f32[3,256]{1,0:T(4,128)S(1)} %copy-done.212), channel_id=1, replica_groups=mesh['seq'=8,'tensor'=4] {'seq'}, dimensions={1}, use_global_device_ids=true | all-gather | bytes 27648 | tf_op jit(solution)/shard_map/all_gather | solution.py:268
  880.5 34.6 %while.223 = (s32[]{:T(128)}, f32[192,3,128]{2,0,1:T(8,128)S(1)}, f32[192,3,128]{2,0,1:T(8,128)}, s32[4]{0:T(128)}, s32[2048]{0:T(1024)}, /*index=5*/bf16[2048,3...) while((s32[]{:T(128)}, f32[192,3,128]{2,0,1:T(8,128)S(1)}, ...), condition=%wide.region_130.131_spmd.clone, body=%wide.region_126.130_spmd.clone.sunk | while | flops 304401408 | bytes 6829921 | solution.py:249
  932.6 40.5 %all-reduce.32.cloned.1.call-done = bf16[448,1536]{1,0:T(8,128)(2,1)} async-done(((bf16[448,1536]{1,0:T(8,128)(2,1)}), bf16[448,1536]{1,0:T(8,128)(2,1)}) %all-reduce.32.cloned.1.call-update) | async-done | bytes 1376272 | tf_op jit(solution)/shard_map/psum | solution.py:262
  985.8 34.8 %all-gather.63.cloned.1.call-done = bf16[2048,3,128]{0,2,1:T(8,128)(2,1)} async-done(((bf16[256,3,128]{0,2,1:T(8,128)(2,1)}), bf16[2048,3,128]{0,2,1:T(8,128)(2,1)}) %all-gather.63.cloned.1.call-update) | async-done | bytes 1572880 | tf_op jit(solution)/shard_map/all_gather | solution.py:573
  1023.2 32.8 %all_gather.143 = f32[3,2048]{1,0:T(4,128)} all-gather(f32[3,256]{1,0:T(4,128)S(1)} %copy-done.214), channel_id=1, replica_groups=mesh['seq'=8,'tensor'=4] {'seq'}, dimensions={1}, use_global_device_ids=true | all-gather | bytes 27648 | tf_op jit(solution)/shard_map/all_gather | solution.py:267
  1058.0 31.4 %while.224 = (s32[]{:T(128)}, f32[256,3,128]{2,0,1:T(8,128)}, s32[1,256]{1,0:T(1,128)S(1)}, s32[4]{0:T(128)S(1)}, s32[2048]{0:T(1024)}, /*index=5*/s32[2048]{0:T...) while((s32[]{:T(128)}, f32[256,3,128]{2,0,1:T(8,128)}, ...), condition=%wide.region_140.141_spmd.clone, body=%wide.region_136.140_spmd.clone.sunk | while | flops 305104128 | bytes 5791557 | solution.py:184
  1091.6 32.0 %all_gather.145 = f32[3,2048]{1,0:T(4,128)} all-gather(f32[3,256]{1,0:T(4,128)S(1)} %get-tuple-element.5629), channel_id=1, replica_groups=mesh['seq'=8,'tensor'=4] {'seq'}, dimensions={1}, use_global_device_ids=true | all-gather | bytes 27648 | tf_op jit(solution)/shard_map/all_gather | solution.py:268
  1128.1 45.4 %while.225 = (s32[]{:T(128)}, f32[256,3,128]{2,0,1:T(8,128)S(1)}, f32[256,3,128]{2,0,1:T(8,128)}, s32[4]{0:T(128)}, s32[2048]{0:T(1024)}, /*index=5*/s32[1,256]{...) while((s32[]{:T(128)}, f32[256,3,128]{2,0,1:T(8,128)S(1)}, ...), condition=%wide.region_146.147_spmd.clone, body=%wide.region_142.146_spmd.clone.sunk | while | flops 406258176 | bytes 8575869 | solution.py:249
  1207.4 25.3 all-reduce.34.cloned.1.call-done
  1256.9 43.7 %all-gather.25.cloned.1.call-done = bf16[2048,3,128]{0,2,1:T(8,128)(2,1)} async-done(((bf16[256,3,128]{0,2,1:T(8,128)(2,1)}), bf16[2048,3,128]{0,2,1:T(8,128)(2,1)}) %all-gather.25.cloned.1.call-update) | async-done | bytes 1572880 | tf_op jit(solution)/shard_map/all_gather | solution.py:423
  1303.2 23.1 while.216
  1326.3 20.1 all-gather.27.cloned.1.call-done
  1349.0 23.8 while.217
  1377.9 30.2 %all-reduce.18.cloned.1.call-done = bf16[256,1536]{1,0:T(8,128)(2,1)} async-done(((bf16[256,1536]{1,0:T(8,128)(2,1)}), bf16[256,1536]{1,0:T(8,128)(2,1)}) %all-reduce.18.cloned.1.call-update) | async-done | bytes 786448 | tf_op jit(solution)/shard_map/psum | solution.py:254
  1424.3 37.8 %all-gather.33.cloned.1.call-done = bf16[1536,3,128]{2,0,1:T(8,128)(2,1)} async-done(((bf16[192,3,128]{2,0,1:T(8,128)(2,1)}), bf16[1536,3,128]{2,0,1:T(8,128)(2,1)}) %all-gather.33.cloned.1.call-update) | async-done | bytes 1179664 | tf_op jit(solution)/shard_map/all_gather | solution.py:462
  1472.7 31.5 %all-gather.35.cloned.1.call-done = bf16[1536,3,128]{2,0,1:T(8,128)(2,1)} async-done(((bf16[192,3,128]{2,0,1:T(8,128)(2,1)}), bf16[1536,3,128]{2,0,1:T(8,128)(2,1)}) %all-gather.35.cloned.1.call-update) | async-done | bytes 1179664 | tf_op jit(solution)/shard_map/all_gather | solution.py:463
  1523.0 35.3 %all-reduce.20.cloned.1.call-done = bf16[256,1536]{1,0:T(8,128)(2,1)} async-done(((bf16[256,1536]{1,0:T(8,128)(2,1)}), bf16[256,1536]{1,0:T(8,128)(2,1)}) %all-reduce.20.cloned.1.call-update) | async-done | bytes 786448 | tf_op jit(solution)/shard_map/psum | solution.py:254
  1584.1 34.2 %all-reduce.26.cloned.1.call-done = bf16[256,1536]{1,0:T(8,128)(2,1)} async-done(((bf16[256,1536]{1,0:T(8,128)(2,1)}), bf16[256,1536]{1,0:T(8,128)(2,1)}) %all-reduce.26.cloned.1.call-update) | async-done | bytes 786448 | tf_op jit(solution)/shard_map/psum | solution.py:262
  1627.0 32.3 %all_gather.131 = f32[3,2048]{1,0:T(4,128)} all-gather(f32[3,256]{1,0:T(4,128)S(1)} %copy-done.219), channel_id=1, replica_groups=mesh['seq'=8,'tensor'=4] {'seq'}, dimensions={1}, use_global_device_ids=true | all-gather | bytes 27648 | tf_op jit(solution)/shard_map/all_gather | solution.py:267
  1670.2 32.7 %all_gather.133 = f32[3,2048]{1,0:T(4,128)} all-gather(f32[3,256]{1,0:T(4,128)} %multiply_reduce_fusion.13), channel_id=1, replica_groups=mesh['seq'=8,'tensor'=4] {'seq'}, dimensions={1}, use_global_device_ids=true | all-gather | bytes 27648 | tf_op jit(solution)/shard_map/all_gather | solution.py:268
  1704.2 16.6 while.214
  1726.4 31.9 %while.220 = (s32[]{:T(128)}, f32[192,3,128]{2,0,1:T(8,128)S(1)}, f32[192,3,128]{2,0,1:T(8,128)}, s32[4]{0:T(128)S(1)}, s32[2048]{0:T(1024)}, /*index=5*/bf16[20...) while((s32[]{:T(128)}, f32[192,3,128]{2,0,1:T(8,128)S(1)}, ...), condition=%wide.region_94.95_spmd.clone, body=%wide.region_90.94_spmd.clone.sunk | while | flops 304401408 | bytes 6829921 | solution.py:249
  1785.6 33.7 %all_gather.135 = f32[3,2048]{1,0:T(4,128)} all-gather(f32[3,256]{1,0:T(4,128)S(1)} %copy-done.216), channel_id=1, replica_groups=mesh['seq'=8,'tensor'=4] {'seq'}, dimensions={1}, use_global_device_ids=true | all-gather | bytes 27648 | tf_op jit(solution)/shard_map/all_gather | solution.py:267
  1839.0 29.9 %while.221 = (s32[]{:T(128)}, f32[256,3,128]{2,0,1:T(8,128)}, s32[1,256]{1,0:T(1,128)S(1)}, s32[4]{0:T(128)S(1)}, s32[2048]{0:T(1024)}, /*index=5*/s32[2048]{0:T...) while((s32[]{:T(128)}, f32[256,3,128]{2,0,1:T(8,128)}, ...), condition=%wide.region_104.105_spmd.clone, body=%wide.region_100.104_spmd.clone.sunk | while | flops 305104128 | bytes 5791557 | solution.py:184
  1871.2 31.9 %all_gather.137 = f32[3,2048]{1,0:T(4,128)} all-gather(f32[3,256]{1,0:T(4,128)S(1)} %get-tuple-element.5630), channel_id=1, replica_groups=mesh['seq'=8,'tensor'=4] {'seq'}, dimensions={1}, use_global_device_ids=true | all-gather | bytes 27648 | tf_op jit(solution)/shard_map/all_gather | solution.py:268
  1907.6 44.7 %while.222 = (s32[]{:T(128)}, f32[256,3,128]{2,0,1:T(8,128)S(1)}, f32[256,3,128]{2,0,1:T(8,128)}, s32[4]{0:T(128)}, s32[2048]{0:T(1024)}, /*index=5*/s32[1,256]{...) while((s32[]{:T(128)}, f32[256,3,128]{2,0,1:T(8,128)S(1)}, ...), condition=%wide.region_110.111_spmd.clone, body=%wide.region_106.110_spmd.clone.sunk | while | flops 406258176 | bytes 8575869 | solution.py:249
  2003.2 30.6 %all-reduce.38.cloned.1.call-done = (bf16[256,1536]{1,0:T(8,128)(2,1)}, bf16[256,1536]{1,0:T(8,128)(2,1)}, bf16[256,1536]{1,0:T(8,128)(2,1)}) async-done(((bf16[256,1536]{1,0:T(8,128)(2,1)}, bf16[256,1536]{1,0:T(8,128)(2,1)}, bf16[256,1536]{1,0:T(8,128)(2,1)}), (bf16[256,1536]{1,0:T(8,128)(2,1)}, bf16[256,1536]{1,0:T(8,128)(2,1)}, bf16[256,1536]{1,0:T(8,128)(2,1)})) %all-reduce.38.cloned.1.call-update) | async-done | bytes 2359312 | tf_op jit(solution)/shard_map/psum | solution.py:254
  2181.0 38.3 %all-reduce.4 = (bf16[2,3,384]{2,1,0:T(4,128)(2,1)S(1)}, bf16[4,384]{1,0:T(4,128)(2,1)S(1)}, bf16[1536]{0:T(1024)(128)(2,1)S(1)}, bf16[1536]{0:T(1024)(128)(2,1)...) all-reduce(bf16[2,3,384]{2,1,0:T(4,128)(2,1)S(1)} %fusion.407, ...), channel_id=1, replica_groups=mesh['seq'=8,'tensor'=4] {'seq'}, use_global_device_ids=true, to_apply=%region_163.164 | all-reduce | flops 13760 | bytes 55040 | tf_op jit(solution)/shard_map/psum | solution.py:700
  2244.4 78.8 %reduce-scatter.11.cloned.1.call-done = bf16[3,192,384]{2,1,0:T(8,128)(2,1)} async-done(((bf16[3,1536,384]{2,1,0:T(8,128)(2,1)}), bf16[3,192,384]{2,1,0:T(8,128)(2,1)}) %reduce-scatter.11.cloned.1.call-update) | async-done | bytes 442384 | tf_op jit(solution)/shard_map/reduce_scatter | solution.py:302
  2325.2 80.7 %reduce-scatter.19.cloned.1.call-done = bf16[192,1152]{1,0:T(8,128)(2,1)} async-done(((bf16[1536,1152]{1,0:T(8,128)(2,1)}), bf16[192,1152]{1,0:T(8,128)(2,1)}) %reduce-scatter.19.cloned.1.call-update) | async-done | bytes 442384
  2409.1 129.5 %reduce-scatter.15.cloned.1.call-done = bf16[192,2240]{1,0:T(8,128)(2,1)} async-done(((bf16[1536,2240]{1,0:T(8,128)(2,1)}), bf16[192,2240]{1,0:T(8,128)(2,1)}) %reduce-scatter.15.cloned.1.call-update) | async-done | bytes 860176 | tf_op jit(solution)/shard_map/reduce_scatter | solution.py:308
  2541.0 129.2 %reduce-scatter.17.cloned.1.call-done = bf16[2240,192]{0,1:T(8,128)(2,1)} async-done(((bf16[2240,1536]{0,1:T(8,128)(2,1)}), bf16[2240,192]{0,1:T(8,128)(2,1)}) %reduce-scatter.17.cloned.1.call-update) | async-done | bytes 860176 | tf_op jit(solution)/shard_map/reduce_scatter | solution.py:311
  (1494 shorter events, 1117.4 us)
Async XLA Ops:
  7.3 70.9 %all-gather.23.cloned.1.call-start = ((), (), s32[]{:S(2)}) async-start(), calls=%async_computation.6 | async-start | bytes 3981312 | tf_op jit(solution)/shard_map/all_gather | solution.py:274
  8.0 146.3 %all-gather.43.cloned.1.call-start = ((), (), s32[]{:S(2)}) async-start(), calls=%async_computation.18 | async-start | bytes 1769472 | tf_op jit(solution)/shard_map/all_gather | solution.py:423
  11.9 329.5 %copy-start.166 = (f32[384]{0:T(512)}, f32[384]{0:T(512)S(1)}, u32[]{:S(2)}) copy-start(f32[384]{0:T(512)S(1)} %get-tuple-element.2902) | copy-start | bytes 4612
  97.5 90.0 %all-gather.45.cloned.1.call-start = ((), (), s32[]{:S(2)}) async-start(), calls=%async_computation.19 | async-start | bytes 1769472 | tf_op jit(solution)/shard_map/all_gather | solution.py:424
  98.5 134.2 %all-gather.29.cloned.1.call-start = ((), (), s32[]{:S(2)}) async-start(), calls=%async_computation.9 | async-start | bytes 1327104 | tf_op jit(solution)/shard_map/all_gather | solution.py:275
  99.1 195.9 %all-gather.31.cloned.1.call-start = ((), (), s32[]{:S(2)}) async-start(), calls=%async_computation.11 | async-start | bytes 3981312 | tf_op jit(solution)/shard_map/all_gather | solution.py:276
  99.7 231.3 %all-reduce.22.cloned.1.call-start = ((), (), s32[]{:S(2)}) async-start(), calls=%async_computation.20 | async-start | bytes 1572864 | tf_op jit(solution)/shard_map/psum | solution.py:254
  235.6 149.0 %all-gather.47.cloned.1.call-start = ((), (), s32[]{:S(2)}) async-start(), calls=%async_computation.21 | async-start | bytes 1327104 | tf_op jit(solution)/shard_map/all_gather | solution.py:462
  235.7 97.3 %copy-start.266 = (f32[384]{0:T(512)}, f32[384]{0:T(512)S(1)}, u32[]{:S(2)}) copy-start(f32[384]{0:T(512)S(1)} %get-tuple-element.2900) | copy-start | bytes 4612
  235.7 97.6 %copy-start.264 = (f32[384]{0:T(512)}, f32[384]{0:T(512)S(1)}, u32[]{:S(2)}) copy-start(f32[384]{0:T(512)S(1)} %get-tuple-element.2899) | copy-start | bytes 4612
  235.7 107.5 %copy-start.262 = (f32[384]{0:T(512)}, f32[384]{0:T(512)S(1)}, u32[]{:S(2)}) copy-start(f32[384]{0:T(512)S(1)} %get-tuple-element.2898) | copy-start | bytes 4612
  235.7 97.6 %copy-start.170 = (f32[1536]{0:T(1024)}, f32[1536]{0:T(1024)S(1)}, u32[]{:S(2)}) copy-start(f32[1536]{0:T(1024)S(1)} %convert_element_type.686) | copy-start | bytes 18436
  235.8 97.6 %copy-start.149 = (f32[1536]{0:T(1024)}, f32[1536]{0:T(1024)S(1)}, u32[]{:S(2)}) copy-start(f32[1536]{0:T(1024)S(1)} %convert_element_type.685) | copy-start | bytes 18436
  236.4 96.5 %copy-start.160 = (f32[1536]{0:T(1024)}, f32[1536]{0:T(1024)S(1)}, u32[]{:S(2)}) copy-start(f32[1536]{0:T(1024)S(1)} %get-tuple-element.2897) | copy-start | bytes 18436
  343.1 83.4 %all-gather.49.cloned.1.call-start = ((), (), s32[]{:S(2)}) async-start(), calls=%async_computation.22 | async-start | bytes 1327104 | tf_op jit(solution)/shard_map/all_gather | solution.py:463
  345.7 122.9 %all-gather.37.cloned.1.call-start = ((), (), s32[]{:S(2)}) async-start(), calls=%async_computation.14 | async-start | bytes 1327104 | tf_op jit(solution)/shard_map/all_gather | solution.py:277
  346.4 158.5 %all-reduce.24.cloned.1.call-start = ((), (), s32[]{:S(2)}) async-start(), calls=%async_computation.23 | async-start | bytes 1572864 | tf_op jit(solution)/shard_map/psum | solution.py:254
  471.4 144.6 %all-gather.41.cloned.1.call-start = ((), (), s32[]{:S(2)}) async-start(), calls=%async_computation.17 | async-start | bytes 7962624 | tf_op jit(solution)/shard_map/all_gather | solution.py:279
  472.2 252.9 %all-gather.39.cloned.1.call-start = ((), (), s32[]{:S(2)}) async-start(), calls=%async_computation.16 | async-start | bytes 7962624 | tf_op jit(solution)/shard_map/all_gather | solution.py:278
  472.7 299.6 %all-reduce.30.cloned.1.call-start = ((), (), s32[]{:S(2)}) async-start(), calls=%async_computation.30 | async-start | bytes 1572864 | tf_op jit(solution)/shard_map/psum | solution.py:262
  506.9 267.8 %copy-start.2 = (f32[256,1536]{1,0:T(8,128)}, f32[256,1536]{1,0:T(8,128)S(1)}, u32[]{:S(2)}) copy-start(f32[256,1536]{1,0:T(8,128)S(1)} %get-tuple-element.3329) | copy-start | bytes 4718596
  739.4 80.9 %all-gather.59.cloned.1.call-start = ((), (), s32[]{:S(2)}) async-start(), calls=%async_computation.31 | async-start | bytes 1769472 | tf_op jit(solution)/shard_map/all_gather | solution.py:511
  740.0 136.6 %all-gather.61.cloned.1.call-start = ((), (), s32[]{:S(2)}) async-start(), calls=%async_computation.32 | async-start | bytes 1769472 | tf_op jit(solution)/shard_map/all_gather | solution.py:512
  780.1 193.0 %all-reduce.32.cloned.1.call-start = ((), (), s32[]{:S(2)}) async-start(), calls=%async_computation.33 | async-start | bytes 2752512 | tf_op jit(solution)/shard_map/psum | solution.py:262
  931.4 89.2 %all-gather.63.cloned.1.call-start = ((), (), s32[]{:S(2)}) async-start(), calls=%async_computation.34 | async-start | bytes 1769472 | tf_op jit(solution)/shard_map/all_gather | solution.py:573
  931.9 191.7 %all-gather.65.cloned.1.call-start = ((), (), s32[]{:S(2)}) async-start(), calls=%async_computation.35 | async-start | bytes 1769472 | tf_op jit(solution)/shard_map/all_gather | solution.py:574
  983.5 249.2 %all-reduce.34.cloned.1.call-start = ((), (), s32[]{:S(2)}) async-start(), calls=%async_computation.36 | async-start | bytes 1572864 | tf_op jit(solution)/shard_map/psum | solution.py:262
  985.8 71.2 %copy-start.67 = (f32[256,3,128]{2,0,1:T(8,128)S(1)}, f32[256,3,128]{2,0,1:T(8,128)}, u32[]{:S(2)}) copy-start(f32[256,3,128]{2,0,1:T(8,128)} %copy-done.66) | copy-start | bytes 1179652
  1200.8 99.8 %all-gather.25.cloned.1.call-start = ((), (), s32[]{:S(2)}) async-start(), calls=%async_computation.7 | async-start | bytes 1769472 | tf_op jit(solution)/shard_map/all_gather | solution.py:423
  1255.0 91.4 %all-gather.27.cloned.1.call-start = ((), (), s32[]{:S(2)}) async-start(), calls=%async_computation.8 | async-start | bytes 1769472 | tf_op jit(solution)/shard_map/all_gather | solution.py:424
  1255.9 152.2 %all-reduce.18.cloned.1.call-start = ((), (), s32[]{:S(2)}) async-start(), calls=%async_computation.10 | async-start | bytes 1572864 | tf_op jit(solution)/shard_map/psum | solution.py:254
  1375.2 86.8 %all-gather.33.cloned.1.call-start = ((), (), s32[]{:S(2)}) async-start(), calls=%async_computation.12 | async-start | bytes 1327104 | tf_op jit(solution)/shard_map/all_gather | solution.py:462
  1420.7 83.5 %all-gather.35.cloned.1.call-start = ((), (), s32[]{:S(2)}) async-start(), calls=%async_computation.13 | async-start | bytes 1327104 | tf_op jit(solution)/shard_map/all_gather | solution.py:463
  1423.2 135.1 %all-reduce.20.cloned.1.call-start = ((), (), s32[]{:S(2)}) async-start(), calls=%async_computation.15 | async-start | bytes 1572864 | tf_op jit(solution)/shard_map/psum | solution.py:254
  1522.6 95.7 %all-reduce.26.cloned.1.call-start = ((), (), s32[]{:S(2)}) async-start(), calls=%async_computation.24 | async-start | bytes 1572864 | tf_op jit(solution)/shard_map/psum | solution.py:262
  1583.5 82.4 %all-gather.51.cloned.1.call-start = ((), (), s32[]{:S(2)}) async-start(), calls=%async_computation.25 | async-start | bytes 1769472 | tf_op jit(solution)/shard_map/all_gather | solution.py:511
  1584.1 138.9 %all-gather.53.cloned.1.call-start = ((), (), s32[]{:S(2)}) async-start(), calls=%async_computation.26 | async-start | bytes 1769472 | tf_op jit(solution)/shard_map/all_gather | solution.py:512
  1626.2 156.9 %all-gather.55.cloned.1.call-start = ((), (), s32[]{:S(2)}) async-start(), calls=%async_computation.28 | async-start | bytes 1769472 | tf_op jit(solution)/shard_map/all_gather | solution.py:573
  1626.9 192.5 %all-reduce.28.cloned.1.call-start = ((), (), s32[]{:S(2)}) async-start(), calls=%async_computation.27 | async-start | bytes 2752512 | tf_op jit(solution)/shard_map/psum | solution.py:262
  1774.4 128.7 %all-gather.57.cloned.1.call-start = ((), (), s32[]{:S(2)}) async-start(), calls=%async_computation.29 | async-start | bytes 1769472 | tf_op jit(solution)/shard_map/all_gather | solution.py:574
  1829.9 203.9 %all-reduce.38.cloned.1.call-start = ((), (), s32[]{:S(2)}) async-start(), calls=%async_computation.44 | async-start | bytes 4718592 | tf_op jit(solution)/shard_map/psum | solution.py:254
  1980.0 183.0 %reduce-scatter.13.cloned.1.call-start = ((), (), s32[]{:S(2)}) async-start(), calls=%async_computation.40 | async-start | bytes 1327104 | tf_op jit(solution)/shard_map/reduce_scatter | solution.py:305
  1984.5 191.0 %reduce-scatter.9.cloned.1.call-start = ((), (), s32[]{:S(2)}) async-start(), calls=%async_computation.38 | async-start | bytes 1327104 | tf_op jit(solution)/shard_map/reduce_scatter | solution.py:299
  2002.9 238.2 %all-reduce.36.cloned.1.call-start = ((), (), s32[]{:S(2)}) async-start(), calls=%async_computation.37 | async-start | bytes 294912 | tf_op jit(solution)/shard_map/psum | solution.py:718
  2083.9 239.4 %reduce-scatter.11.cloned.1.call-start = ((), (), s32[]{:S(2)}) async-start(), calls=%async_computation.39 | async-start | bytes 3981312 | tf_op jit(solution)/shard_map/reduce_scatter | solution.py:302
  2091.4 314.4 %reduce-scatter.19.cloned.1.call-start = ((), (), s32[]{:S(2)}) async-start(), calls=%async_computation.43 | async-start | bytes 3981312
  2110.9 427.7 %reduce-scatter.15.cloned.1.call-start = ((), (), s32[]{:S(2)}) async-start(), calls=%async_computation.41 | async-start | bytes 7962624 | tf_op jit(solution)/shard_map/reduce_scatter | solution.py:308
  2129.8 540.4 %reduce-scatter.17.cloned.1.call-start = ((), (), s32[]{:S(2)}) async-start(), calls=%async_computation.42 | async-start | bytes 7962624 | tf_op jit(solution)/shard_map/reduce_scatter | solution.py:311
  (263 other events, 2431.9 us)
Sparse Core Ops, SparseCore 0:
  10.3 67.8 all-gather.22
  97.7 44.1 all-gather.42
  143.9 43.6 all-gather.44
  189.6 39.2 all-gather.28
  231.0 63.9 all-gather.30
  297.8 33.0 all-reduce.21
  343.3 41.2 all-gather.46
  386.7 39.7 all-gather.48
  428.7 39.8 all-gather.36
  471.5 33.3 all-reduce.23
  507.1 108.8 all-gather.40
  618.1 106.9 all-gather.38
  739.5 32.7 all-reduce.29
  774.8 45.4 all-gather.58
  822.8 43.7 all-gather.60
  931.5 41.5 all-reduce.31
  975.2 45.3 all-gather.62
  1023.2 44.5 all-gather.64
  1200.9 31.7 all-reduce.33
  1255.1 45.4 all-gather.24
  1302.9 43.4 all-gather.26
  1375.3 32.7 all-reduce.17
  1420.8 41.1 all-gather.32
  1464.3 39.8 all-gather.34
  1522.7 35.5 all-reduce.19
  1583.6 34.6 all-reduce.25
  1620.4 45.4 all-gather.50
  1668.7 43.5 all-gather.52
  1714.6 43.4 all-gather.54
  1774.5 41.5 all-reduce.27
  1830.0 42.7 all-gather.56
  1980.1 53.6 all-reduce.37
  2037.0 64.2 reduce-scatter.12
  2105.3 62.9 reduce-scatter.8
  2172.2 68.8 all-reduce.35
  2245.0 78.1 reduce-scatter.10
  2327.1 78.6 reduce-scatter.18
  2410.0 128.5 reduce-scatter.14
  2542.1 128.0 reduce-scatter.16
where the time goes:
time: 2710 us; the launch traced here: 2680 us
  waiting for transfers between devices  1350 us (50%)
  blocking collectives  396 us (15%)
  matrix products  309 us (11%)
  local copies, waits for them, and re-layouts  291 us (11%)
  other arithmetic  232 us (9%)
  loops' own time  76 us (3%)
    psum x5, waiting for transfers between devices, sum_heads(): lax.psum(partial_rows.astype(jnp.bfloat16), 'tensor').astype(jnp.float32)  161 us
    psum x5, waiting for transfers between devices, sum_features(): lax.psum(partial_rows.astype(jnp.bfloat16), 'tensor').astype(jnp.float32)  132 us
    all_gather x4, blocking collectives, gather_stats(): lax.all_gather(log_total, 'seq', axis=1, tiled=True)  131 us
    reduce_scatter x1, waiting for transfers between devices, scatter_grads(): lax.psum_scatter(grad_up.astype(jnp.bfloat16), 'seq', scatter_dimension=0...  129 us
    reduce_scatter x1, waiting for transfers between devices, scatter_grads(): lax.psum_scatter(grad_down.astype(jnp.bfloat16), 'seq', scatter_dimension...  129 us
    all_gather x4, blocking collectives, gather_stats(): lax.all_gather(delta_rows, 'seq', axis=1, tiled=True)  129 us
    all_gather x1, waiting for transfers between devices, gather_weights(): lax.all_gather(ffn_out, 'seq', axis=1, tiled=True)  103 us
    all_gather x1, waiting for transfers between devices, gather_weights(): lax.all_gather(ffn_in, 'seq', axis=0, tiled=True)  102 us
  transfers between devices with their start and end apart: 39, of which 29 were waited for; matrix products, arithmetic and copies ran while one was open for 19% of the time, Pallas kernels for 0%

commit v1 on v0

v1 whole, which is shorter than its diff:
```python
from functools import partial
import math

import jax
import jax.numpy as jnp
from jax import lax
from jax.experimental import pallas as pl
from jax.experimental.pallas import tpu as pltpu
from jax.sharding import PartitionSpec as P

HD = 128
TXT = 512
EPS = 1e-06
HIGH = lax.Precision.HIGHEST
NEG = -1e30
F32 = jnp.float32
BF16 = jnp.bfloat16
AXES = ("seq", "tensor")


def norm_stats(values):
    center = values - jnp.mean(values, -1, keepdims=True)
    return center, lax.rsqrt(jnp.mean(center * center, -1, keepdims=True) + EPS)


def norm_plain(values):
    center, inverse = norm_stats(values)
    return center * inverse


def norm_back(values, cotangent):
    center, inverse = norm_stats(values)
    normed = center * inverse
    return inverse * (
        cotangent
        - jnp.mean(cotangent, -1, keepdims=True)
        - normed * jnp.mean(cotangent * normed, -1, keepdims=True)
    )


def nn(a, b):
    return lax.dot_general(a, b, (((1,), (0,)), ((), ())), preferred_element_type=F32)


def nt(a, b):
    return lax.dot_general(a, b, (((1,), (1,)), ((), ())), preferred_element_type=F32)


def tn(a, b):
    return lax.dot_general(a, b, (((0,), (0,)), ((), ())), preferred_element_type=F32)


def allowed_pairs(query_code, key_code, row_base, shape, transposed, diagonal):
    same = query_code == key_code
    if not diagonal:
        return same
    rows = lax.broadcasted_iota(jnp.int32, shape, 1 if transposed else 0) + row_base
    cols = lax.broadcasted_iota(jnp.int32, shape, 0 if transposed else 1)
    return same | (rows == cols)


def forward_kernel(
    query_ref, key_ref, value_ref, qcode_ref, kcode_ref, out_ref, total_ref, *, diagonal
):
    rows = query_ref.shape[0]
    count = key_ref.shape[0]
    mask = allowed_pairs(
        qcode_ref[...],
        kcode_ref[...],
        pl.program_id(0) * rows,
        (rows, count),
        False,
        diagonal,
    )
    factor = 1.0 / math.sqrt(HD)
    for head in range(query_ref.shape[1] // HD):
        cols = slice(head * HD, (head + 1) * HD)
        scores = jnp.where(mask, nt(query_ref[:, cols], key_ref[:, cols]) * factor, NEG)
        top = jnp.max(scores, -1, keepdims=True)
        weights = jnp.exp(scores - top)
        total = jnp.sum(weights, -1, keepdims=True)
        probs = (weights * (1.0 / total)).astype(BF16)
        out_ref[:, cols] = nn(probs, value_ref[:, cols]).astype(out_ref.dtype)
        total_ref[:, head : head + 1] = top + jnp.log(total)


def backward_kernel(
    query_ref,
    grad_ref,
    key_ref,
    value_ref,
    qcode_ref,
    kcode_ref,
    total_ref,
    dquery_ref,
    dkey_ref,
    dvalue_ref,
    key_sum,
    value_sum,
    *,
    diagonal,
):
    rows = query_ref.shape[0]
    count = key_ref.shape[0]
    step = pl.program_id(1)
    mask = allowed_pairs(
        qcode_ref[...],
        kcode_ref[...],
        step * rows,
        (count, rows),
        True,
        diagonal,
    )
    factor = 1.0 / math.sqrt(HD)

    @pl.when(step == 0)
    def _():
        key_sum[...] = jnp.zeros_like(key_sum)
        value_sum[...] = jnp.zeros_like(value_sum)

    for head in range(query_ref.shape[1] // HD):
        cols = slice(head * HD, (head + 1) * HD)
        query, grad = query_ref[:, cols], grad_ref[:, cols]
        key, value = key_ref[:, cols], value_ref[:, cols]
        scores = nt(key, query) * factor
        probs = jnp.where(mask, jnp.exp(scores - total_ref[head]), 0.0)
        dprobs = nt(value, grad)
        delta = jnp.sum(probs * dprobs, 0, keepdims=True)
        dscores = (probs * (dprobs - delta)).astype(BF16)
        value_sum[:, cols] += nn(probs.astype(BF16), grad)
        key_sum[:, cols] += nn(dscores, query)
        dquery_ref[:, cols] = tn(dscores, key) * factor

    @pl.when(step == pl.num_programs(1) - 1)
    def _():
        dkey_ref[...] = (key_sum[...] * factor).astype(BF16)
        dvalue_ref[...] = value_sum[...].astype(BF16)


def tile_rows(rows, count):
    tile = rows
    while tile > 128 and (tile * count > 256 * 2048) and tile % 2 == 0:
        tile //= 2
    return tile


def attend(queries, keys, values, query_code, key_code, diagonal):
    rows, width = queries.shape
    count = keys.shape[0]
    tile = tile_rows(rows, count)
    whole = lambda i: (0, 0)
    part = lambda i: (i, 0)
    return pl.pallas_call(
        partial(forward_kernel, diagonal=diagonal),
        grid=(rows // tile,),
        in_specs=[
            pl.BlockSpec((tile, width), part),
            pl.BlockSpec((count, width), whole),
            pl.BlockSpec((count, width), whole),
            pl.BlockSpec((tile, 1), part),
            pl.BlockSpec((1, count), whole),
        ],
        out_specs=[pl.BlockSpec((tile, width), part), pl.BlockSpec((tile, HD), part)],
        out_shape=[
            jax.ShapeDtypeStruct((rows, width), BF16),
            jax.ShapeDtypeStruct((rows, HD), F32),
        ],
        cost_estimate=pl.CostEstimate(
            flops=4 * rows * count * width,
            bytes_accessed=4 * (rows + count) * width,
            transcendentals=rows * count * (width // HD),
        ),
        compiler_params=pltpu.CompilerParams(vmem_limit_bytes=60 * 2**20),
        name="attend" if diagonal else "attend_text",
    )(queries, keys, values, query_code[:, None], key_code[None, :])


def attend_back(queries, grads, keys, values, query_code, key_code, totals, diagonal):
    rows, width = queries.shape
    count = keys.shape[0]
    tile = tile_rows(rows, count)
    heads = width // HD
    part_heads = heads if count * width <= 4096 * 3 * HD else 1
    cols = part_heads * HD
    whole = lambda h, i: (0, h)
    part = lambda h, i: (i, h)
    lines = totals[:, :heads].T[:, None, :]
    return pl.pallas_call(
        partial(backward_kernel, diagonal=diagonal),
        grid=(heads // part_heads, rows // tile),
        in_specs=[
            pl.BlockSpec((tile, cols), part),
            pl.BlockSpec((tile, cols), part),
            pl.BlockSpec((count, cols), whole),
            pl.BlockSpec((count, cols), whole),
            pl.BlockSpec((1, tile), lambda h, i: (0, i)),
            pl.BlockSpec((count, 1), lambda h, i: (0, 0)),
            pl.BlockSpec((part_heads, 1, tile), lambda h, i: (h, 0, i)),
        ],
        out_specs=[
            pl.BlockSpec((tile, cols), part),
            pl.BlockSpec((count, cols), whole),
            pl.BlockSpec((count, cols), whole),
        ],
        out_shape=[
            jax.ShapeDtypeStruct((rows, width), F32),
            jax.ShapeDtypeStruct((count, width), BF16),
            jax.ShapeDtypeStruct((count, width), BF16),
        ],
        scratch_shapes=[pltpu.VMEM((count, cols), F32), pltpu.VMEM((count, cols), F32)],
        cost_estimate=pl.CostEstimate(
            flops=10 * rows * count * width,
            bytes_accessed=8 * (rows + count) * width,
            transcendentals=rows * count * heads,
        ),
        compiler_params=pltpu.CompilerParams(vmem_limit_bytes=60 * 2**20),
        name="attend_back" if diagonal else "attend_text_back",
    )(queries, grads, keys, values, query_code[None, :], key_code[:, None], lines)


def rope_tables(frames, rows_pos, cols_pos):
    part_size = HD // 6
    widths = (HD - 4 * part_size, 2 * part_size, 2 * part_size)
    angles = []
    for position, group_width in zip((frames, rows_pos, cols_pos), widths):
        exponent = jnp.arange(0, group_width, 2).astype(F32) / group_width
        exponent = jnp.repeat(exponent, 2)
        angles.append(
            position.astype(F32)[:, None] * jnp.power(10000.0, -exponent)[None, :]
        )
    joined = jnp.concatenate(angles, -1)
    return jnp.cos(joined), jnp.sin(joined)


def rotate(values, cosine, sine):
    rows, width = values.shape
    low = lax.broadcasted_iota(jnp.int32, (width, width), 0)
    high = lax.broadcasted_iota(jnp.int32, (width, width), 1)
    turn = jnp.where(
        low == (high ^ 1), jnp.where(high % 2 == 0, -1.0, 1.0), 0.0
    ).astype(F32)
    heads = width // HD
    turned = jnp.dot(values, turn, precision=HIGH, preferred_element_type=F32)
    return values * jnp.tile(cosine, (1, heads)) + turned * jnp.tile(sine, (1, heads))


def shards(
    inputs,
    text_states,
    timestep_emb,
    modulation,
    attn_in,
    in_bias,
    norm_gains,
    attn_out,
    cross_in,
    cross_out,
    cross_norm_gain,
    cross_norm_bias,
    ffn_in,
    ffn_bias,
    ffn_out,
    out_bias,
    latent_ids,
    pad_mask,
    frame_pos,
    row_pos,
    col_pos,
    cotangent,
):
    micros, tok_rows, width = inputs.shape
    text_rows = text_states.shape[1]
    latents = timestep_emb.shape[1]
    columns = attn_in.shape[2]
    hidden = ffn_in.shape[1]
    slice_rows = attn_in.shape[1]
    seq_size, tensor_size = lax.axis_size("seq"), lax.axis_size("tensor")
    places = seq_size * tensor_size
    bits = seq_size.bit_length() - 1
    s, t = lax.axis_index("seq"), lax.axis_index("tensor")
    top = bits - 1
    rest = [b for b in range(bits) if b not in (1, top)]

    def seq_bit(b):
        return (s >> b) & 1

    k, w, x, c = seq_bit(top), seq_bit(1), t >> 1, t & 1
    own_slice = (s & ~2) | (c << 1)
    hop_c, hop_x, hop_w, hop_k = 1, 2, tensor_size << 1, tensor_size << top
    hop_rest = [tensor_size << b for b in rest]
    hop_group = [0, hop_x, hop_w, hop_x | hop_w]

    def hop(value, mask):
        return lax.ppermute(value, AXES, [(d, d ^ mask) for d in range(places)])

    def swap(value):
        def other(d):
            low, high = d & 1, (d // hop_w) & 1
            return d if low == high else d ^ 1 ^ hop_w

        return lax.ppermute(value, AXES, [(d, other(d)) for d in range(places)])

    def gather_weight(block):
        held = [(0, swap(block))]
        for mask, offset in (
            [(hop_k, 1 << top)]
            + [(m, 1 << b) for m, b in zip(hop_rest, rest)]
            + [(hop_c, 2)]
        ):
            held = held + [(o | offset, hop(v, mask)) for o, v in held]
        out = jnp.zeros((seq_size,) + block.shape, block.dtype)
        for offset, value in held:
            out = lax.dynamic_update_index_in_dim(out, value, own_slice ^ offset, 0)
        return out.reshape(seq_size * block.shape[0], block.shape[1])

    def scatter_weight(grad):
        cols = grad.shape[1]
        current = grad.astype(BF16).reshape((2,) * bits + (slice_rows, cols))
        for mask, b, mine in (
            [(hop_c, 1, c)]
            + [(m, b, seq_bit(b)) for m, b in zip(hop_rest, rest)]
            + [(hop_k, top, k)]
        ):
            axis = bits - 1 - b
            given = lax.dynamic_index_in_dim(current, 1 - mine, axis, keepdims=True)
            kept = lax.dynamic_index_in_dim(current, mine, axis, keepdims=True)
            current = (kept.astype(F32) + hop(given, mask).astype(F32)).astype(BF16)
        return swap(current.reshape(slice_rows, cols))

    def gather_tokens(value):
        for mask in hop_rest + [hop_c]:
            value = jnp.concatenate((value, hop(value, mask)), 0)
        return value

    def scatter_tokens(value):
        for mask in [hop_c] + hop_rest[::-1]:
            half = value.shape[0] // 2
            value = (
                value[:half].astype(F32) + hop(value[half:], mask).astype(F32)
            ).astype(BF16)
        return value

    def spread(value):
        return jnp.concatenate([value] + [hop(value, m) for m in hop_group[1:]], 0)

    def collect(value):
        parts = value.astype(BF16).reshape(4, value.shape[0] // 4, value.shape[1])
        total = parts[0].astype(F32)
        for j in (1, 2, 3):
            total = total + hop(parts[j], hop_group[j]).astype(F32)
        return total

    def group_sum(value, flips):
        rows = value.shape[-1]
        total = value
        for j in (1, 2, 3):
            other = hop(value, hop_group[j])
            shift = flips(j)
            if shift:
                count = 4 if flips(1) else 2
                size = rows // count
                order = [i ^ shift for i in range(count)]
                other = jnp.concatenate(
                    [other[..., i * size : (i + 1) * size] for i in order], -1
                )
            total = total + other
        return total

    def token_sum(value):
        return group_sum(value, lambda j: j)

    def text_sum(value):
        return group_sum(value, lambda j: j >> 1)

    def all_sum(value, masks):
        for mask in masks:
            value = value.astype(BF16)
            value = value.astype(F32) + hop(value, mask).astype(F32)
        return value

    def by_home(own, other):
        return jnp.where(c == w, own, other)

    pack = lambda a: a.transpose(1, 0, 2).reshape(slice_rows, -1)
    w_attn = gather_weight(pack(attn_in))
    w_text = gather_weight(pack(cross_in[1:]))
    w_mid = gather_weight(jnp.concatenate((attn_out.T, cross_in[0], cross_out.T), 1))
    w_attn_out = w_mid[:, :columns]
    w_cross_q = w_mid[:, columns : 2 * columns]
    w_cross_out = w_mid[:, 2 * columns :]
    w_up = gather_weight(ffn_in)
    w_down = gather_weight(ffn_out.T)

    flat = jnp.concatenate((in_bias.reshape(-1), norm_gains.reshape(-1), ffn_bias))
    flat = by_home(flat, hop(flat, hop_c)).astype(F32)
    bias_in = flat[: 6 * columns].reshape(2, 3, columns)
    gains = flat[6 * columns : 10 * columns].reshape(4, columns)
    bias_ffn = flat[10 * columns :]
    bias_out = out_bias.astype(F32)
    cgain = cross_norm_gain.astype(F32)
    cbias = cross_norm_bias.astype(F32)

    meta = jnp.stack((latent_ids, pad_mask, frame_pos, row_pos, col_pos))[None]
    for mask in [hop_k, hop_w] + hop_rest:
        meta = jnp.concatenate((meta, hop(meta, mask)), 0)
    meta = lax.dynamic_index_in_dim(meta, k, 2, keepdims=False)
    piece = tok_rows // 4
    meta = meta.reshape((2,) * bits + (5, 2, 2, piece))
    meta = jnp.where(x == 1, jnp.flip(meta, bits + 1), meta)
    meta = jnp.where(c == 1, jnp.flip(meta, bits + 2), meta)
    others = list(range(bits - 2))
    meta = meta.transpose([bits, bits + 2] + others + [bits - 2, bits + 1, bits - 1, bits + 3])
    meta = meta.reshape(5, -1)
    group_rows = 8 * piece
    share_rows = 2 * piece
    ids_all = meta[0]
    key_code = jnp.where(meta[1] == 1, ids_all, -1)
    ids_here = ids_all[:group_rows]
    ids_share = ids_here[:share_rows, None]
    cosine, sine = rope_tables(*(meta[i, :group_rows] for i in (2, 3, 4)))

    def take_share(array):
        parts = array.reshape(micros, 4, piece, width)
        own = lax.dynamic_index_in_dim(
            lax.dynamic_index_in_dim(parts, k, 0, keepdims=False), t, 0, keepdims=False
        )
        given = lax.dynamic_index_in_dim(
            lax.dynamic_index_in_dim(parts, 1 - k, 0, keepdims=False), t, 0, keepdims=False
        )
        return jnp.concatenate((own, hop(given, hop_k)), 0).astype(F32)

    def give_back(share, rows_each, order):
        own, far = share[:rows_each], hop(share[rows_each:], hop_k)
        both = jnp.where(k == 0, jnp.stack((own, far)), jnp.stack((far, own)))
        across = hop(both, hop_x)
        pieces = ((0, both), (1, hop(both, hop_c)), (2, across), (3, hop(across, hop_c)))
        out = jnp.zeros((micros, 4, rows_each, width), both.dtype)
        for offset, value in pieces:
            out = lax.dynamic_update_index_in_dim(out, value, order(t ^ offset), 1)
        return out.reshape(micros, 4 * rows_each, width)

    state_in = take_share(inputs)
    grad_top = take_share(cotangent)
    table = modulation + lax.dynamic_index_in_dim(timestep_emb, k, 0, keepdims=False)

    def shift(number):
        out = table[0, number][None]
        for latent in range(1, latents):
            out = jnp.where(ids_share == latent, table[latent, number][None], out)
        return out

    half = text_rows // 2
    texts = text_states.reshape(micros, 2, half, width)

    def text_of(micro):
        return lax.dynamic_index_in_dim(
            lax.dynamic_index_in_dim(texts, micro, 0, keepdims=False), c, 0, keepdims=False
        )

    text_here = jnp.concatenate((text_of(k), hop(text_of(1 - k), hop_k)), 0)
    text_here = jnp.concatenate((text_here, hop(text_here, hop_w)), 0)
    number = jnp.arange(4 * half * seq_size // 2, dtype=jnp.int32)
    row, blocks = number % half, number // half
    row_k, row_w, row_rest = blocks & 1, (blocks >> 1) & 1, blocks >> 2
    place = ((row_k ^ k) << top) | ((row_w ^ w) << 1)
    for i, b in enumerate(rest):
        place = place | ((((row_rest >> i) & 1) ^ seq_bit(b)) << b)
    row_c = (row_rest >> len(rest)) ^ c
    text_code = (place * text_rows + row_c * half + row) // TXT

    normed_one = norm_plain(state_in)
    act_low = spread((normed_one * (1.0 + shift(1)) + shift(0)).astype(BF16))
    grad_branch_three_share = (grad_top * shift(5)).astype(BF16)
    grad_branch_three = spread(grad_branch_three_share)
    projected = nn(act_low, w_attn) + bias_in[0].reshape(1, -1)
    query_pre = projected[:, :columns]
    key_pre = projected[:, columns : 2 * columns]
    value_low = projected[:, 2 * columns :].astype(BF16)
    sums = token_sum(
        jnp.stack((jnp.sum(query_pre * query_pre, -1), jnp.sum(key_pre * key_pre, -1)))
    )
    inverse_q, inverse_k = lax.rsqrt(sums / width + EPS)[:, :, None]
    query_low = rotate(query_pre * inverse_q * gains[0], cosine, sine).astype(BF16)
    key_low = rotate(key_pre * inverse_k * gains[1], cosine, sine).astype(BF16)
    pair_all = gather_tokens(jnp.concatenate((key_low, value_low), 1))
    key_all, value_all = pair_all[:, :columns], pair_all[:, columns:]
    attn_low, total_self = attend(query_low, key_all, value_all, ids_here, key_code, True)
    branch_one = collect(nt(attn_low, w_attn_out)) + bias_out[0]
    state_one = state_in + branch_one * shift(2)

    text_pre = nn(text_here, w_text) + bias_in[1, 1:].reshape(1, -1)
    ckey_pre = text_pre[:, :columns]
    inverse_ck = lax.rsqrt(
        text_sum(jnp.sum(ckey_pre * ckey_pre, -1)[None])[0] / width + EPS
    )[:, None]
    ckey_low = (ckey_pre * inverse_ck * gains[3]).astype(BF16)
    cpair_all = gather_tokens(
        jnp.concatenate((ckey_low, text_pre[:, columns:].astype(BF16)), 1)
    )
    ckey_all, cvalue_all = cpair_all[:, :columns], cpair_all[:, columns:]

    normed_three = norm_plain(state_one)
    cross_act = spread((normed_three * cgain + cbias).astype(BF16))
    cquery_pre = nn(cross_act, w_cross_q) + bias_in[1, 0]
    inverse_cq = lax.rsqrt(
        token_sum(jnp.sum(cquery_pre * cquery_pre, -1)[None])[0] / width + EPS
    )[:, None]
    cquery_low = (cquery_pre * inverse_cq * gains[2]).astype(BF16)
    cross_low, total_cross = attend(
        cquery_low, ckey_all, cvalue_all, ids_here, text_code, False
    )
    branch_two = collect(nt(cross_low, w_cross_out)) + bias_out[1]
    state_two = state_one + branch_two

    normed_two = norm_plain(state_two)
    ffn_act = spread((normed_two * (1.0 + shift(4)) + shift(3)).astype(BF16))
    hidden_pre = nn(ffn_act, w_up) + bias_ffn
    hidden_low = jax.nn.gelu(hidden_pre, approximate=True).astype(BF16)
    branch_three = collect(nt(hidden_low, w_down)) + bias_out[2]
    out_share = (state_two + branch_three * shift(5)).astype(BF16)

    gelu_pull = jax.vjp(partial(jax.nn.gelu, approximate=True), hidden_pre)[1]
    grad_hidden = gelu_pull(nn(grad_branch_three, w_down))[0].astype(BF16)
    grad_ffn_act = collect(nt(grad_hidden, w_up))
    grad_up = scatter_weight(tn(ffn_act, grad_hidden))
    grad_down = scatter_weight(tn(grad_branch_three, hidden_low))
    grad_state_two = grad_top + norm_back(state_two, grad_ffn_act * (1.0 + shift(4)))

    grad_branch_two_share = grad_state_two.astype(BF16)
    grad_branch_two = spread(grad_branch_two_share)
    grad_cross = nn(grad_branch_two, w_cross_out).astype(BF16)
    grad_cquery, grad_ckey, grad_cvalue = attend_back(
        cquery_low,
        grad_cross,
        ckey_all,
        cvalue_all,
        ids_here,
        text_code,
        total_cross,
        False,
    )
    sums_cq = token_sum(jnp.sum(gains[2] * grad_cquery * cquery_pre, -1)[None])[0]

    def rms_back(pre, inverse, gain, cotangent_here, summed):
        scaled = inverse * inverse * inverse * summed[:, None] / width
        return (inverse * gain * cotangent_here - pre * scaled).astype(BF16)

    gcq_low = rms_back(cquery_pre, inverse_cq, gains[2], grad_cquery, sums_cq)
    grad_cross_act = collect(nt(gcq_low, w_cross_q))
    grad_state_one = grad_state_two + norm_back(state_one, grad_cross_act * cgain)

    gpair = scatter_tokens(jnp.concatenate((grad_ckey, grad_cvalue), 1))
    gckey = gpair[:, :columns].astype(F32)
    sums_ck = text_sum(jnp.sum(gains[3] * gckey * ckey_pre, -1)[None])[0]
    gck_low = rms_back(ckey_pre, inverse_ck, gains[3], gckey, sums_ck)
    gtext = jnp.concatenate((gck_low, gpair[:, columns:]), 1)
    text_part = nt(gtext, w_text).astype(BF16)
    text_sub = half // 2
    text_part = text_part[: 2 * half].astype(F32) + hop(
        text_part[2 * half :], hop_w
    ).astype(F32)
    text_part = text_part.reshape(2, 2, text_sub, width)
    text_share = lax.dynamic_index_in_dim(text_part, x, 1, keepdims=False)
    text_given = lax.dynamic_index_in_dim(text_part, 1 - x, 1, keepdims=False)
    text_share = text_share + hop(text_given.astype(BF16), hop_x).astype(F32)
    grad_text = give_back(
        text_share.astype(BF16).reshape(2 * text_sub, width),
        text_sub,
        lambda place_here: ((place_here & 1) << 1) | (place_here >> 1),
    ).astype(F32)

    grad_branch_one_share = (grad_state_one * shift(2)).astype(BF16)
    grad_branch_one = spread(grad_branch_one_share)
    grad_attn = nn(grad_branch_one, w_attn_out).astype(BF16)
    grad_query, grad_key, grad_value = attend_back(
        query_low, grad_attn, key_all, value_all, ids_here, key_code, total_self, True
    )
    kv_back = scatter_tokens(jnp.concatenate((grad_key, grad_value), 1))
    grad_qnorm = rotate(grad_query, cosine, -sine)
    grad_knorm = rotate(kv_back[:, :columns].astype(F32), cosine, -sine)
    sums_self = token_sum(
        jnp.stack(
            (
                jnp.sum(gains[0] * grad_qnorm * query_pre, -1),
                jnp.sum(gains[1] * grad_knorm * key_pre, -1),
            )
        )
    )
    gq_low = rms_back(query_pre, inverse_q, gains[0], grad_qnorm, sums_self[0])
    gk_low = rms_back(key_pre, inverse_k, gains[1], grad_knorm, sums_self[1])
    grad_proj = jnp.concatenate((gq_low, gk_low, kv_back[:, columns:]), 1)
    grad_act = collect(nt(grad_proj, w_attn))
    grad_input_share = grad_state_one + norm_back(state_in, grad_act * (1.0 + shift(1)))

    grad_mid = scatter_weight(
        jnp.concatenate(
            (
                tn(grad_branch_one, attn_low),
                tn(cross_act, gcq_low),
                tn(grad_branch_two, cross_low),
            ),
            1,
        )
    )
    grad_text_in = scatter_weight(tn(text_here, gtext))
    grad_attn_in = scatter_weight(tn(act_low, grad_proj))

    rows_sum = lambda a: jnp.sum(a.astype(F32), 0)
    column_sums = jnp.concatenate(
        (
            rows_sum(grad_proj),
            rows_sum(gcq_low),
            rows_sum(gtext),
            rows_sum(grad_qnorm * query_pre * inverse_q),
            rows_sum(grad_knorm * key_pre * inverse_k),
            rows_sum(grad_cquery * cquery_pre * inverse_cq),
            rows_sum(gckey * ckey_pre * inverse_ck),
            rows_sum(grad_hidden),
        )
    )
    column_sums = all_sum(column_sums, [hop_c] + hop_rest + [hop_k])
    low_sums = column_sums.astype(BF16)
    column_sums = by_home(low_sums, hop(low_sums, hop_w)).astype(F32)
    grad_in_bias = column_sums[: 6 * columns].reshape(2, 3, columns)
    grad_gains = column_sums[6 * columns : 10 * columns].reshape(4, columns)
    grad_ffn_bias = column_sums[10 * columns :]

    picker = (
        ids_share == jnp.arange(latents, dtype=jnp.int32)[None, :]
    ).astype(F32)

    def by_latent(value):
        return lax.dot_general(
            picker, value, (((0,), (0,)), ((), ())), precision=HIGH, preferred_element_type=F32
        )

    feature_sums = jnp.concatenate(
        [
            by_latent(grad_act),
            by_latent(grad_act * normed_one),
            by_latent(grad_state_one * branch_one),
            by_latent(grad_ffn_act),
            by_latent(grad_ffn_act * normed_two),
            by_latent(grad_top * branch_three),
        ]
        + [
            rows_sum(a)[None]
            for a in (
                grad_branch_one_share,
                grad_branch_two_share,
                grad_branch_three_share,
                grad_cross_act * normed_three,
                grad_cross_act,
            )
        ],
        0,
    )
    feature_sums = all_sum(feature_sums, [hop_c, hop_x, hop_w] + hop_rest)
    low_features = feature_sums.astype(BF16)
    far_features = hop(low_features, hop_k).astype(F32)
    near_features = low_features.astype(F32)
    both_sums = near_features + far_features
    count = 6 * latents
    near_temb = near_features[:count].reshape(6, latents, width).transpose(1, 0, 2)
    far_temb = far_features[:count].reshape(6, latents, width).transpose(1, 0, 2)
    grad_temb = jnp.where(
        k == 0, jnp.stack((near_temb, far_temb)), jnp.stack((far_temb, near_temb))
    )
    grad_mod = jnp.sum(grad_temb, (0, 1))

    block_out = give_back(out_share, piece, lambda place_here: place_here)
    grad_inputs = give_back(
        grad_input_share.astype(BF16), piece, lambda place_here: place_here
    ).astype(F32)
    unpack = lambda a: a.reshape(slice_rows, -1, columns).transpose(1, 0, 2).astype(F32)
    return (
        block_out,
        grad_inputs,
        grad_text,
        grad_temb,
        grad_mod,
        unpack(grad_attn_in),
        grad_in_bias,
        grad_gains,
        grad_mid[:, :columns].T.astype(F32),
        jnp.concatenate(
            (grad_mid[None, :, columns : 2 * columns].astype(F32), unpack(grad_text_in)), 0
        ),
        grad_mid[:, 2 * columns :].T.astype(F32),
        both_sums[count + 3],
        both_sums[count + 4],
        grad_up.astype(F32),
        grad_ffn_bias,
        grad_down.T.astype(F32),
        both_sums[count : count + 3],
    )


def solution(mesh):
    placed = (
        P(None, "seq", None),
        P(None, "seq", None),
        P(),
        P(),
        P(None, "seq", "tensor"),
        P(None, None, "tensor"),
        P(None, "tensor"),
        P("tensor", "seq"),
        P(None, "seq", "tensor"),
        P("tensor", "seq"),
        P(),
        P(),
        P("seq", "tensor"),
        P("tensor"),
        P("tensor", "seq"),
        P(),
        P(None, "seq"),
        P(None, "seq"),
        P(None, "seq"),
        P(None, "seq"),
        P(None, "seq"),
        P(None, "seq", None),
    )
    return jax.shard_map(
        shards,
        mesh=mesh,
        in_specs=placed,
        out_specs=(
            P(None, "seq", None),
            P(None, "seq", None),
            P(None, "seq", None),
            P(),
            P(),
            P(None, "seq", "tensor"),
            P(None, None, "tensor"),
            P(None, "tensor"),
            P("tensor", "seq"),
            P(None, "seq", "tensor"),
            P("tensor", "seq"),
            P(),
            P(),
            P("seq", "tensor"),
            P("tensor"),
            P("tensor", "seq"),
            P(),
        ),
        check_vma=False,
    )
```

time: 2710 us -> 1120 us (0.41)
  waiting for transfers between devices: 1350 us -> 557 us
  blocking collectives: 396 us -> 0 us
  matrix products: 309 us -> 96.6 us
  starting transfers between devices: 3.61 us -> 178 us
  other arithmetic: 232 us -> 73.4 us
  local copies, waits for them, and re-layouts: 291 us -> 133 us
  loops' own time: 76 us -> 0 us
  Pallas kernels: 0 us -> 50.2 us
    all_gather x22 -> x0, waiting for transfers between devices: 629 us -> none  [the longest x1 103 us: gather_weights(): lax.all_gather(ffn_out, 'seq', axis=1, tiled=True)]
    ppermute x0 -> x153, waiting for transfers between devices: none -> 557 us  [the longest x143 557 us: hop(): return lax.ppermute(value, AXES, [(d, d ^ mask) for d in range(places)])]
    reduce_scatter x5 -> x0, waiting for transfers between devices: 337 us -> none  [the longest x1 129 us: scatter_grads(): lax.psum_scatter(grad_up.astype(jnp.bfloat16), 'seq', scatter_dimension=0...]
    all_gather x10 -> x0, blocking collectives: 312 us -> none  [the longest x4 131 us: gather_stats(): lax.all_gather(log_total, 'seq', axis=1, tiled=True)]
    psum x11 -> x0, waiting for transfers between devices: 300 us -> none  [the longest x5 161 us: sum_heads(): lax.psum(partial_rows.astype(jnp.bfloat16), 'tensor').astype(jnp.float32)]
    dot_general x120 -> x31, matrix products: 309 us -> 96.6 us  [the longest x7 31.8 us: nn(): lax.dot_general(a, b, (((1,), (0,)), ((), ())), preferred_element_type=F32)]
    ppermute x0 -> x153, starting transfers between devices: none -> 178 us  [the longest x143 160 us: hop(): return lax.ppermute(value, AXES, [(d, d ^ mask) for d in range(places)])]
    unnamed x40 -> x0, waiting for transfers between devices: 87 us -> none
  transfers between devices with their start and end apart: 39 -> 153, of which waited for: 29 -> 78; matrix products, arithmetic and copies ran while one was open for 19% -> 27% of each run, Pallas kernels for 0% -> 5%
where the time goes in v1:
time: 1120 us; the launch traced here: 1090 us
  waiting for transfers between devices  557 us (50%)
  starting transfers between devices  178 us (16%)
  local copies, waits for them, and re-layouts  133 us (12%)
  matrix products  96.6 us (9%)
  other arithmetic  73.4 us (7%)
  Pallas kernels  50.2 us (4%)
    ppermute x143, waiting for transfers between devices, hop(): return lax.ppermute(value, AXES, [(d, d ^ mask) for d in range(places)])  557 us
    ppermute x143, starting transfers between devices, hop(): return lax.ppermute(value, AXES, [(d, d ^ mask) for d in range(places)])  160 us
    dot_general x7, matrix products, nn(): lax.dot_general(a, b, (((1,), (0,)), ((), ())), preferred_element_type=F32)  31.8 us
    pallas_call x2, Pallas kernels, attend_back(): pl.pallas_call(partial(backward_kernel, diagonal=diagonal), grid=(heads /...  31.1 us
    dot_general x7, matrix products, tn(): lax.dot_general(a, b, (((0,), (0,)), ((), ())), preferred_element_type=F32)  26.3 us
    dot_general x7, matrix products, nt(): lax.dot_general(a, b, (((1,), (1,)), ((), ())), preferred_element_type=F32)  24.3 us
  transfers between devices with their start and end apart: 153, of which 78 were waited for; matrix products, arithmetic and copies ran while one was open for 27% of the time, Pallas kernels for 5%

profile of v1, /device:TPU:0, one launch (start us, length us, event | category | flops | bytes accessed | tf_op | source)
XLA Modules:
  0.0 1093.7 jit_solution(108382820576755689)
XLA Ops:
  21.4 5.2 collective-permute-start.21
  65.0 6.1 collective-permute-done.82
  88.2 8.2 collective-permute-done.41
  96.4 15.1 %collective-permute-start.5 = (bf16[128,1536]{1,0:T(8,128)(2,1)S(1)}, bf16[128,1536]{1,0:T(8,128)(2,1)S(1)}, u32[]{:S(2)}, u32[]{:S(2)}) collective-permute-start(bf16[128,1536]{1,0:T(8,128)(2,1)S(1)} %fusion.32), channel_id=1, source_target_pairs={{0,8},{1,9},{2,10},{3,11},{4,12},{5,13},{6,14},{7,15},{8,0},{9,1},... | collective-permute-start | bytes 1179656 | tf_op jit(solution)/shard_map/ppermute | solution.py:294
  116.9 21.4 %collective-permute-done.8 = bf16[192,1152]{1,0:T(8,128)(2,1)S(1)} collective-permute-done((bf16[192,1152]{1,0:T(8,128)(2,1)S(1)}, bf16[192,1152]{1,0:T(8,128)(2,1)S(1)}, u32[]{:S(2)}, u32[]{:S(2)}) %collective-permute-start.8) | collective-permute-done | bytes 442400 | tf_op jit(solution)/shard_map/ppermute | solution.py:294
  139.7 6.9 collective-permute-done.9
  150.0 6.4 collective-permute-done.22
  157.9 5.3 collective-permute-done.43
  170.6 9.2 collective-permute-done.23
  179.7 13.3 %collective-permute-start.50 = (f32[1,384]{1,0:T(1,128)S(1)}, f32[1,384]{1,0:T(1,128)S(1)}, u32[]{:S(2)}, u32[]{:S(2)}) collective-permute-start(f32[1,384]{1,0:T(1,128)S(1)} %broadcast_in_dim.578), channel_id=1, source_target_pairs={{0,10},{1,11},{2,8},{3,9},{4,14},{5,15},{6,12},{7,13},{8,2},{9,3},... | collective-permute-start | bytes 4616 | tf_op jit(solution)/shard_map/ppermute | solution.py:294
  203.8 6.9 collective-permute-done.10
  216.4 10.8 collective-permute-done.24
  235.6 32.9 %collective-permute-done.68 = bf16[192,2240]{1,0:T(8,128)(2,1)S(1)} collective-permute-done((bf16[192,2240]{1,0:T(8,128)(2,1)S(1)}, bf16[192,2240]{1,0:T(8,128)(2,1)S(1)}, u32[]{:S(2)}, u32[]{:S(2)}) %collective-permute-start.68) | collective-permute-done | bytes 860192 | tf_op jit(solution)/shard_map/ppermute | solution.py:294
  275.1 33.5 %collective-permute-done.60 = bf16[192,2240]{1,0:T(8,128)(2,1)S(1)} collective-permute-done((bf16[192,2240]{1,0:T(8,128)(2,1)S(1)}, bf16[192,2240]{1,0:T(8,128)(2,1)S(1)}, u32[]{:S(2)}, u32[]{:S(2)}) %collective-permute-start.60) | collective-permute-done | bytes 860192 | tf_op jit(solution)/shard_map/ppermute | solution.py:294
  315.4 17.6 %collective-permute-done.61 = bf16[192,2240]{1,0:T(8,128)(2,1)} collective-permute-done((bf16[192,2240]{1,0:T(8,128)(2,1)S(1)}, bf16[192,2240]{1,0:T(8,128)(2,1)}, u32[]{:S(2)}, u32[]{:S(2)}) %collective-permute-start.61) | collective-permute-done | bytes 860192 | tf_op jit(solution)/shard_map/ppermute | solution.py:294
  353.3 27.3 %collective-permute-done.19 = bf16[512,768]{1,0:T(8,128)(2,1)S(1)} collective-permute-done((bf16[512,768]{1,0:T(8,128)(2,1)S(1)}, bf16[512,768]{1,0:T(8,128)(2,1)S(1)}, u32[]{:S(2)}, u32[]{:S(2)}) %collective-permute-start.19) | collective-permute-done | bytes 786464 | tf_op jit(solution)/shard_map/ppermute | solution.py:294
  387.2 16.8 %collective-permute-done.62 = bf16[192,2240]{1,0:T(8,128)(2,1)S(1)} collective-permute-done((bf16[192,2240]{1,0:T(8,128)(2,1)S(1)}, bf16[192,2240]{1,0:T(8,128)(2,1)S(1)}, u32[]{:S(2)}, u32[]{:S(2)}) %collective-permute-start.62) | collective-permute-done | bytes 860192 | tf_op jit(solution)/shard_map/ppermute | solution.py:294
  412.6 10.7 attend.1
  433.1 5.8 collective-permute-done.31
  438.9 7.2 collective-permute-done.30
  452.6 7.8 collective-permute-done.34
  460.4 8.1 collective-permute-done.33
  481.5 8.4 attend_text.1
  501.8 5.8 collective-permute-done.55
  523.4 5.1 collective-permute-done.58
  529.4 6.0 collective-permute-done.57
  536.1 7.3 convolution_add_fusion
  543.4 8.9 convolution_convert_fusion.7
  556.2 12.8 %fusion.223 = (bf16[2240]{0:T(1024)(128)(2,1)}, bf16[512,2240]{0,1:T(8,128)(2,1)S(1)}) fusion(f32[512,2240]{0,1:T(8,128)S(1)} %convolution_add_fusion, bf16[1536,2240]{1,0:T(8,128)(2,1)} %bitcast.85, bf16[128,1536]{1,0:T(8,128)(2,1)} %collective-permute-done.85, bf16[128,1536]{1,0:T(8,128)(2,1)} %collective-permute-done.84, ...), kind=kOutput, calls=%fused_computation.573 | convolution fusion | flops 3553588992 | bytes 15339904 | tf_op jit(solution)/shard_map/dot_general | solution.py:42
  578.6 6.9 convolution_convert_fusion.1
  585.5 10.3 copy.133
  595.8 9.7 convolution_convert_fusion
  605.5 9.8 copy.134
  629.2 11.7 %collective-permute-done.75 = bf16[128,1536]{1,0:T(8,128)(2,1)S(1)} collective-permute-done((bf16[128,1536]{1,0:T(8,128)(2,1)}, bf16[128,1536]{1,0:T(8,128)(2,1)S(1)}, u32[]{:S(2)}, u32[]{:S(2)}) %collective-permute-start.75) | collective-permute-done | bytes 393248 | tf_op jit(solution)/shard_map/ppermute | solution.py:294
  645.6 6.9 collective-permute-done.78
  664.6 13.8 %attend_text_back.1 = (f32[512,384]{1,0:T(8,128)}, bf16[1536,384]{1,0:T(8,128)(2,1)}, bf16[1536,384]{1,0:T(8,128)(2,1)}) custom-call(bf16[512,384]{1,0:T(8,128)(2,1)} %multiply_convert_fusion.2.query_ref, bf16[512,384]{1,0:T(8,128)(2,1)} %convolution_convert_fusion.21.grad_ref, bf16[1536,384]{1,0:T(8,128)(2,1)} %get-tuple-element.140.key_ref, ...), custom_call_target="tpu_custom_call" | custom-call | flops 3019898880 | bytes 6291456 | tf_op jit(solution)/shard_map/attend_text_back/pallas_call | solution.py:188
  729.8 17.3 %attend_back.1 = (f32[512,384]{1,0:T(8,128)}, bf16[2048,384]{1,0:T(8,128)(2,1)}, bf16[2048,384]{1,0:T(8,128)(2,1)}) custom-call(bf16[512,384]{1,0:T(8,128)(2,1)} %fusion.13.query_ref, bf16[512,384]{1,0:T(8,128)(2,1)} %convolution_convert_fusion.20.grad_ref, bf16[2048,384]{1,0:T(8,128)(2,1)} %get-tuple-element.136.key_ref, ...), custom_call_target="tpu_custom_call" | custom-call | flops 4026531840 | bytes 7864320 | tf_op jit(solution)/shard_map/attend_back/pallas_call | solution.py:188
  756.0 11.1 %collective-permute-done.114 = bf16[384,768]{1,0:T(8,128)(2,1)S(1)} collective-permute-done((bf16[384,768]{1,0:T(8,128)(2,1)S(1)}, bf16[384,768]{1,0:T(8,128)(2,1)S(1)}, u32[]{:S(2)}, u32[]{:S(2)}) %collective-permute-start.114) | collective-permute-done | bytes 589856 | tf_op jit(solution)/shard_map/ppermute | solution.py:294
  811.6 5.5 collective-permute-done.120
  821.8 5.2 collective-permute-done.122
  851.8 31.8 %collective-permute-done.134 = bf16[6080]{0:T(1024)(128)(2,1)S(1)} collective-permute-done((bf16[6080]{0:T(1024)(128)(2,1)S(1)}, bf16[6080]{0:T(1024)(128)(2,1)S(1)}, u32[]{:S(2)}, u32[]{:S(2)}) %collective-permute-start.134) | collective-permute-done | bytes 12192 | tf_op jit(solution)/shard_map/ppermute | solution.py:294
  922.4 17.4 %collective-permute-done.109 = bf16[64,1536]{1,0:T(8,128)(2,1)S(1)} collective-permute-done((bf16[64,1536]{1,0:T(8,128)(2,1)S(1)}, bf16[64,1536]{1,0:T(8,128)(2,1)S(1)}, u32[]{:S(2)}, u32[]{:S(2)}) %collective-permute-start.109) | collective-permute-done | bytes 196640 | tf_op jit(solution)/shard_map/ppermute | solution.py:294
  949.3 12.9 %collective-permute-done.143 = bf16[1,1,1,192,768]{4,3,2,1,0:T(8,128)(2,1)} collective-permute-done((bf16[1,1,1,192,768]{4,3,2,1,0:T(8,128)(2,1)}, bf16[1,1,1,192,768]{4,3,2,1,0:T(8,128)(2,1)}, u32[]{:S(2)}, u32[]{:S(2)}) %collective-permute-start.143) | collective-permute-done | bytes 294944 | tf_op jit(solution)/shard_map/ppermute | solution.py:294
  965.1 5.0 collective-permute-done.128
  978.0 5.6 collective-permute-done.111
  1000.3 52.1 %collective-permute-done.147 = bf16[1,1,1,192,2240]{4,3,2,1,0:T(8,128)(2,1)S(1)} collective-permute-done((bf16[1,1,1,192,2240]{4,3,2,1,0:T(8,128)(2,1)S(1)}, bf16[1,1,1,192,2240]{4,3,2,1,0:T(8,128)(2,1)S(1)}, u32[]{:S(2)}, u32[]{:S(2)}) %collective-permute-start.147) | collective-permute-done | bytes 860192 | tf_op jit(solution)/shard_map/ppermute | solution.py:294
  1053.3 18.1 %collective-permute-done.151 = bf16[1,1,1,192,2240]{4,3,2,1,0:T(8,128)(2,1)S(1)} collective-permute-done((bf16[1,1,1,192,2240]{4,3,2,1,0:T(8,128)(2,1)S(1)}, bf16[1,1,1,192,2240]{4,3,2,1,0:T(8,128)(2,1)S(1)}, u32[]{:S(2)}, u32[]{:S(2)}) %collective-permute-start.151) | collective-permute-done | bytes 860192 | tf_op jit(solution)/shard_map/ppermute | solution.py:294
  1076.3 13.7 %collective-permute-done.131 = bf16[1,1,1,192,1152]{4,3,2,1,0:T(8,128)(2,1)S(1)} collective-permute-done((bf16[1,1,1,192,1152]{4,3,2,1,0:T(8,128)(2,1)S(1)}, bf16[1,1,1,192,1152]{4,3,2,1,0:T(8,128)(2,1)S(1)}, u32[]{:S(2)}, u32[]{:S(2)}) %collective-permute-start.131) | collective-permute-done | bytes 442400 | tf_op jit(solution)/shard_map/ppermute | solution.py:294
  (976 shorter events, 487.9 us)
Async XLA Ops:
  4.2 33.2 %collective-permute-start.1 = (s32[1,5,2,256]{3,2,1,0:T(2,128)S(1)}, s32[1,5,2,256]{3,2,1,0:T(2,128)S(1)}, u32[]{:S(2)}, u32[]{:S(2)}) collective-permute-start(s32[1,5,2,256]{3,2,1,0:T(2,128)S(1)} %bitcast.362), channel_id=1, source_target_pairs={{0,16},{1,17},{2,18},{3,19},{4,20},{5,21},{6,22},{7,23},{8,24},{9,... | collective-permute-start | bytes 30728 | tf_op jit(solution)/shard_map/ppermute | solution.py:294
  10.1 71.4 %collective-permute-start.7 = (bf16[192,1152]{1,0:T(8,128)(2,1)}, bf16[192,1152]{1,0:T(8,128)(2,1)S(1)}, u32[]{:S(2)}, u32[]{:S(2)}) collective-permute-start(bf16[192,1152]{1,0:T(8,128)(2,1)} %bitcast.172), channel_id=1, source_target_pairs={{0,0},{1,8},{2,2},{3,10},{4,4},{5,12},{6,6},{7,14},{8,1},{9,9},{10... | collective-permute-start | bytes 1327112 | tf_op jit(solution)/shard_map/ppermute | solution.py:301
  18.3 44.3 %collective-permute-start = (bf16[64,1536]{1,0:T(8,128)(2,1)}, bf16[64,1536]{1,0:T(8,128)(2,1)S(1)}, u32[]{:S(2)}, u32[]{:S(2)}) collective-permute-start(bf16[64,1536]{1,0:T(8,128)(2,1)} %get-tuple-element.162), channel_id=1, source_target_pairs={{0,16},{1,17},{2,18},{3,19},{4,20},{5,21},{6,22},{7,23},{8,24},{9,... | collective-permute-start | bytes 589832 | tf_op jit(solution)/shard_map/ppermute | solution.py:294
  21.4 63.9 %collective-permute-start.21 = (bf16[192,1152]{1,0:T(8,128)(2,1)}, bf16[192,1152]{1,0:T(8,128)(2,1)}, u32[]{:S(2)}, u32[]{:S(2)}) collective-permute-start(bf16[192,1152]{1,0:T(8,128)(2,1)} %pad_maximum_fusion.19), channel_id=1, source_target_pairs={{0,0},{1,8},{2,2},{3,10},{4,4},{5,12},{6,6},{7,14},{8,1},{9,9},{10... | collective-permute-start | bytes 1327112 | tf_op jit(solution)/shard_map/ppermute | solution.py:301
  37.4 37.1 %collective-permute-start.40 = (bf16[192,768]{1,0:T(8,128)(2,1)}, bf16[192,768]{1,0:T(8,128)(2,1)}, u32[]{:S(2)}, u32[]{:S(2)}) collective-permute-start(bf16[192,768]{1,0:T(8,128)(2,1)} %bitcast.174), channel_id=1, source_target_pairs={{0,0},{1,8},{2,2},{3,10},{4,4},{5,12},{6,6},{7,14},{8,1},{9,9},{10... | collective-permute-start | bytes 884744 | tf_op jit(solution)/shard_map/ppermute | solution.py:301
  71.1 40.5 %collective-permute-start.67 = (bf16[192,2240]{1,0:T(8,128)(2,1)}, bf16[192,2240]{1,0:T(8,128)(2,1)S(1)}, u32[]{:S(2)}, u32[]{:S(2)}) collective-permute-start(bf16[192,2240]{1,0:T(8,128)(2,1)} %bitcast.402), channel_id=1, source_target_pairs={{0,0},{1,8},{2,2},{3,10},{4,4},{5,12},{6,6},{7,14},{8,1},{9,9},{10... | collective-permute-start | bytes 2580488 | tf_op jit(solution)/shard_map/ppermute | solution.py:301
  74.5 41.5 %collective-permute-start.59 = (bf16[192,2240]{1,0:T(8,128)(2,1)S(1)}, bf16[192,2240]{1,0:T(8,128)(2,1)S(1)}, u32[]{:S(2)}, u32[]{:S(2)}) collective-permute-start(bf16[192,2240]{1,0:T(8,128)(2,1)S(1)} %copy-done.134), channel_id=1, source_target_pairs={{0,0},{1,8},{2,2},{3,10},{4,4},{5,12},{6,6},{7,14},{8,1},{9,9},{10... | collective-permute-start | bytes 2580488 | tf_op jit(solution)/shard_map/ppermute | solution.py:301
  76.6 235.3 %collective-permute-start.6 = (bf16[128,1536]{1,0:T(8,128)(2,1)S(1)}, bf16[128,1536]{1,0:T(8,128)(2,1)S(1)}, u32[]{:S(2)}, u32[]{:S(2)}) collective-permute-start(bf16[128,1536]{1,0:T(8,128)(2,1)S(1)} %fusion.32), channel_id=1, source_target_pairs={{0,10},{1,11},{2,8},{3,9},{4,14},{5,15},{6,12},{7,13},{8,2},{9,3},... | collective-permute-start | bytes 1179656 | tf_op jit(solution)/shard_map/ppermute | solution.py:294
  96.4 215.6 %collective-permute-start.5 = (bf16[128,1536]{1,0:T(8,128)(2,1)S(1)}, bf16[128,1536]{1,0:T(8,128)(2,1)S(1)}, u32[]{:S(2)}, u32[]{:S(2)}) collective-permute-start(bf16[128,1536]{1,0:T(8,128)(2,1)S(1)} %fusion.32), channel_id=1, source_target_pairs={{0,8},{1,9},{2,10},{3,11},{4,12},{5,13},{6,14},{7,15},{8,0},{9,1},... | collective-permute-start | bytes 1179656 | tf_op jit(solution)/shard_map/ppermute | solution.py:294
  111.5 55.4 %collective-permute-start.39 = (bf16[192,1536]{1,0:T(8,128)(2,1)S(1)}, bf16[192,1536]{1,0:T(8,128)(2,1)S(1)}, u32[]{:S(2)}, u32[]{:S(2)}) collective-permute-start(bf16[192,1536]{1,0:T(8,128)(2,1)S(1)} %pad_maximum_fusion.14), channel_id=1, source_target_pairs={{0,8},{1,9},{2,10},{3,11},{4,12},{5,13},{6,14},{7,15},{8,0},{9,1},... | collective-permute-start | bytes 1769480 | tf_op jit(solution)/shard_map/ppermute | solution.py:294
  111.6 51.6 %collective-permute-start.44 = (bf16[192,768]{1,0:T(8,128)(2,1)}, bf16[192,768]{1,0:T(8,128)(2,1)S(1)}, u32[]{:S(2)}, u32[]{:S(2)}) collective-permute-start(bf16[192,768]{1,0:T(8,128)(2,1)} %collective-permute-done.40), channel_id=1, source_target_pairs={{0,1},{1,0},{2,3},{3,2},{4,5},{5,4},{6,7},{7,6},{8,9},{9,8},{10,11... | collective-permute-start | bytes 884744 | tf_op jit(solution)/shard_map/ppermute | solution.py:294
  165.2 147.5 %collective-permute-start.4 = (bf16[128,1536]{1,0:T(8,128)(2,1)S(1)}, bf16[128,1536]{1,0:T(8,128)(2,1)S(1)}, u32[]{:S(2)}, u32[]{:S(2)}) collective-permute-start(bf16[128,1536]{1,0:T(8,128)(2,1)S(1)} %fusion.32), channel_id=1, source_target_pairs={{0,2},{1,3},{2,0},{3,1},{4,6},{5,7},{6,4},{7,5},{8,10},{9,11},{10,... | collective-permute-start | bytes 1179656 | tf_op jit(solution)/shard_map/ppermute | solution.py:294
  166.7 44.1 %collective-permute-start.11 = (bf16[192,1152]{1,0:T(8,128)(2,1)S(1)}, bf16[192,1152]{1,0:T(8,128)(2,1)S(1)}, u32[]{:S(2)}, u32[]{:S(2)}) collective-permute-start(bf16[192,1152]{1,0:T(8,128)(2,1)S(1)} %collective-permute-done.7), channel_id=1, source_target_pairs={{0,1},{1,0},{2,3},{3,2},{4,5},{5,4},{6,7},{7,6},{8,9},{9,8},{10,11... | collective-permute-start | bytes 1327112 | tf_op jit(solution)/shard_map/ppermute | solution.py:294
  227.2 41.4 %collective-permute-start.68 = (bf16[192,2240]{1,0:T(8,128)(2,1)S(1)}, bf16[192,2240]{1,0:T(8,128)(2,1)S(1)}, u32[]{:S(2)}, u32[]{:S(2)}) collective-permute-start(bf16[192,2240]{1,0:T(8,128)(2,1)S(1)} %collective-permute-done.67), channel_id=1, source_target_pairs={{0,16},{1,17},{2,18},{3,19},{4,20},{5,21},{6,22},{7,23},{8,24},{9,... | collective-permute-start | bytes 2580488 | tf_op jit(solution)/shard_map/ppermute | solution.py:294
  234.2 35.4 %collective-permute-start.69 = (bf16[192,2240]{1,0:T(8,128)(2,1)S(1)}, bf16[192,2240]{1,0:T(8,128)(2,1)S(1)}, u32[]{:S(2)}, u32[]{:S(2)}) collective-permute-start(bf16[192,2240]{1,0:T(8,128)(2,1)S(1)} %collective-permute-done.67), channel_id=1, source_target_pairs={{0,4},{1,5},{2,6},{3,7},{4,0},{5,1},{6,2},{7,3},{8,12},{9,13},{10,... | collective-permute-start | bytes 2580488 | tf_op jit(solution)/shard_map/ppermute | solution.py:294
  268.5 40.1 %collective-permute-start.60 = (bf16[192,2240]{1,0:T(8,128)(2,1)S(1)}, bf16[192,2240]{1,0:T(8,128)(2,1)S(1)}, u32[]{:S(2)}, u32[]{:S(2)}) collective-permute-start(bf16[192,2240]{1,0:T(8,128)(2,1)S(1)} %collective-permute-done.59), channel_id=1, source_target_pairs={{0,16},{1,17},{2,18},{3,19},{4,20},{5,21},{6,22},{7,23},{8,24},{9,... | collective-permute-start | bytes 2580488 | tf_op jit(solution)/shard_map/ppermute | solution.py:294
  269.5 286.7 %collective-permute-start.85 = (bf16[128,1536]{1,0:T(8,128)(2,1)}, bf16[128,1536]{1,0:T(8,128)(2,1)}, u32[]{:S(2)}, u32[]{:S(2)}) collective-permute-start(bf16[128,1536]{1,0:T(8,128)(2,1)} %get-tuple-element.119), channel_id=1, source_target_pairs={{0,10},{1,11},{2,8},{3,9},{4,14},{5,15},{6,12},{7,13},{8,2},{9,3},... | collective-permute-start | bytes 1179656 | tf_op jit(solution)/shard_map/ppermute | solution.py:294
  311.9 70.4 %collective-permute-start.71 = (bf16[192,2240]{1,0:T(8,128)(2,1)S(1)}, bf16[192,2240]{1,0:T(8,128)(2,1)S(1)}, u32[]{:S(2)}, u32[]{:S(2)}) collective-permute-start(bf16[192,2240]{1,0:T(8,128)(2,1)S(1)} %collective-permute-done.67), channel_id=1, source_target_pairs={{0,1},{1,0},{2,3},{3,2},{4,5},{5,4},{6,7},{7,6},{8,9},{9,8},{10,11... | collective-permute-start | bytes 2580488 | tf_op jit(solution)/shard_map/ppermute | solution.py:294
  312.0 36.9 %collective-permute-start.51 = (bf16[384,768]{1,0:T(8,128)(2,1)S(1)}, bf16[384,768]{1,0:T(8,128)(2,1)S(1)}, u32[]{:S(2)}, u32[]{:S(2)}) collective-permute-start(bf16[384,768]{1,0:T(8,128)(2,1)S(1)} %pad_maximum_fusion.15), channel_id=1, source_target_pairs={{0,4},{1,5},{2,6},{3,7},{4,0},{5,1},{6,2},{7,3},{8,12},{9,13},{10,... | collective-permute-start | bytes 1769480 | tf_op jit(solution)/shard_map/ppermute | solution.py:294
  312.7 35.4 %collective-permute-start.28 = (bf16[192,1152]{1,0:T(8,128)(2,1)S(1)}, bf16[192,1152]{1,0:T(8,128)(2,1)S(1)}, u32[]{:S(2)}, u32[]{:S(2)}) collective-permute-start(bf16[192,1152]{1,0:T(8,128)(2,1)S(1)} %collective-permute-done.24), channel_id=1, source_target_pairs={{0,1},{1,0},{2,3},{3,2},{4,5},{5,4},{6,7},{7,6},{8,9},{9,8},{10,11... | collective-permute-start | bytes 1327112 | tf_op jit(solution)/shard_map/ppermute | solution.py:294
  344.7 35.9 %collective-permute-start.70 = (bf16[192,2240]{1,0:T(8,128)(2,1)S(1)}, bf16[192,2240]{1,0:T(8,128)(2,1)S(1)}, u32[]{:S(2)}, u32[]{:S(2)}) collective-permute-start(bf16[192,2240]{1,0:T(8,128)(2,1)S(1)} %collective-permute-done.68), channel_id=1, source_target_pairs={{0,4},{1,5},{2,6},{3,7},{4,0},{5,1},{6,2},{7,3},{8,12},{9,13},{10,... | collective-permute-start | bytes 2580488 | tf_op jit(solution)/shard_map/ppermute | solution.py:294
  348.2 32.4 %collective-permute-start.19 = (bf16[512,768]{1,0:T(8,128)(2,1)S(1)}, bf16[512,768]{1,0:T(8,128)(2,1)S(1)}, u32[]{:S(2)}, u32[]{:S(2)}) collective-permute-start(bf16[512,768]{1,0:T(8,128)(2,1)S(1)} %pad_maximum_fusion.13), channel_id=1, source_target_pairs={{0,4},{1,5},{2,6},{3,7},{4,0},{5,1},{6,2},{7,3},{8,12},{9,13},{10,... | collective-permute-start | bytes 2359304 | tf_op jit(solution)/shard_map/ppermute | solution.py:294
  348.9 55.1 %collective-permute-start.63 = (bf16[192,2240]{1,0:T(8,128)(2,1)S(1)}, bf16[192,2240]{1,0:T(8,128)(2,1)S(1)}, u32[]{:S(2)}, u32[]{:S(2)}) collective-permute-start(bf16[192,2240]{1,0:T(8,128)(2,1)S(1)} %collective-permute-done.59), channel_id=1, source_target_pairs={{0,1},{1,0},{2,3},{3,2},{4,5},{5,4},{6,7},{7,6},{8,9},{9,8},{10,11... | collective-permute-start | bytes 2580488 | tf_op jit(solution)/shard_map/ppermute | solution.py:294
  385.7 42.9 %collective-permute-start.65 = (bf16[192,2240]{1,0:T(8,128)(2,1)}, bf16[192,2240]{1,0:T(8,128)(2,1)}, u32[]{:S(2)}, u32[]{:S(2)}) collective-permute-start(bf16[192,2240]{1,0:T(8,128)(2,1)} %collective-permute-done.61), channel_id=1, source_target_pairs={{0,1},{1,0},{2,3},{3,2},{4,5},{5,4},{6,7},{7,6},{8,9},{9,8},{10,11... | collective-permute-start | bytes 2580488 | tf_op jit(solution)/shard_map/ppermute | solution.py:294
  431.6 39.7 %collective-permute-start.74 = (bf16[192,2240]{1,0:T(8,128)(2,1)S(1)}, bf16[192,2240]{1,0:T(8,128)(2,1)S(1)}, u32[]{:S(2)}, u32[]{:S(2)}) collective-permute-start(bf16[192,2240]{1,0:T(8,128)(2,1)S(1)} %copy-done.61), channel_id=1, source_target_pairs={{0,1},{1,0},{2,3},{3,2},{4,5},{5,4},{6,7},{7,6},{8,9},{9,8},{10,11... | collective-permute-start | bytes 2580488 | tf_op jit(solution)/shard_map/ppermute | solution.py:294
  460.4 95.8 %collective-permute-start.84 = (bf16[128,1536]{1,0:T(8,128)(2,1)}, bf16[128,1536]{1,0:T(8,128)(2,1)}, u32[]{:S(2)}, u32[]{:S(2)}) collective-permute-start(bf16[128,1536]{1,0:T(8,128)(2,1)} %get-tuple-element.119), channel_id=1, source_target_pairs={{0,8},{1,9},{2,10},{3,11},{4,12},{5,13},{6,14},{7,15},{8,0},{9,1},... | collective-permute-start | bytes 1179656 | tf_op jit(solution)/shard_map/ppermute | solution.py:294
  553.9 72.9 %collective-permute-start.77 = (bf16[128,1536]{1,0:T(8,128)(2,1)}, bf16[128,1536]{1,0:T(8,128)(2,1)}, u32[]{:S(2)}, u32[]{:S(2)}) collective-permute-start(bf16[128,1536]{1,0:T(8,128)(2,1)} %get-tuple-element.153), channel_id=1, source_target_pairs={{0,10},{1,11},{2,8},{3,9},{4,14},{5,15},{6,12},{7,13},{8,2},{9,3},... | collective-permute-start | bytes 1179656 | tf_op jit(solution)/shard_map/ppermute | solution.py:294
  554.2 73.2 %collective-permute-start.76 = (bf16[128,1536]{1,0:T(8,128)(2,1)}, bf16[128,1536]{1,0:T(8,128)(2,1)}, u32[]{:S(2)}, u32[]{:S(2)}) collective-permute-start(bf16[128,1536]{1,0:T(8,128)(2,1)} %get-tuple-element.154), channel_id=1, source_target_pairs={{0,8},{1,9},{2,10},{3,11},{4,12},{5,13},{6,14},{7,15},{8,0},{9,1},... | collective-permute-start | bytes 1179656 | tf_op jit(solution)/shard_map/ppermute | solution.py:294
  575.1 47.4 %collective-permute-start.88 = (bf16[128,1536]{1,0:T(8,128)(2,1)}, bf16[128,1536]{1,0:T(8,128)(2,1)S(1)}, u32[]{:S(2)}, u32[]{:S(2)}) collective-permute-start(bf16[128,1536]{1,0:T(8,128)(2,1)} %get-tuple-element.148), channel_id=1, source_target_pairs={{0,10},{1,11},{2,8},{3,9},{4,14},{5,15},{6,12},{7,13},{8,2},{9,3},... | collective-permute-start | bytes 1179656 | tf_op jit(solution)/shard_map/ppermute | solution.py:294
  576.0 47.7 %collective-permute-start.87 = (bf16[128,1536]{1,0:T(8,128)(2,1)}, bf16[128,1536]{1,0:T(8,128)(2,1)}, u32[]{:S(2)}, u32[]{:S(2)}) collective-permute-start(bf16[128,1536]{1,0:T(8,128)(2,1)} %get-tuple-element.149), channel_id=1, source_target_pairs={{0,8},{1,9},{2,10},{3,11},{4,12},{5,13},{6,14},{7,15},{8,0},{9,1},... | collective-permute-start | bytes 1179656 | tf_op jit(solution)/shard_map/ppermute | solution.py:294
  577.8 46.0 %collective-permute-start.86 = (bf16[128,1536]{1,0:T(8,128)(2,1)}, bf16[128,1536]{1,0:T(8,128)(2,1)}, u32[]{:S(2)}, u32[]{:S(2)}) collective-permute-start(bf16[128,1536]{1,0:T(8,128)(2,1)} %get-tuple-element.147), channel_id=1, source_target_pairs={{0,2},{1,3},{2,0},{3,1},{4,6},{5,7},{6,4},{7,5},{8,10},{9,11},{10,... | collective-permute-start | bytes 1179656 | tf_op jit(solution)/shard_map/ppermute | solution.py:294
  623.8 173.0 %collective-permute-start.145 = (bf16[2,1,2,192,2240]{4,3,2,1,0:T(8,128)(2,1)}, bf16[2,1,2,192,2240]{4,3,2,1,0:T(8,128)(2,1)}, u32[]{:S(2)}, u32[]{:S(2)}) collective-permute-start(bf16[2,1,2,192,2240]{4,3,2,1,0:T(8,128)(2,1)} %constant_dynamic-slice_fusion.5), channel_id=1, source_target_pairs={{0,1},{1,0},{2,3},{3,2},{4,5},{5,4},{6,7},{7,6},{8,9},{9,8},{10,11... | collective-permute-start | bytes 10321928 | tf_op jit(solution)/shard_map/ppermute | solution.py:294
  623.8 178.5 %collective-permute-start.149 = (bf16[2,1,2,192,2240]{4,3,2,1,0:T(8,128)(2,1)}, bf16[2,1,2,192,2240]{4,3,2,1,0:T(8,128)(2,1)}, u32[]{:S(2)}, u32[]{:S(2)}) collective-permute-start(bf16[2,1,2,192,2240]{4,3,2,1,0:T(8,128)(2,1)} %constant_dynamic-slice_fusion.2), channel_id=1, source_target_pairs={{0,1},{1,0},{2,3},{3,2},{4,5},{5,4},{6,7},{7,6},{8,9},{9,8},{10,11... | collective-permute-start | bytes 10321928 | tf_op jit(solution)/shard_map/ppermute | solution.py:294
  655.9 42.0 %collective-permute-start.79 = (bf16[2,64,1536]{2,1,0:T(8,128)(2,1)}, bf16[2,64,1536]{2,1,0:T(8,128)(2,1)}, u32[]{:S(2)}, u32[]{:S(2)}) collective-permute-start(bf16[2,64,1536]{2,1,0:T(8,128)(2,1)} %maximum_select_fusion.1), channel_id=1, source_target_pairs={{0,1},{1,0},{2,3},{3,2},{4,5},{5,4},{6,7},{7,6},{8,9},{9,8},{10,11... | collective-permute-start | bytes 1179656 | tf_op jit(solution)/shard_map/ppermute | solution.py:294
  655.9 45.7 %collective-permute-start.80 = (bf16[2,64,1536]{2,1,0:T(8,128)(2,1)}, bf16[2,64,1536]{2,1,0:T(8,128)(2,1)}, u32[]{:S(2)}, u32[]{:S(2)}) collective-permute-start(bf16[2,64,1536]{2,1,0:T(8,128)(2,1)} %maximum_select_fusion.1), channel_id=1, source_target_pairs={{0,2},{1,3},{2,0},{3,1},{4,6},{5,7},{6,4},{7,5},{8,10},{9,11},{10,... | collective-permute-start | bytes 1179656 | tf_op jit(solution)/shard_map/ppermute | solution.py:294
  749.5 41.9 %collective-permute-start.101 = (bf16[1024,768]{1,0:T(8,128)(2,1)S(1)}, bf16[1024,768]{1,0:T(8,128)(2,1)S(1)}, u32[]{:S(2)}, u32[]{:S(2)}) collective-permute-start(bf16[1024,768]{1,0:T(8,128)(2,1)S(1)} %slice.823), channel_id=1, source_target_pairs={{0,1},{1,0},{2,3},{3,2},{4,5},{5,4},{6,7},{7,6},{8,9},{9,8},{10,11... | collective-permute-start | bytes 4718600 | tf_op jit(solution)/shard_map/ppermute | solution.py:294
  793.9 33.1 %collective-permute-start.102 = (bf16[512,768]{1,0:T(8,128)(2,1)}, bf16[512,768]{1,0:T(8,128)(2,1)}, u32[]{:S(2)}, u32[]{:S(2)}) collective-permute-start(bf16[512,768]{1,0:T(8,128)(2,1)} %slice.825), channel_id=1, source_target_pairs={{0,4},{1,5},{2,6},{3,7},{4,0},{5,1},{6,2},{7,3},{8,12},{9,13},{10,... | collective-permute-start | bytes 2359304 | tf_op jit(solution)/shard_map/ppermute | solution.py:294
  796.8 104.1 %collective-permute-start.138 = (bf16[2,1,1,192,1152]{4,3,2,1,0:T(8,128)(2,1)}, bf16[2,1,1,192,1152]{4,3,2,1,0:T(8,128)(2,1)}, u32[]{:S(2)}, u32[]{:S(2)}) collective-permute-start(bf16[2,1,1,192,1152]{4,3,2,1,0:T(8,128)(2,1)} %constant_dynamic-slice_fusion.10), channel_id=1, source_target_pairs={{0,4},{1,5},{2,6},{3,7},{4,0},{5,1},{6,2},{7,3},{8,12},{9,13},{10,... | collective-permute-start | bytes 2654216 | tf_op jit(solution)/shard_map/ppermute | solution.py:294
  802.3 187.2 %collective-permute-start.146 = (bf16[2,1,1,192,2240]{4,3,2,1,0:T(8,128)(2,1)}, bf16[2,1,1,192,2240]{4,3,2,1,0:T(8,128)(2,1)}, u32[]{:S(2)}, u32[]{:S(2)}) collective-permute-start(bf16[2,1,1,192,2240]{4,3,2,1,0:T(8,128)(2,1)} %constant_dynamic-slice_fusion.4), channel_id=1, source_target_pairs={{0,4},{1,5},{2,6},{3,7},{4,0},{5,1},{6,2},{7,3},{8,12},{9,13},{10,... | collective-permute-start | bytes 5160968 | tf_op jit(solution)/shard_map/ppermute | solution.py:294
  820.9 83.8 %collective-permute-start.142 = (bf16[2,1,1,192,768]{4,3,2,1,0:T(8,128)(2,1)}, bf16[2,1,1,192,768]{4,3,2,1,0:T(8,128)(2,1)}, u32[]{:S(2)}, u32[]{:S(2)}) collective-permute-start(bf16[2,1,1,192,768]{4,3,2,1,0:T(8,128)(2,1)} %constant_dynamic-slice_fusion.7), channel_id=1, source_target_pairs={{0,4},{1,5},{2,6},{3,7},{4,0},{5,1},{6,2},{7,3},{8,12},{9,13},{10,... | collective-permute-start | bytes 1769480 | tf_op jit(solution)/shard_map/ppermute | solution.py:294
  827.0 68.2 %collective-permute-start.123 = (bf16[2,48,1536]{2,1,0:T(8,128)(2,1)}, bf16[2,48,1536]{2,1,0:T(8,128)(2,1)}, u32[]{:S(2)}, u32[]{:S(2)}) collective-permute-start(bf16[2,48,1536]{2,1,0:T(8,128)(2,1)} %collective-permute-done.122), channel_id=1, source_target_pairs={{0,1},{1,0},{2,3},{3,2},{4,5},{5,4},{6,7},{7,6},{8,9},{9,8},{10,11... | collective-permute-start | bytes 884744 | tf_op jit(solution)/shard_map/ppermute | solution.py:294
  849.8 33.8 %collective-permute-start.134 = (bf16[6080]{0:T(1024)(128)(2,1)S(1)}, bf16[6080]{0:T(1024)(128)(2,1)S(1)}, u32[]{:S(2)}, u32[]{:S(2)}) collective-permute-start(bf16[6080]{0:T(1024)(128)(2,1)S(1)} %add_convert_fusion.28), channel_id=1, source_target_pairs={{0,4},{1,5},{2,6},{3,7},{4,0},{5,1},{6,2},{7,3},{8,12},{9,13},{10,... | collective-permute-start | bytes 36488 | tf_op jit(solution)/shard_map/ppermute | solution.py:294
  904.7 87.6 %collective-permute-start.150 = (bf16[2,1,1,192,2240]{4,3,2,1,0:T(8,128)(2,1)}, bf16[2,1,1,192,2240]{4,3,2,1,0:T(8,128)(2,1)}, u32[]{:S(2)}, u32[]{:S(2)}) collective-permute-start(bf16[2,1,1,192,2240]{4,3,2,1,0:T(8,128)(2,1)} %constant_dynamic-slice_fusion.1), channel_id=1, source_target_pairs={{0,4},{1,5},{2,6},{3,7},{4,0},{5,1},{6,2},{7,3},{8,12},{9,13},{10,... | collective-permute-start | bytes 5160968 | tf_op jit(solution)/shard_map/ppermute | solution.py:294
  908.1 89.4 %collective-permute-start.129 = (bf16[2,1,2,192,1152]{4,3,2,1,0:T(8,128)(2,1)}, bf16[2,1,2,192,1152]{4,3,2,1,0:T(8,128)(2,1)}, u32[]{:S(2)}, u32[]{:S(2)}) collective-permute-start(bf16[2,1,2,192,1152]{4,3,2,1,0:T(8,128)(2,1)} %constant_dynamic-slice_fusion.14), channel_id=1, source_target_pairs={{0,1},{1,0},{2,3},{3,2},{4,5},{5,4},{6,7},{7,6},{8,9},{9,8},{10,11... | collective-permute-start | bytes 5308424 | tf_op jit(solution)/shard_map/ppermute | solution.py:294
  910.5 53.5 %collective-permute-start.139 = (bf16[1,1,1,192,1152]{4,3,2,1,0:T(8,128)(2,1)}, bf16[1,1,1,192,1152]{4,3,2,1,0:T(8,128)(2,1)}, u32[]{:S(2)}, u32[]{:S(2)}) collective-permute-start(bf16[1,1,1,192,1152]{4,3,2,1,0:T(8,128)(2,1)} %constant_dynamic-slice_fusion.9), channel_id=1, source_target_pairs={{0,16},{1,17},{2,18},{3,19},{4,20},{5,21},{6,22},{7,23},{8,24},{9,... | collective-permute-start | bytes 1327112 | tf_op jit(solution)/shard_map/ppermute | solution.py:294
  992.3 60.1 %collective-permute-start.147 = (bf16[1,1,1,192,2240]{4,3,2,1,0:T(8,128)(2,1)S(1)}, bf16[1,1,1,192,2240]{4,3,2,1,0:T(8,128)(2,1)S(1)}, u32[]{:S(2)}, u32[]{:S(2)}) collective-permute-start(bf16[1,1,1,192,2240]{4,3,2,1,0:T(8,128)(2,1)S(1)} %constant_dynamic-slice_fusion.3), channel_id=1, source_target_pairs={{0,16},{1,17},{2,18},{3,19},{4,20},{5,21},{6,22},{7,23},{8,24},{9,... | collective-permute-start | bytes 2580488 | tf_op jit(solution)/shard_map/ppermute | solution.py:294
  994.6 76.9 %collective-permute-start.151 = (bf16[1,1,1,192,2240]{4,3,2,1,0:T(8,128)(2,1)S(1)}, bf16[1,1,1,192,2240]{4,3,2,1,0:T(8,128)(2,1)S(1)}, u32[]{:S(2)}, u32[]{:S(2)}) collective-permute-start(bf16[1,1,1,192,2240]{4,3,2,1,0:T(8,128)(2,1)S(1)} %constant_dynamic-slice_fusion), channel_id=1, source_target_pairs={{0,16},{1,17},{2,18},{3,19},{4,20},{5,21},{6,22},{7,23},{8,24},{9,... | collective-permute-start | bytes 2580488 | tf_op jit(solution)/shard_map/ppermute | solution.py:294
  999.6 72.8 %collective-permute-start.130 = (bf16[2,1,1,192,1152]{4,3,2,1,0:T(8,128)(2,1)S(1)}, bf16[2,1,1,192,1152]{4,3,2,1,0:T(8,128)(2,1)S(1)}, u32[]{:S(2)}, u32[]{:S(2)}) collective-permute-start(bf16[2,1,1,192,1152]{4,3,2,1,0:T(8,128)(2,1)S(1)} %constant_dynamic-slice_fusion.13), channel_id=1, source_target_pairs={{0,4},{1,5},{2,6},{3,7},{4,0},{5,1},{6,2},{7,3},{8,12},{9,13},{10,... | collective-permute-start | bytes 2654216 | tf_op jit(solution)/shard_map/ppermute | solution.py:294
  (275 other events, 5485.6 us)

commit v2 on v1

v2 whole, which is shorter than its diff:
```python
import math

import jax
import jax.numpy as jnp
from jax import lax
from jax.experimental import pallas as pl
from jax.experimental.layout import Layout, with_layout_constraint
from jax.experimental.pallas import tpu as pltpu
from jax.sharding import PartitionSpec as P

HD = 128
TXT = 512
EPS = 1e-06
NEG = -1e30
F32 = jnp.float32
BF16 = jnp.bfloat16
AXES = ("seq", "tensor")
SCALE = 1.0 / math.sqrt(HD)
SCALE_TWO = SCALE * math.log2(math.e)
STEP = 32


def nn(a, b):
    return lax.dot_general(a, b, (((1,), (0,)), ((), ())), preferred_element_type=F32)


def nt(a, b):
    return lax.dot_general(a, b, (((1,), (1,)), ((), ())), preferred_element_type=F32)


def tn(a, b):
    return lax.dot_general(a, b, (((0,), (0,)), ((), ())), preferred_element_type=F32)


def shape_of(rows, cols, kind=F32):
    return jax.ShapeDtypeStruct((rows, cols), kind)


def padded_bytes(array):
    size = jnp.dtype(array.dtype).itemsize
    rows, cols = array.shape[-2:]
    return -(-rows // (32 // size)) * (32 // size) * -(-cols // HD) * HD * size


def vmem_call(kernel, outs, args, name, scratch=(), room=2):
    whole = pl.BlockSpec(memory_space=pltpu.VMEM)
    held = sum(padded_bytes(a) for a in (*outs, *args, *scratch))
    return pl.pallas_call(
        kernel,
        out_shape=outs,
        in_specs=[whole] * len(args),
        out_specs=[whole] * len(outs),
        scratch_shapes=list(scratch),
        cost_estimate=pl.CostEstimate(flops=1024, bytes_accessed=1024, transcendentals=0),
        compiler_params=pltpu.CompilerParams(
            vmem_limit_bytes=min(held + room * 2**20, 60 * 2**20)
        ),
        name=name,
    )(*args)


def by_rows(rows, step, body):
    def one(i, carry):
        body(pl.ds(pl.multiple_of(i * step, step), step))
        return carry

    lax.fori_loop(0, rows // step, one, 0)


def center_of(values):
    center = values - jnp.mean(values, -1, keepdims=True)
    return center, lax.rsqrt(jnp.mean(center * center, -1, keepdims=True) + EPS)


def pull_norm(center, inverse, cotangent):
    normed = center * inverse
    return inverse * (
        cotangent
        - jnp.mean(cotangent, -1, keepdims=True)
        - normed * jnp.mean(cotangent * normed, -1, keepdims=True)
    )


def chooser(vec_ref, ids, latents):
    def choose(number):
        out = vec_ref[number : number + 1, :]
        for latent in range(1, latents):
            row = latent * 6 + number
            out = jnp.where(ids == latent, vec_ref[row : row + 1, :], out)
        return out

    return choose


def add_latents(sums_ref, first, ids, value, latents):
    for latent in range(latents):
        row = first + latent
        part = jnp.sum(jnp.where(ids == latent, value, 0.0), 0, keepdims=True)
        sums_ref[row : row + 1, :] += part


def add_row(sums_ref, row, value):
    sums_ref[row : row + 1, :] += jnp.sum(value.astype(F32), 0, keepdims=True)


def share_kernels(latents):
    base = 6 * latents

    def three(refs, rows):
        return sum(ref[rows, :].astype(F32) for ref in refs)

    def first(state_ref, grad_ref, ids_ref, vec_ref, act_ref, top_ref):
        def body(rows):
            choose = chooser(vec_ref, ids_ref[rows, :], latents)
            center, inverse = center_of(state_ref[rows, :].astype(F32))
            act_ref[rows, :] = (
                center * inverse * (1.0 + choose(1)) + choose(0)
            ).astype(BF16)
            top_ref[rows, :] = (grad_ref[rows, :].astype(F32) * choose(5)).astype(BF16)

        by_rows(state_ref.shape[0], STEP, body)

    def middle(p0, p1, p2, state_ref, ids_ref, vec_ref, next_ref, branch_ref, act_ref):
        def body(rows):
            choose = chooser(vec_ref, ids_ref[rows, :], latents)
            branch = three((p0, p1, p2), rows) + vec_ref[base : base + 1, :]
            state = state_ref[rows, :].astype(F32) + branch * choose(2)
            branch_ref[rows, :] = branch
            next_ref[rows, :] = state
            center, inverse = center_of(state)
            act_ref[rows, :] = (
                center * inverse * vec_ref[base + 3 : base + 4, :]
                + vec_ref[base + 4 : base + 5, :]
            ).astype(BF16)

        by_rows(state_ref.shape[0], STEP, body)

    def last(p0, p1, p2, state_ref, ids_ref, vec_ref, next_ref, act_ref):
        def body(rows):
            choose = chooser(vec_ref, ids_ref[rows, :], latents)
            branch = three((p0, p1, p2), rows) + vec_ref[base + 1 : base + 2, :]
            state = state_ref[rows, :] + branch
            next_ref[rows, :] = state
            center, inverse = center_of(state)
            act_ref[rows, :] = (
                center * inverse * (1.0 + choose(4)) + choose(3)
            ).astype(BF16)

        by_rows(state_ref.shape[0], STEP, body)

    def result(p0, p1, p2, state_ref, grad_ref, ids_ref, vec_ref, out_ref, sums_ref):
        sums_ref[...] = jnp.zeros_like(sums_ref)

        def body(rows):
            ids = ids_ref[rows, :]
            choose = chooser(vec_ref, ids, latents)
            branch = three((p0, p1, p2), rows) + vec_ref[base + 2 : base + 3, :]
            out_ref[rows, :] = (state_ref[rows, :] + branch * choose(5)).astype(BF16)
            grad = grad_ref[rows, :].astype(F32)
            add_latents(sums_ref, 0, ids, grad * branch, latents)

        by_rows(state_ref.shape[0], STEP, body)

    def back_last(
        p0, p1, p2, state_ref, grad_ref, top_ref, ids_ref, vec_ref, next_ref, low_ref, sums_ref
    ):
        sums_ref[...] = jnp.zeros_like(sums_ref)

        def body(rows):
            ids = ids_ref[rows, :]
            choose = chooser(vec_ref, ids, latents)
            grad_act = three((p0, p1, p2), rows)
            center, inverse = center_of(state_ref[rows, :])
            grad = grad_ref[rows, :].astype(F32) + pull_norm(
                center, inverse, grad_act * (1.0 + choose(4))
            )
            next_ref[rows, :] = grad
            low = grad.astype(BF16)
            low_ref[rows, :] = low
            add_latents(sums_ref, 0, ids, grad_act, latents)
            add_latents(sums_ref, latents, ids, grad_act * center * inverse, latents)
            add_row(sums_ref, 2 * latents, low)
            add_row(sums_ref, 2 * latents + 1, top_ref[rows, :])

        by_rows(state_ref.shape[0], STEP, body)

    def back_middle(
        p0,
        p1,
        p2,
        state_ref,
        grad_ref,
        branch_ref,
        ids_ref,
        vec_ref,
        next_ref,
        low_ref,
        sums_ref,
    ):
        sums_ref[...] = jnp.zeros_like(sums_ref)

        def body(rows):
            ids = ids_ref[rows, :]
            choose = chooser(vec_ref, ids, latents)
            grad_act = three((p0, p1, p2), rows)
            center, inverse = center_of(state_ref[rows, :])
            grad = grad_ref[rows, :] + pull_norm(
                center, inverse, grad_act * vec_ref[base + 3 : base + 4, :]
            )
            next_ref[rows, :] = grad
            low = (grad * choose(2)).astype(BF16)
            low_ref[rows, :] = low
            add_latents(sums_ref, 0, ids, grad * branch_ref[rows, :], latents)
            add_row(sums_ref, latents, low)
            add_row(sums_ref, latents + 1, grad_act * center * inverse)
            add_row(sums_ref, latents + 2, grad_act)

        by_rows(state_ref.shape[0], STEP, body)

    def back_first(p0, p1, p2, state_ref, grad_ref, ids_ref, vec_ref, out_ref, sums_ref):
        sums_ref[...] = jnp.zeros_like(sums_ref)

        def body(rows):
            ids = ids_ref[rows, :]
            choose = chooser(vec_ref, ids, latents)
            grad_act = three((p0, p1, p2), rows)
            center, inverse = center_of(state_ref[rows, :].astype(F32))
            out_ref[rows, :] = (
                grad_ref[rows, :] + pull_norm(center, inverse, grad_act * (1.0 + choose(1)))
            ).astype(BF16)
            add_latents(sums_ref, 0, ids, grad_act, latents)
            add_latents(sums_ref, latents, ids, grad_act * center * inverse, latents)

        by_rows(state_ref.shape[0], STEP, body)

    return first, middle, last, result, back_last, back_middle, back_first


def join_kernel(*refs):
    start = 0
    for ref in refs[:-1]:
        rows = ref.shape[0]
        refs[-1][start : start + rows, :] = ref[...]
        start += rows


def join(pieces):
    rows, cols = sum(p.shape[0] for p in pieces), pieces[0].shape[1]
    return vmem_call(join_kernel, [shape_of(rows, cols, BF16)], pieces, "join")[0]


def fold_kernel(to_x, to_w, from_x, from_w, out_x, out_w):
    half = from_x.shape[0]
    add = lambda a, b: (a.astype(F32) + b.astype(F32)).astype(BF16)
    out_x[:half, :] = to_x[:half, :]
    out_x[half:, :] = add(to_x[half:, :], from_w[...])
    out_w[:half, :] = add(to_w[:half, :], from_x[...])
    out_w[half:, :] = to_w[half:, :]


def project_out(values, weight, first, count):
    rows, width = values.shape[0], weight.shape[0]
    share = rows // 4
    heights = (share, share, share, share // 2, share // 2)
    tile = 256 if width % 256 == 0 else width

    def kernel(value_ref, weight_ref, *outs):
        for n in range(width // tile):
            cols = slice(n * tile, (n + 1) * tile)
            part = nt(value_ref[...], weight_ref[cols, first : first + count]).astype(BF16)
            start = 0
            for out in outs:
                out[:, cols] = part[start : start + out.shape[0], :]
                start += out.shape[0]

    return vmem_call(
        kernel, [shape_of(h, width, BF16) for h in heights], (values, weight), "project_out"
    )


def put_lines(out_ref, columns):
    rows = columns[0].shape[0]
    lane = lax.broadcasted_iota(jnp.int32, (rows, HD), 1)
    flat = jnp.zeros((rows, HD), F32)
    for i, column in enumerate(columns):
        flat = jnp.where(lane == i, column, flat)
    out_ref[...] = flat.T[:8, :]


def take_lines(refs):
    rows = refs[0].shape[1]
    share = rows // 4
    total = refs[0][...]
    for j in (1, 2, 3):
        total = total + jnp.concatenate(
            [refs[j][:, (i ^ j) * share : ((i ^ j) + 1) * share] for i in range(4)], 1
        )
    return jnp.concatenate([total] * (HD // 8), 0).T


def squares(values, columns, count):
    rows = values.shape[0]

    def kernel(value_ref, out_ref):
        parts = []
        for i in range(count):
            part = value_ref[:, i * columns : (i + 1) * columns]
            parts.append(jnp.sum(part * part, -1, keepdims=True))
        put_lines(out_ref, parts)

    return vmem_call(kernel, [shape_of(8, rows)], (values,), "squares")[0]


def turn(values, cosine, signed):
    even = lax.broadcasted_iota(jnp.int32, values.shape, 1) % 2 == 0
    other = jnp.where(even, pltpu.roll(values, HD - 1, 1), pltpu.roll(values, 1, 1))
    return values * cosine + other * signed


def shape_heads(projected, lines, gains, cosine, signed, width):
    rows = projected.shape[0]
    columns = gains.shape[1]

    def kernel(value_ref, l0, l1, l2, l3, gain_ref, cos_ref, sin_ref, query_ref, pair_ref, inv_ref):
        inv_ref[...] = lax.rsqrt(take_lines((l0, l1, l2, l3)) / width + EPS)

        def body(here):
            cos, sin = cos_ref[here, :], sin_ref[here, :]
            for head in range(columns // HD):
                for i, ref in ((0, query_ref), (1, pair_ref)):
                    at = i * columns + head * HD
                    cols = slice(head * HD, (head + 1) * HD)
                    value = (
                        value_ref[here, at : at + HD]
                        * inv_ref[here, i : i + 1]
                        * gain_ref[i : i + 1, cols]
                    )
                    ref[here, cols] = turn(value, cos, sin).astype(BF16)
            pair_ref[here, columns:] = value_ref[here, 2 * columns :].astype(BF16)

        by_rows(rows, STEP, body)

    return vmem_call(
        kernel,
        [shape_of(rows, columns, BF16), shape_of(rows, 2 * columns, BF16), shape_of(rows, HD)],
        (projected, *lines, gains, cosine, signed),
        "shape_heads",
    )


def shape_cross(projected, lines, gains, width):
    rows, columns = projected.shape

    def kernel(value_ref, l0, l1, l2, l3, gain_ref, query_ref, inv_ref):
        inv_ref[...] = lax.rsqrt(take_lines((l0, l1, l2, l3)) / width + EPS)

        def body(here):
            query_ref[here, :] = (
                value_ref[here, :] * inv_ref[here, 0:1] * gain_ref[2:3, :]
            ).astype(BF16)

        by_rows(rows, STEP, body)

    return vmem_call(
        kernel,
        [shape_of(rows, columns, BF16), shape_of(rows, HD)],
        (projected, *lines, gains),
        "shape_cross",
    )


def turn_back(dquery, pair, projected, gains, cosine, signed):
    rows, columns = dquery.shape

    def kernel(dq_ref, pair_ref, value_ref, gain_ref, cos_ref, sin_ref, gq_ref, gk_ref, line_ref, sum_ref):
        lane = lax.broadcasted_iota(jnp.int32, (STEP, HD), 1)

        def body(here):
            cos, sin = cos_ref[here, :], -sin_ref[here, :]
            totals = []
            for i, ref, out in ((0, dq_ref, gq_ref), (1, pair_ref, gk_ref)):
                total = jnp.zeros((STEP, 1), F32)
                for head in range(columns // HD):
                    cols = slice(head * HD, (head + 1) * HD)
                    at = i * columns + head * HD
                    back = turn(ref[here, cols].astype(F32), cos, sin)
                    out[here, cols] = back
                    total = total + jnp.sum(
                        gain_ref[i : i + 1, cols] * back * value_ref[here, at : at + HD],
                        -1,
                        keepdims=True,
                    )
                totals.append(total)
            sum_ref[here, :] = jnp.where(
                lane == 0, totals[0], jnp.where(lane == 1, totals[1], 0.0)
            )

        by_rows(rows, STEP, body)
        line_ref[...] = sum_ref[...].T[:8, :]

    return vmem_call(
        kernel,
        [shape_of(rows, columns), shape_of(rows, columns), shape_of(8, rows)],
        (dquery, pair, projected, gains, cosine, signed),
        "turn_back",
        [pltpu.VMEM((rows, HD), F32)],
    )


def rms_pull(pre, inverse, gain, cotangent, summed, width):
    scaled = inverse * inverse * inverse * summed / width
    return (inverse * gain * cotangent - pre * scaled).astype(BF16)


def back_heads(gquery, gkey, projected, inverse, pair, lines, gains, width):
    rows, columns = gquery.shape

    def kernel(gq_ref, gk_ref, value_ref, inv_ref, pair_ref, l0, l1, l2, l3, gain_ref, out_ref, sums_ref, sum_ref):
        sum_ref[...] = take_lines((l0, l1, l2, l3))
        sums_ref[...] = jnp.zeros_like(sums_ref)

        def body(here):
            for i, ref in ((0, gq_ref), (1, gk_ref)):
                cols = slice(i * columns, (i + 1) * columns)
                pre, grad, inv = value_ref[here, cols], ref[here, :], inv_ref[here, i : i + 1]
                low = rms_pull(pre, inv, gain_ref[i : i + 1, :], grad, sum_ref[here, i : i + 1], width)
                out_ref[here, cols] = low
                sums_ref[0:1, cols] += jnp.sum(low.astype(F32), 0, keepdims=True)
                sums_ref[1:2, cols] += jnp.sum(grad * pre * inv, 0, keepdims=True)
            cols = slice(2 * columns, 3 * columns)
            value = pair_ref[here, columns:]
            out_ref[here, cols] = value
            sums_ref[0:1, cols] += jnp.sum(value.astype(F32), 0, keepdims=True)

        by_rows(rows, STEP, body)

    return vmem_call(
        kernel,
        [shape_of(rows, 3 * columns, BF16), shape_of(8, 3 * columns)],
        (gquery, gkey, projected, inverse, pair, *lines, gains),
        "back_heads",
        [pltpu.VMEM((rows, HD), F32)],
    )


def cross_lines(dquery, pre, gains):
    rows = dquery.shape[0]

    def kernel(dq_ref, pre_ref, gain_ref, line_ref):
        put_lines(
            line_ref,
            [jnp.sum(gain_ref[2:3, :] * dq_ref[...] * pre_ref[...], -1, keepdims=True)],
        )

    return vmem_call(kernel, [shape_of(8, rows)], (dquery, pre, gains), "cross_lines")[0]


def back_cross(dquery, pre, inverse, lines, gains, width):
    rows, columns = dquery.shape

    def kernel(dq_ref, pre_ref, inv_ref, l0, l1, l2, l3, gain_ref, out_ref, sums_ref, sum_ref):
        sum_ref[...] = take_lines((l0, l1, l2, l3))
        sums_ref[...] = jnp.zeros_like(sums_ref)

        def body(here):
            grad, before, inv = dq_ref[here, :], pre_ref[here, :], inv_ref[here, 0:1]
            low = rms_pull(before, inv, gain_ref[2:3, :], grad, sum_ref[here, 0:1], width)
            out_ref[here, :] = low
            sums_ref[0:1, :] += jnp.sum(low.astype(F32), 0, keepdims=True)
            sums_ref[1:2, :] += jnp.sum(grad * before * inv, 0, keepdims=True)

        by_rows(rows, STEP, body)

    return vmem_call(
        kernel,
        [shape_of(rows, columns, BF16), shape_of(8, columns)],
        (dquery, pre, inverse, *lines, gains),
        "back_cross",
        [pltpu.VMEM((rows, HD), F32)],
    )


def own_pairs(same, first, diagonal):
    if not (diagonal and first):
        return same
    row = lax.broadcasted_iota(jnp.int32, same.shape, 0)
    col = lax.broadcasted_iota(jnp.int32, same.shape, 1)
    return same | (row == col)


def attend(queries, pairs, query_code, key_code, diagonal):
    rows, width = queries.shape
    height = pairs[0].shape[0]
    count = height * len(pairs)

    def kernel(query_ref, qcode_ref, kcode_ref, *refs):
        piece_refs = refs[: len(pairs)]
        out_ref, low_ref, line_ref, score_ref = refs[len(pairs) :]
        code = qcode_ref[...]
        totals = []
        for head in range(width // HD):
            cols = slice(head * HD, (head + 1) * HD)
            query = query_ref[:, cols]
            top = None
            for i, ref in enumerate(piece_refs):
                here = slice(i * height, (i + 1) * height)
                same = own_pairs(code == kcode_ref[:, here], i == 0, diagonal)
                scores = jnp.where(same, nt(query, ref[:, cols]), NEG)
                score_ref[:, here] = scores
                peak = jnp.max(scores, -1, keepdims=True)
                top = peak if top is None else jnp.maximum(top, peak)
            out = None
            total = None
            for i, ref in enumerate(piece_refs):
                here = slice(i * height, (i + 1) * height)
                weights = jnp.exp2((score_ref[:, here] - top) * SCALE_TWO)
                score_ref[:, here] = weights
                part = jnp.sum(weights, -1, keepdims=True)
                total = part if total is None else total + part
            inverse = 1.0 / total
            for i, ref in enumerate(piece_refs):
                here = slice(i * height, (i + 1) * height)
                probs = (score_ref[:, here] * inverse).astype(BF16)
                at = width + head * HD
                part = nn(probs, ref[:, at : at + HD])
                out = part if out is None else out + part
            out_ref[:, cols] = out
            low_ref[:, cols] = out.astype(BF16)
            totals.append(top * SCALE_TWO + jnp.log2(total))
        put_lines(line_ref, totals)

    return vmem_call(
        kernel,
        [shape_of(rows, width), shape_of(rows, width, BF16), shape_of(8, rows)],
        (queries, query_code[:, None], key_code[None, :], *pairs),
        "attend" if diagonal else "attend_text",
        [pltpu.VMEM((rows, count), F32)],
        2 * len(pairs),
    )


def attend_back(queries, grads, full, lines, pairs, query_code, key_code, diagonal):
    rows, width = queries.shape
    height = pairs[0].shape[0]
    number = len(pairs)

    def kernel(query_ref, grad_ref, full_ref, line_ref, qcode_ref, kcode_ref, *refs):
        piece_refs = refs[:number]
        dquery_ref, near_ref, far_ref = refs[number:]
        heads = width // HD
        lane = lax.broadcasted_iota(jnp.int32, (rows, HD), 1)
        flat = jnp.zeros((rows, HD), F32)
        for head in range(heads):
            cols = slice(head * HD, (head + 1) * HD)
            delta = jnp.sum(grad_ref[:, cols].astype(F32) * full_ref[:, cols], -1, keepdims=True)
            flat = jnp.where(lane == head, delta, flat)
        deltas = flat.T
        code = qcode_ref[...]
        for head in range(heads):
            cols = slice(head * HD, (head + 1) * HD)
            query, grad = query_ref[:, cols], grad_ref[:, cols]
            dquery = None
            for i, ref in enumerate(piece_refs):
                here = slice(i * height, (i + 1) * height)
                key, value = ref[:, cols], ref[:, width + head * HD : width + (head + 1) * HD]
                same = own_pairs(kcode_ref[here, :] == code, i == 0, diagonal)
                weights = jnp.exp2(nt(key, query) * SCALE_TWO - line_ref[head : head + 1, :])
                probs = jnp.where(same, weights, 0.0)
                dscores = (probs * (nt(value, grad) - deltas[head : head + 1, :])).astype(BF16)
                out, start = (near_ref, i) if 2 * i < number else (far_ref, i - number // 2)
                spot = slice(start * height, (start + 1) * height)
                out[spot, cols] = (nn(dscores, query) * SCALE).astype(BF16)
                out[spot, width + head * HD : width + (head + 1) * HD] = nn(
                    probs.astype(BF16), grad
                ).astype(BF16)
                part = tn(dscores, key)
                dquery = part if dquery is None else dquery + part
            dquery_ref[:, cols] = dquery * SCALE

    half = shape_of(height * number // 2, 2 * width, BF16)
    return vmem_call(
        kernel,
        [shape_of(rows, width), half, half],
        (queries, grads, full, lines, query_code[None, :], key_code[:, None], *pairs),
        "attend_back" if diagonal else "attend_text_back",
        (),
        2 * number,
    )


def rope_tables(frames, rows_pos, cols_pos):
    part_size = HD // 6
    widths = (HD - 4 * part_size, 2 * part_size, 2 * part_size)
    rates, picks = [], []
    for i, group_width in enumerate(widths):
        exponent = jnp.arange(0, group_width, 2).astype(F32) / group_width
        rates.append(jnp.repeat(jnp.power(10000.0, -exponent), 2))
        picks.append(jnp.full((group_width,), i, jnp.int32))
    rate, pick = jnp.concatenate(rates)[None], jnp.concatenate(picks)[None]
    places = [p.astype(F32)[:, None] for p in (frames, rows_pos, cols_pos)]
    angle = jnp.where(pick == 0, places[0], jnp.where(pick == 1, places[1], places[2])) * rate
    sign = jnp.where(jnp.arange(HD) % 2 == 0, -1.0, 1.0).astype(F32)
    return jnp.cos(angle), jnp.sin(angle) * sign[None]


def shards(
    inputs,
    text_states,
    timestep_emb,
    modulation,
    attn_in,
    in_bias,
    norm_gains,
    attn_out,
    cross_in,
    cross_out,
    cross_norm_gain,
    cross_norm_bias,
    ffn_in,
    ffn_bias,
    ffn_out,
    out_bias,
    latent_ids,
    pad_mask,
    frame_pos,
    row_pos,
    col_pos,
    cotangent,
):
    micros, tok_rows, width = inputs.shape
    text_rows = text_states.shape[1]
    latents = timestep_emb.shape[1]
    columns = attn_in.shape[2]
    hidden = ffn_in.shape[1]
    slice_rows = attn_in.shape[1]
    seq_size, tensor_size = lax.axis_size("seq"), lax.axis_size("tensor")
    places = seq_size * tensor_size
    bits = seq_size.bit_length() - 1
    s, t = lax.axis_index("seq"), lax.axis_index("tensor")
    top = bits - 1
    rest = [b for b in range(bits) if b not in (1, top)]

    def seq_bit(b):
        return (s >> b) & 1

    k, w, x, c = seq_bit(top), seq_bit(1), t >> 1, t & 1
    own_slice = (s & ~2) | (c << 1)
    hop_c, hop_x, hop_w, hop_k = 1, 2, tensor_size << 1, tensor_size << top
    hop_rest = [tensor_size << b for b in rest]
    hop_group = [0, hop_x, hop_w, hop_x | hop_w]

    def hop(value, mask):
        return lax.ppermute(value, AXES, [(d, d ^ mask) for d in range(places)])

    def swap(value):
        def other(d):
            low, high = d & 1, (d // hop_w) & 1
            return d if low == high else d ^ 1 ^ hop_w

        return lax.ppermute(value, AXES, [(d, other(d)) for d in range(places)])

    def swap_far(value):
        def other(d):
            low, high = d & 1, (d // hop_w) & 1
            return (d if low == high else d ^ 1 ^ hop_w) ^ hop_k

        return lax.ppermute(value, AXES, [(d, other(d)) for d in range(places)])

    near_masks = [hop_c] + hop_rest[::-1]
    near_groups = []
    taken = set()
    for d in range(places):
        if d not in taken:
            members = [d]
            for mask in near_masks[::-1]:
                members = members + [m ^ mask for m in members]
            taken |= set(members)
            near_groups.append(members)

    far_groups = []
    for members in near_groups:
        if not members[0] & hop_k:
            far_groups.append([m ^ mask for m in members for mask in (0, hop_k)])

    def by_k(own, far):
        return jnp.where(k == 0, jnp.stack((own, far)), jnp.stack((far, own)))

    def place_weight(block):
        return by_k(swap(block), swap_far(block))

    def gather_weight(placed):
        out = lax.all_gather(
            placed, AXES, axis=0, tiled=False, axis_index_groups=near_groups
        )
        return out.reshape(seq_size * slice_rows, -1)

    def gather_far(block):
        out = lax.all_gather(
            block, AXES, axis=0, tiled=False, axis_index_groups=far_groups
        )
        return out.reshape(seq_size * slice_rows, -1)

    def scatter_weight(grad):
        return lax.psum_scatter(
            grad,
            AXES,
            scatter_dimension=0,
            tiled=True,
            axis_index_groups=near_groups,
        ).reshape(2, slice_rows, grad.shape[1])

    def home_parts(parts):
        own = lax.dynamic_index_in_dim(parts, k, 0, keepdims=False)
        far = lax.dynamic_index_in_dim(parts, 1 - k, 0, keepdims=False)
        return swap(own), swap_far(far)

    def whole_of(home):
        return home[0].astype(F32) + home[1].astype(F32)

    def weight_grad(a, b):
        return with_layout_constraint(tn(a, b).astype(BF16), Layout((0, 1)))

    def slice_at(place):
        number = (place & 1) << top
        place >>= 1
        for bit_number in rest:
            number |= (place & 1) << bit_number
            place >>= 1
        return number | (place << 1)

    order = [slice_at(place) for place in range(seq_size)]
    order_back = [order.index(i) for i in range(seq_size)]

    def arrange(value, order_here):
        return jnp.concatenate(
            [value[..., i * slice_rows : (i + 1) * slice_rows] for i in order_here], -1
        )

    def tie(*values):
        return lax.optimization_barrier(values)

    def after(value, *anchors):
        return tie(value, *anchors)[0]

    def gather_pieces(value):
        pieces = [value]
        for mask in hop_rest + [hop_c]:
            pieces = pieces + [hop(p, mask) for p in pieces]
        return pieces

    def add_low(a, b):
        return (a.astype(F32) + b.astype(F32)).astype(BF16)

    def spread(value, beside=(), later=()):
        half = value.shape[0] // 2
        by_x, by_w = hop(value, hop_x), hop(value, hop_w)
        if beside:
            by_x, by_w, beside = tie(by_x, by_w, beside)
        far = (hop(by_w[:half], hop_x), hop(by_x[half:], hop_w))
        if later:
            far, later = tie(far, later)
        whole = join((value, by_x, by_w) + far)
        return (whole, *beside, *later) if beside or later else whole

    def collect(values, weight, first, count, beside=(), later=()):
        own, to_x, to_w, far_x, far_w = project_out(values, weight, first, count)
        from_x, from_w = hop(far_x, hop_x), hop(far_w, hop_w)
        if beside:
            from_x, from_w, beside = tie(from_x, from_w, beside)
        kinds = [shape_of(*to_x.shape, BF16)] * 2
        to_x, to_w = vmem_call(fold_kernel, kinds, (to_x, to_w, from_x, from_w), "fold")
        got_x, got_w = hop(to_x, hop_x), hop(to_w, hop_w)
        if later:
            got_x, got_w, later = tie(got_x, got_w, later)
        return ((own, got_x, got_w), *beside, *later)

    def lines_of(value):
        return (value,) + tuple(hop(value, m) for m in hop_group[1:])

    def text_sum(value):
        total = value
        half_rows = value.shape[-1] // 2
        for j in (1, 2, 3):
            other = hop(value, hop_group[j])
            if j > 1:
                other = jnp.concatenate((other[..., half_rows:], other[..., :half_rows]), -1)
            total = total + other
        return total

    def all_sum(value, masks):
        for mask in masks:
            value = value.astype(BF16)
            value = value.astype(F32) + hop(value, mask).astype(F32)
        return value

    def by_home(own, other):
        return jnp.where(c == w, own, other)

    piece = tok_rows // 4
    group_rows = 8 * piece
    share_rows = 2 * piece

    def take_share(array):
        parts = array.reshape(micros, 4, piece, width)
        pick = lambda micro: arrange(
            lax.dynamic_index_in_dim(
                lax.dynamic_index_in_dim(parts, micro, 0, keepdims=False), t, 0, keepdims=False
            ),
            order,
        )
        return jnp.concatenate((pick(k), hop(pick(1 - k), hop_k)), 0)

    def give_far(share):
        rows_each = share.shape[0] // 2
        share = arrange(share, order_back)
        own, far = share[:rows_each], hop(share[rows_each:], hop_k)
        return jnp.where(k == 0, jnp.stack((own, far)), jnp.stack((far, own)))

    def give_across(both):
        return both, hop(both, hop_x)

    def give_back(both, across, position):
        rows_each = both.shape[1]
        pieces = ((0, both), (1, hop(both, hop_c)), (2, across), (3, hop(across, hop_c)))
        out = jnp.zeros((micros, 4, rows_each, width), both.dtype)
        for offset, value in pieces:
            out = lax.dynamic_update_index_in_dim(out, value, position(t ^ offset), 1)
        return out.reshape(micros, 4 * rows_each, width)

    meta = jnp.stack((latent_ids, pad_mask, frame_pos, row_pos, col_pos))[None]
    for mask in [hop_k, hop_w] + hop_rest:
        meta = jnp.concatenate((meta, hop(meta, mask)), 0)
    meta = lax.dynamic_index_in_dim(meta, k, 2, keepdims=False)
    meta = meta.reshape((2,) * bits + (5, 2, 2, piece))
    meta = jnp.where(x == 1, jnp.flip(meta, bits + 1), meta)
    meta = jnp.where(c == 1, jnp.flip(meta, bits + 2), meta)
    others = list(range(bits - 2))
    meta = meta.transpose([bits, bits + 2] + others + [bits - 2, bits + 1, bits - 1, bits + 3])
    meta = meta.reshape(5, -1)
    ids_all = meta[0]
    key_code = jnp.where(meta[1] == 1, ids_all, -1)
    ids_here = ids_all[:group_rows]
    ids_share = ids_here[:share_rows, None]
    cosine, signed = rope_tables(*(meta[i, :group_rows] for i in (2, 3, 4)))

    state_in = take_share(inputs)
    table = modulation + lax.dynamic_index_in_dim(timestep_emb, k, 0, keepdims=False)
    vectors = arrange(
        jnp.concatenate(
            (
                table.reshape(latents * 6, width),
                out_bias.astype(F32),
                cross_norm_gain[None].astype(F32),
                cross_norm_bias[None].astype(F32),
            ),
            0,
        ),
        order,
    )

    pack = lambda a: a.transpose(1, 0, 2).reshape(slice_rows, -1)
    placed_attn = place_weight(pack(attn_in))
    grad_top = take_share(cotangent)
    (
        share_first,
        share_middle,
        share_last,
        share_result,
        share_back_last,
        share_back_middle,
        share_back_first,
    ) = share_kernels(latents)
    share_low = shape_of(share_rows, width, BF16)
    share_full = shape_of(share_rows, width)
    sums_shape = lambda count: shape_of(count, width)
    act_share, top_share = vmem_call(
        share_first,
        [share_low, share_low],
        (state_in, grad_top, ids_share, vectors),
        "share_first",
    )
    act_low = spread(act_share)
    w_attn = gather_weight(after(placed_attn, act_low))
    mid_block = jnp.concatenate((pack(cross_in[1:]), attn_out.T, cross_in[0], cross_out.T), 1)
    placed_mid = place_weight(after(mid_block, placed_attn))

    flat = jnp.concatenate((in_bias.reshape(-1), norm_gains.reshape(-1), ffn_bias))
    flat = by_home(flat, hop(flat, hop_c)).astype(F32)
    bias_in = flat[: 6 * columns].reshape(2, 3, columns)
    gains = flat[6 * columns : 10 * columns].reshape(4, columns)
    bias_ffn = flat[10 * columns :]

    half = text_rows // 2
    texts = text_states.reshape(micros, 2, half, width)

    def text_of(micro):
        own = lax.dynamic_index_in_dim(
            lax.dynamic_index_in_dim(texts, micro, 0, keepdims=False), c, 0, keepdims=False
        )
        return arrange(own, order)

    text_here = jnp.concatenate((text_of(k), hop(text_of(1 - k), hop_k)), 0)
    text_here = jnp.concatenate((text_here, hop(text_here, hop_w)), 0)
    number = jnp.arange(4 * half * seq_size // 2, dtype=jnp.int32)
    row, chunk = number % half, number // half
    row_k, row_w, row_rest = chunk & 1, (chunk >> 1) & 1, chunk >> 2
    place = ((row_k ^ k) << top) | ((row_w ^ w) << 1)
    for i, b in enumerate(rest):
        place = place | ((((row_rest >> i) & 1) ^ seq_bit(b)) << b)
    row_c = (row_rest >> len(rest)) ^ c
    text_code = (place * text_rows + row_c * half + row) // TXT

    act_low, placed_mid, text_here = tie(act_low, placed_mid, text_here)
    projected = nn(act_low, w_attn) + bias_in[0].reshape(1, -1)
    w_mid = gather_weight(after(placed_mid, projected))
    lines = lines_of(squares(projected, columns, 2))
    swapped_up = swap(after(ffn_in, projected))
    query_low, pair, inverse = shape_heads(projected, lines, gains, cosine, signed, width)
    pairs = gather_pieces(pair)
    pairs, swapped_up = tie(pairs, swapped_up)
    w_up = gather_far(swapped_up)
    attn_full, attn_low, attn_lines = attend(query_low, pairs, ids_here, key_code, True)
    down_block = after(ffn_out.T, query_low)
    hidden_half = hidden // 2
    down_parts = [down_block[:, :hidden_half], down_block[:, hidden_half:]]
    placed_down = [place_weight(down_parts[0])]
    text_pre = nn(text_here, w_mid[:, : 2 * columns]) + bias_in[1, 1:].reshape(1, -1)
    parts, text_pre, placed_first = collect(
        attn_low, w_mid, 2 * columns, columns, (text_pre,), (placed_down[0],)
    )
    state_one, branch_one, cross_share = vmem_call(
        share_middle,
        [share_full, share_full, share_low],
        (*parts, state_in, ids_share, vectors),
        "share_middle",
    )

    ckey_pre = text_pre[:, :columns]
    inverse_ck = lax.rsqrt(
        text_sum(jnp.sum(ckey_pre * ckey_pre, -1)[None])[0] / width + EPS
    )[:, None]
    text_pair = jnp.concatenate(
        (
            (ckey_pre * inverse_ck * gains[3]).astype(BF16),
            text_pre[:, columns:].astype(BF16),
        ),
        1,
    )

    cross_act, text_pair = spread(cross_share, (text_pair,))
    text_pairs = gather_pieces(text_pair)
    placed_second = place_weight(after(down_parts[1], placed_first))
    cquery_pre = nn(cross_act, w_mid[:, 3 * columns : 4 * columns]) + bias_in[1, 0]
    cross_lines_here = lines_of(squares(cquery_pre, columns, 1))
    cross_lines_here, text_pairs = tie(cross_lines_here, text_pairs)
    cquery_low, inverse_cq = shape_cross(cquery_pre, cross_lines_here, gains, width)
    cross_full, cross_low, total_lines = attend(
        cquery_low, text_pairs, ids_here, text_code, False
    )
    parts, placed_second = collect(
        cross_low, w_mid, 4 * columns, columns, (), (placed_second,)
    )
    w_down = gather_weight(jnp.concatenate((placed_first, placed_second), 2))
    state_two, ffn_share = vmem_call(
        share_last,
        [share_full, share_low],
        (*parts, state_one, ids_share, vectors),
        "share_last",
    )

    ffn_act = spread(ffn_share)
    hidden_pre = nn(ffn_act, w_up) + bias_ffn
    hidden_low = jax.nn.gelu(hidden_pre, approximate=True).astype(BF16)
    grad_branch_three = spread(after(top_share, cross_act))

    gelu_pull = jax.vjp(lambda h: jax.nn.gelu(h, approximate=True), hidden_pre)[1]
    grad_hidden = gelu_pull(nn(grad_branch_three, w_down))[0].astype(BF16)
    part_down = weight_grad(grad_branch_three, hidden_low)
    part_up = weight_grad(ffn_act, grad_hidden)
    half_down = scatter_weight(part_down)
    half_up = scatter_weight(part_up)
    parts, part_down, part_up = collect(
        grad_hidden, w_up, 0, hidden, (part_down,), (part_up,)
    )
    grad_two, gb2_share, sums_two = vmem_call(
        share_back_last,
        [share_full, share_low, sums_shape(2 * latents + 2)],
        (*parts, state_two, grad_top, top_share, ids_share, vectors),
        "share_back_last",
    )

    grad_branch_two = spread(gb2_share)
    out_parts, = collect(after(hidden_low, gb2_share), w_down, 0, hidden)
    out_share, sums_three = vmem_call(
        share_result,
        [share_low, sums_shape(latents)],
        (*out_parts, state_two, grad_top, ids_share, vectors),
        "share_result",
    )
    grad_cross = nn(grad_branch_two, w_mid[:, 4 * columns :]).astype(BF16)
    grad_cquery, text_near, text_far = attend_back(
        cquery_low,
        grad_cross,
        cross_full,
        total_lines,
        text_pairs,
        ids_here,
        text_code,
        False,
    )
    back_lines = lines_of(cross_lines(grad_cquery, cquery_pre, gains))
    text_far = hop(text_far, hop_c)
    back_lines, text_far = tie(back_lines, text_far)
    gcq_low, sums_cq = back_cross(
        grad_cquery, cquery_pre, inverse_cq, back_lines, gains, width
    )
    gpair = add_low(text_near, text_far)
    for mask in hop_rest[::-1]:
        rows_left = gpair.shape[0] // 2
        gpair = add_low(gpair[:rows_left], hop(gpair[rows_left:], mask))
    parts, gpair, out_share = collect(
        gcq_low, w_mid, 3 * columns, columns, (), (gpair, out_share)
    )
    grad_one, gb1_share, sums_one = vmem_call(
        share_back_middle,
        [share_full, share_low, sums_shape(latents + 3)],
        (*parts, state_one, grad_two, branch_one, ids_share, vectors),
        "share_back_middle",
    )

    gckey = gpair[:, :columns].astype(F32)
    sums_ck = text_sum(jnp.sum(gains[3] * gckey * ckey_pre, -1)[None])[0]
    out_both = give_far(out_share)
    grad_branch_one, sums_ck, out_both = spread(gb1_share, (sums_ck,), (out_both,))
    out_both, out_across = give_across(out_both)
    gck_low = rms_pull(ckey_pre, inverse_ck, gains[3], gckey, sums_ck[:, None], width)
    gtext = jnp.concatenate((gck_low, gpair[:, columns:]), 1)
    text_part = nt(gtext, w_mid[:, : 2 * columns]).astype(BF16)
    text_back = hop(text_part[2 * half :], hop_w)

    grad_attn = nn(grad_branch_one, w_mid[:, 2 * columns : 3 * columns]).astype(BF16)
    part_mid = jnp.concatenate(
        (
            weight_grad(text_here, gtext),
            weight_grad(grad_branch_one, attn_low),
            weight_grad(cross_act, gcq_low),
            weight_grad(grad_branch_two, cross_low),
        ),
        1,
    )
    half_mid = scatter_weight(part_mid)
    grad_attn, text_back, out_across = tie(grad_attn, text_back, out_across)
    block_out = give_back(out_both, out_across, lambda place_here: place_here)
    grad_query, near, far = attend_back(
        query_low, grad_attn, attn_full, attn_lines, pairs, ids_here, key_code, True
    )
    text_sub = half // 2
    text_part = text_part[: 2 * half].astype(F32) + text_back.astype(F32)
    text_part = text_part.reshape(2, 2, text_sub, width)
    text_share = lax.dynamic_index_in_dim(text_part, x, 1, keepdims=False)
    text_given = lax.dynamic_index_in_dim(text_part, 1 - x, 1, keepdims=False)
    text_got = hop(text_given.astype(BF16), hop_x)
    far = hop(far, hop_c)
    far, text_got = tie(far, text_got)
    kv_back = add_low(near, far)
    text_share = (text_share + text_got.astype(F32)).astype(BF16)
    text_both = give_far(text_share.reshape(2 * text_sub, width))
    home_down = [home_parts(half_down[:, :, :hidden_half])]
    for mask in hop_rest[::-1]:
        rows_left = kv_back.shape[0] // 2
        given = hop(kv_back[rows_left:], mask)
        if mask == hop_rest[0]:
            given, text_both, home_down[0] = tie(given, text_both, home_down[0])
        kv_back = add_low(kv_back[:rows_left], given)
    text_both, text_across = give_across(text_both)
    gquery, gkey, head_lines = turn_back(
        grad_query, kv_back, projected, gains, cosine, signed
    )
    head_lines = lines_of(head_lines)
    head_lines, text_across, block_out = tie(head_lines, text_across, block_out)
    grad_proj, sums_heads = back_heads(
        gquery, gkey, projected, inverse, kv_back, head_lines, gains, width
    )
    grad_text = give_back(
        text_both,
        text_across,
        lambda place_here: ((place_here & 1) << 1) | (place_here >> 1),
    ).astype(F32)
    part_attn = weight_grad(act_low, grad_proj)
    part_attn = part_attn.reshape((2,) * (bits - 1) + (2, slice_rows, 3 * columns))
    steps = [(0, hop_c, c)] + [
        (1 + i, tensor_size << b, seq_bit(b)) for i, b in enumerate(rest[::-1])
    ]
    for axis, mask, mine in steps:
        kept = lax.dynamic_index_in_dim(part_attn, mine, axis, keepdims=True)
        given = lax.dynamic_index_in_dim(part_attn, 1 - mine, axis, keepdims=True)
        part_attn = add_low(kept, hop(given, mask))
    part_attn = part_attn.reshape(2, slice_rows, 3 * columns)
    home_down.append(home_parts(after(half_down[:, :, hidden_half:], home_down[0])))
    home_up = [home_parts(half_up[:, :, :hidden_half])]
    parts, home_down[1], home_up[0] = collect(
        grad_proj, w_attn, 0, 3 * columns, (home_down[1],), (home_up[0],)
    )
    grad_share, sums_zero = vmem_call(
        share_back_first,
        [share_low, sums_shape(2 * latents)],
        (*parts, state_in, grad_one, ids_share, vectors),
        "share_back_first",
    )
    home_up.append(home_parts(after(half_up[:, :, hidden_half:], home_up[0])))
    in_both = give_far(grad_share)
    in_both, home_up[1] = tie(in_both, home_up[1])
    in_both, in_across = give_across(in_both)
    home_mid = home_parts(half_mid)
    in_across, home_mid = tie(in_across, home_mid)
    grad_inputs = give_back(in_both, in_across, lambda place_here: place_here).astype(F32)
    grad_attn_in = whole_of(home_parts(part_attn))
    grad_mid = whole_of(home_mid)
    grad_up = jnp.concatenate([whole_of(h) for h in home_up], 1)
    grad_down = jnp.concatenate([whole_of(h) for h in home_down], 1)

    rows_sum = lambda a: jnp.sum(a.astype(F32), 0)
    extra = -hidden % columns
    column_sums = jnp.concatenate(
        (
            sums_heads[0].reshape(3, columns),
            sums_cq[:1],
            rows_sum(gtext).reshape(2, columns),
            sums_heads[1, : 2 * columns].reshape(2, columns),
            sums_cq[1:2],
            rows_sum(gckey * ckey_pre * inverse_ck)[None],
            jnp.pad(rows_sum(grad_hidden), (0, extra)).reshape(-1, columns),
        ),
        0,
    )
    column_sums = all_sum(column_sums, [hop_c] + hop_rest + [hop_k])
    low_sums = column_sums.astype(BF16)
    column_sums = by_home(low_sums, hop(low_sums, hop_w)).astype(F32)
    grad_in_bias = column_sums[:6].reshape(2, 3, columns)
    grad_gains = column_sums[6:10]
    grad_ffn_bias = column_sums[10:].reshape(-1)[:hidden]

    count = latents
    feature_sums = jnp.concatenate(
        (
            sums_zero,
            sums_one[:count],
            sums_two[: 2 * count],
            sums_three,
            sums_one[count : count + 1],
            sums_two[2 * count :],
            sums_one[count + 1 :],
        ),
        0,
    )
    feature_sums = all_sum(feature_sums, [hop_c, hop_x, hop_w] + hop_rest)
    low_features = arrange(feature_sums.astype(BF16), order_back)
    far_features = hop(low_features, hop_k).astype(F32)
    near_features = low_features.astype(F32)
    both_sums = near_features + far_features
    count = 6 * latents
    near_temb = near_features[:count].reshape(6, latents, width).transpose(1, 0, 2)
    far_temb = far_features[:count].reshape(6, latents, width).transpose(1, 0, 2)
    grad_temb = jnp.where(
        k == 0, jnp.stack((near_temb, far_temb)), jnp.stack((far_temb, near_temb))
    )
    grad_mod = jnp.sum(grad_temb, (0, 1))

    unpack = lambda a: a.reshape(slice_rows, -1, columns).transpose(1, 0, 2)
    part = lambda i: grad_mid[:, i * columns : (i + 1) * columns]
    return (
        block_out,
        grad_inputs,
        grad_text,
        grad_temb,
        grad_mod,
        unpack(grad_attn_in),
        grad_in_bias,
        grad_gains,
        part(2).T,
        jnp.stack((part(3), part(0), part(1))),
        part(4).T,
        both_sums[count + 3],
        both_sums[count + 4],
        grad_up,
        grad_ffn_bias,
        grad_down.T,
        both_sums[count : count + 3],
    )


def solution(mesh):
    placed = (
        P(None, "seq", None),
        P(None, "seq", None),
        P(),
        P(),
        P(None, "seq", "tensor"),
        P(None, None, "tensor"),
        P(None, "tensor"),
        P("tensor", "seq"),
        P(None, "seq", "tensor"),
        P("tensor", "seq"),
        P(),
        P(),
        P("seq", "tensor"),
        P("tensor"),
        P("tensor", "seq"),
        P(),
        P(None, "seq"),
        P(None, "seq"),
        P(None, "seq"),
        P(None, "seq"),
        P(None, "seq"),
        P(None, "seq", None),
    )
    return jax.shard_map(
        shards,
        mesh=mesh,
        in_specs=placed,
        out_specs=(
            P(None, "seq", None),
            P(None, "seq", None),
            P(None, "seq", None),
            P(),
            P(),
            P(None, "seq", "tensor"),
            P(None, None, "tensor"),
            P(None, "tensor"),
            P("tensor", "seq"),
            P(None, "seq", "tensor"),
            P("tensor", "seq"),
            P(),
            P(),
            P("seq", "tensor"),
            P("tensor"),
            P("tensor", "seq"),
            P(),
        ),
        check_vma=False,
    )
```

time: 1120 us -> 873 us (0.78); the launches traced: 1090 us -> 862 us
  waiting for transfers between devices: 557 us -> 366 us
  matrix products: 96.6 us -> 61 us
  Pallas kernels: 50.2 us -> 79.2 us
  other arithmetic: 73.4 us -> 50.3 us
  local copies, waits for them, and re-layouts: 133 us -> 120 us
  between operations: 4.29 us -> 16.8 us
    ppermute x143 -> x109, waiting for transfers between devices: 557 us -> 297 us  [hop(): return lax.ppermute(value, AXES, [(d, d ^ mask) for d in range(places)])]
    ppermute x0 -> x10, waiting for transfers between devices: none -> 65.7 us  [swap_far(): return lax.ppermute(value, AXES, [(d, other(d)) for d in range(places)])]
    ppermute x143 -> x109, starting transfers between devices: 160 us -> 114 us  [hop(): return lax.ppermute(value, AXES, [(d, d ^ mask) for d in range(places)])]
    unnamed x359 -> x319, local copies, waits for them, and re-layouts: 18.6 us -> 56.1 us
    pallas_call x4 -> x37, Pallas kernels: 50.2 us -> 79.2 us  [vmem_call(): pl.pallas_call(kernel, out_shape=outs, in_specs=[whole] * len(args), out_...]
    convert_element_type x34 -> x14, other arithmetic: 37.8 us -> 12.6 us  [the longest x6 7.3 us: add_low(): return (a.astype(F32) + b.astype(F32)).astype(BF16)]
    ppermute x0 -> x10, starting transfers between devices: none -> 23.1 us  [swap_far(): return lax.ppermute(value, AXES, [(d, other(d)) for d in range(places)])]
    dot_general x7 -> x1, matrix products: 24.3 us -> 2.89 us  [nt(): lax.dot_general(a, b, (((1,), (1,)), ((), ())), preferred_element_type=F32)]
  transfers between devices with their start and end apart: 153 -> 137, of which waited for: 78 -> 60; matrix products, arithmetic and copies ran while one was open for 27% -> 20% of each run, Pallas kernels for 5% -> 9%
where the time goes in v2:
time: 873 us; the launch traced here: 862 us
  waiting for transfers between devices  366 us (42%)
  starting transfers between devices  169 us (19%)
  local copies, waits for them, and re-layouts  120 us (14%)
  Pallas kernels  79.2 us (9%)
  matrix products  61 us (7%)
  other arithmetic  50.3 us (6%)
  between operations  16.8 us (2%)
    ppermute x109, waiting for transfers between devices, hop(): return lax.ppermute(value, AXES, [(d, d ^ mask) for d in range(places)])  297 us
    ppermute x109, starting transfers between devices, hop(): return lax.ppermute(value, AXES, [(d, d ^ mask) for d in range(places)])  114 us
    pallas_call x37, Pallas kernels, vmem_call(): pl.pallas_call(kernel, out_shape=outs, in_specs=[whole] * len(args), out_...  79.2 us
    ppermute x10, waiting for transfers between devices, swap_far(): return lax.ppermute(value, AXES, [(d, other(d)) for d in range(places)])  65.7 us
    unnamed x319, local copies, waits for them, and re-layouts  56.1 us
    dot_general x7, matrix products, nn(): lax.dot_general(a, b, (((1,), (0,)), ((), ())), preferred_element_type=F32)  34.3 us
    ppermute x11, starting transfers between devices, swap(): return lax.ppermute(value, AXES, [(d, other(d)) for d in range(places)])  31.6 us
    dot_general x7, matrix products, tn(): lax.dot_general(a, b, (((0,), (0,)), ((), ())), preferred_element_type=F32)  23.8 us
  transfers between devices with their start and end apart: 137, of which 60 were waited for; matrix products, arithmetic and copies ran while one was open for 20% of the time, Pallas kernels for 9%

profile of v2, /device:TPU:0, one launch (start us, length us, event | category | flops | bytes accessed | tf_op | source)
XLA Modules:
  0.0 861.6 jit_solution(5860808026932043744)
XLA Ops:
  8.4 4.1 collective-permute-start.10
  19.8 30.4 %collective-permute-done.2 = s32[1,5,2,256]{3,2,1,0:T(2,128)S(1)} collective-permute-done((s32[1,5,2,256]{3,2,1,0:T(2,128)S(1)}, s32[1,5,2,256]{3,2,1,0:T(2,128)S(1)}, u32[]{:S(2)}, u32[]{:S(2)}) %collective-permute-start.2) | collective-permute-done | bytes 10272 | tf_op jit(solution)/shard_map/ppermute | solution.py:653
  63.0 7.2 collective-permute-done.6.refs_2_
  84.1 8.2 collective-permute-done.13
  100.8 9.2 %collective-permute-done.14 = bf16[192,1536]{1,0:T(8,128)(2,1)} collective-permute-done((bf16[192,1536]{1,0:T(8,128)(2,1)}, bf16[192,1536]{1,0:T(8,128)(2,1)}, u32[]{:S(2)}, u32[]{:S(2)}) %collective-permute-start.14) | collective-permute-done | bytes 589856 | tf_op jit(solution)/shard_map/ppermute | solution.py:653
  112.2 17.2 %collective-permute-done.12 = bf16[192,1920]{1,0:T(8,128)(2,1)} collective-permute-done((bf16[192,1920]{1,0:T(8,128)(2,1)S(1)}, bf16[192,1920]{1,0:T(8,128)(2,1)}, u32[]{:S(2)}, u32[]{:S(2)}) %collective-permute-start.12) | collective-permute-done | bytes 737312 | tf_op jit(solution)/shard_map/ppermute | solution.py:667
  132.7 4.7 convolution_add_fusion.1.value_ref
  154.7 30.7 %collective-permute-done.19.refs_1_ = bf16[512,768]{1,0:T(8,128)(2,1)} collective-permute-done((bf16[512,768]{1,0:T(8,128)(2,1)S(1)}, bf16[512,768]{1,0:T(8,128)(2,1)}, u32[]{:S(2)}, u32[]{:S(2)}) %collective-permute-start.19) | collective-permute-done | bytes 786464 | tf_op jit(solution)/shard_map/ppermute | solution.py:653
  194.4 5.3 collective-permute-start.27
  200.7 7.6 attend.1
  220.6 4.7 collective-permute-done.24.from_w
  234.9 7.0 collective-permute-done.25.p1
  241.9 5.1 collective-permute-done.26.p2
  253.6 4.2 collective-permute-done.29.refs_1_
  257.8 11.1 %collective-permute-done.30.refs_2_ = bf16[128,1536]{1,0:T(8,128)(2,1)S(1)} collective-permute-done((bf16[128,1536]{1,0:T(8,128)(2,1)S(1)}, bf16[128,1536]{1,0:T(8,128)(2,1)S(1)}, u32[]{:S(2)}, u32[]{:S(2)}) %collective-permute-start.30) | collective-permute-done | bytes 393248 | tf_op jit(solution)/shard_map/ppermute | solution.py:653
  274.9 4.2 collective-permute-done.39.refs_1_
  291.3 12.9 %collective-permute-done.38.l3 = f32[8,512]{1,0:T(8,128)S(1)} collective-permute-done((f32[8,512]{1,0:T(8,128)S(1)}, f32[8,512]{1,0:T(8,128)S(1)}, u32[]{:S(2)}, u32[]{:S(2)}) %collective-permute-start.38) | collective-permute-done | bytes 16416 | tf_op jit(solution)/shard_map/ppermute | solution.py:653
  307.4 6.3 attend_text.1
  320.4 3.9 collective-permute-done.46.from_x
  328.1 7.3 collective-permute-done.48.p1
  355.3 5.3 collective-permute-done.53.refs_2_
  368.9 10.4 %multiply_convert_fusion = (bf16[512,2240]{1,0:T(8,128)(2,1)S(1)}, f32[512,2240]{1,0:T(8,128)}) fusion(f32[2240]{0:T(1024)S(1)} %slice.794, bf16[512,1536]{1,0:T(8,128)(2,1)} %copy-done.46, bf16[1536,2240]{1,0:T(8,128)(2,1)} %all-gather.15.cloned.1.call-done.weight_ref), kind=kOutput, calls=%fused_computation.14 | convolution fusion | flops 3534684160 | bytes 15344384 | tf_op jit(solution)/shard_map/dot_general | solution.py:24
  379.2 5.9 convolution_convert_fusion.1
  388.9 9.9 %fusion.47 = (bf16[2240]{0:T(1024)(128)(2,1)S(1)}, bf16[512,2240]{1,0:T(8,128)(2,1)S(1)}) fusion(f32[512,2240]{1,0:T(8,128)} %get-tuple-element.557, bf16[512,1536]{1,0:T(8,128)(2,1)} %copy-done.44, bf16[1536,2240]{1,0:T(8,128)(2,1)} %bitcast.204), kind=kOutput, calls=%fused_computation.212 | convolution fusion | flops 3547297536 | bytes 15339904 | tf_op jit(solution)/shard_map/dot_general | solution.py:24
  398.8 5.9 convolution_convert_fusion
  410.9 3.8 project_out.8
  417.8 4.1 collective-permute-done.56.from_x
  425.3 8.2 collective-permute-done.58.p1
  440.2 6.3 collective-permute-done.61.refs_2_
  457.6 10.0 %attend_text_back.1 = (f32[512,384]{1,0:T(8,128)S(1)}, bf16[768,768]{1,0:T(8,128)(2,1)S(1)}, bf16[768,768]{1,0:T(8,128)(2,1)}) custom-call(bf16[512,384]{1,0:T(8,128)(2,1)S(1)} %copy-done.38, bf16[512,384]{1,0:T(8,128)(2,1)S(1)} %convolution_convert_fusion.9.grad_ref, f32[512,384]{1,0:T(8,128)S(1)} %copy-done.71, f32[8,512]{1,0:T(8,128)S(1)} %get-tuple-element.259.line_ref, ...), custom_call_target="tpu_custom_call" | custom-call | flops 1024 | bytes 1024 | tf_op jit(solution)/shard_map/attend_text_back/pallas_call | solution.py:48
  468.6 4.5 project_out.10
  514.8 7.4 collective-permute-done.72
  542.2 5.5 collective-permute-done.84
  576.4 12.0 %attend_back.1 = (f32[512,384]{1,0:T(8,128)S(1)}, bf16[1024,768]{1,0:T(8,128)(2,1)S(1)}, bf16[1024,768]{1,0:T(8,128)(2,1)}) custom-call(bf16[512,384]{1,0:T(8,128)(2,1)S(1)} %copy-done.55, bf16[512,384]{1,0:T(8,128)(2,1)S(1)} %copy-done.89, f32[512,384]{1,0:T(8,128)S(1)} %copy-done.69, f32[8,512]{1,0:T(8,128)S(1)} %get-tuple-element.301.line_ref, ...), custom_call_target="tpu_custom_call" | custom-call | flops 1024 | bytes 1024 | tf_op jit(solution)/shard_map/attend_back/pallas_call | solution.py:48
  600.2 5.4 collective-permute-start.91
  619.0 13.9 %collective-permute-done.90 = bf16[48,1536]{1,0:T(8,128)(2,1)S(1)} collective-permute-done((bf16[48,1536]{1,0:T(8,128)(2,1)S(1)}, bf16[48,1536]{1,0:T(8,128)(2,1)S(1)}, u32[]{:S(2)}, u32[]{:S(2)}) %collective-permute-start.90) | collective-permute-done | bytes 147488 | tf_op jit(solution)/shard_map/ppermute | solution.py:653
  633.0 9.0 %collective-permute-done.89 = bf16[512,768]{1,0:T(8,128)(2,1)} collective-permute-done((bf16[512,768]{1,0:T(8,128)(2,1)}, bf16[512,768]{1,0:T(8,128)(2,1)}, u32[]{:S(2)}, u32[]{:S(2)}) %collective-permute-start.89) | collective-permute-done | bytes 786464 | tf_op jit(solution)/shard_map/ppermute | solution.py:653
  643.4 5.6 turn_back.1
  657.4 5.0 collective-permute-start.101
  668.2 4.1 convolution_convert_fusion.2
  704.9 15.7 %collective-permute-done.123 = bf16[1,1,2,192,1152]{4,3,2,1,0:T(8,128)(2,1)S(1)} collective-permute-done((bf16[1,1,2,192,1152]{4,3,2,1,0:T(8,128)(2,1)S(1)}, bf16[1,1,2,192,1152]{4,3,2,1,0:T(8,128)(2,1)S(1)}, u32[]{:S(2)}, u32[]{:S(2)}) %collective-permute-start.123) | collective-permute-done | bytes 884768 | tf_op jit(solution)/shard_map/ppermute | solution.py:653
  730.3 5.2 collective-permute-start.105
  735.5 8.1 collective-permute-done.125
  749.3 13.4 %collective-permute-done.106 = bf16[192,1120]{1,0:T(8,128)(2,1)} collective-permute-done((bf16[192,1120]{1,0:T(8,128)(2,1)}, bf16[192,1120]{1,0:T(8,128)(2,1)}, u32[]{:S(2)}, u32[]{:S(2)}) %collective-permute-start.106) | collective-permute-done | bytes 430112 | tf_op jit(solution)/shard_map/ppermute | solution.py:667
  768.4 3.8 collective-permute-start.107
  785.6 21.7 %collective-permute-done.121 = bf16[23,1536]{1,0:T(8,128)(2,1)S(1)} collective-permute-done((bf16[23,1536]{1,0:T(8,128)(2,1)S(1)}, bf16[23,1536]{1,0:T(8,128)(2,1)S(1)}, u32[]{:S(2)}, u32[]{:S(2)}) %collective-permute-start.121) | collective-permute-done | bytes 70688 | tf_op jit(solution)/shard_map/ppermute | solution.py:653
  818.4 3.9 collective-permute-done.111
  822.2 26.9 %collective-permute-done.113 = bf16[192,1920]{1,0:T(8,128)(2,1)S(1)} collective-permute-done((bf16[192,1920]{1,0:T(8,128)(2,1)S(1)}, bf16[192,1920]{1,0:T(8,128)(2,1)S(1)}, u32[]{:S(2)}, u32[]{:S(2)}) %collective-permute-start.113) | collective-permute-done | bytes 737312 | tf_op jit(solution)/shard_map/ppermute | solution.py:667
  (830 shorter events, 412.7 us)
Async XLA Ops:
  7.2 125.5 %all-gather.9.cloned.1.call-start = ((), (), s32[]{:S(2)}) async-start(), calls=%async_computation.6 | async-start | bytes 4423680 | tf_op jit(solution)/shard_map/all_gather | solution.py:692
  8.4 66.0 %collective-permute-start.10 = (bf16[192,1152]{1,0:T(8,128)(2,1)S(1)}, bf16[192,1152]{1,0:T(8,128)(2,1)S(1)}, u32[]{:S(2)}, u32[]{:S(2)}) collective-permute-start(bf16[192,1152]{1,0:T(8,128)(2,1)S(1)} %bitcast.228), channel_id=1, source_target_pairs={{0,16},{1,24},{2,18},{3,26},{4,20},{5,28},{6,22},{7,30},{8,17},{9,... | collective-permute-start | bytes 1327112 | tf_op jit(solution)/shard_map/ppermute | solution.py:667
  12.5 61.9 %collective-permute-start.9 = (bf16[192,1152]{1,0:T(8,128)(2,1)S(1)}, bf16[192,1152]{1,0:T(8,128)(2,1)}, u32[]{:S(2)}, u32[]{:S(2)}) collective-permute-start(bf16[192,1152]{1,0:T(8,128)(2,1)S(1)} %bitcast.229), channel_id=1, source_target_pairs={{0,0},{1,8},{2,2},{3,10},{4,4},{5,12},{6,6},{7,14},{8,1},{9,9},{10... | collective-permute-start | bytes 1327112 | tf_op jit(solution)/shard_map/ppermute | solution.py:660
  15.5 43.1 %collective-permute-start = (bf16[64,1536]{1,0:T(8,128)(2,1)S(1)}, bf16[64,1536]{1,0:T(8,128)(2,1)S(1)}, u32[]{:S(2)}, u32[]{:S(2)}) collective-permute-start(bf16[64,1536]{1,0:T(8,128)(2,1)S(1)} %concatenate.108), channel_id=1, source_target_pairs={{0,16},{1,17},{2,18},{3,19},{4,20},{5,21},{6,22},{7,23},{8,24},{9,... | collective-permute-start | bytes 589832 | tf_op jit(solution)/shard_map/ppermute | solution.py:653
  15.9 42.8 %collective-permute-start.1 = (bf16[64,1536]{1,0:T(8,128)(2,1)S(1)}, bf16[64,1536]{1,0:T(8,128)(2,1)S(1)}, u32[]{:S(2)}, u32[]{:S(2)}) collective-permute-start(bf16[64,1536]{1,0:T(8,128)(2,1)S(1)} %concatenate.111), channel_id=1, source_target_pairs={{0,16},{1,17},{2,18},{3,19},{4,20},{5,21},{6,22},{7,23},{8,24},{9,... | collective-permute-start | bytes 589832 | tf_op jit(solution)/shard_map/ppermute | solution.py:653
  18.9 31.2 %collective-permute-start.2 = (s32[1,5,2,256]{3,2,1,0:T(2,128)S(1)}, s32[1,5,2,256]{3,2,1,0:T(2,128)S(1)}, u32[]{:S(2)}, u32[]{:S(2)}) collective-permute-start(s32[1,5,2,256]{3,2,1,0:T(2,128)S(1)} %bitcast.240), channel_id=1, source_target_pairs={{0,16},{1,17},{2,18},{3,19},{4,20},{5,21},{6,22},{7,23},{8,24},{9,... | collective-permute-start | bytes 30728 | tf_op jit(solution)/shard_map/ppermute | solution.py:653
  79.4 130.5 %all-gather.11.cloned.1.call-start = ((), (), s32[]{:S(2)}) async-start(), calls=%async_computation.7 | async-start | bytes 7372800 | tf_op jit(solution)/shard_map/all_gather | solution.py:692
  93.7 35.8 %collective-permute-start.12 = (bf16[192,1920]{1,0:T(8,128)(2,1)S(1)}, bf16[192,1920]{1,0:T(8,128)(2,1)}, u32[]{:S(2)}, u32[]{:S(2)}) collective-permute-start(bf16[192,1920]{1,0:T(8,128)(2,1)S(1)} %pad_maximum_fusion.5), channel_id=1, source_target_pairs={{0,16},{1,24},{2,18},{3,26},{4,20},{5,28},{6,22},{7,30},{8,17},{9,... | collective-permute-start | bytes 2211848 | tf_op jit(solution)/shard_map/ppermute | solution.py:667
  97.1 32.3 %collective-permute-start.11 = (bf16[192,1920]{1,0:T(8,128)(2,1)S(1)}, bf16[192,1920]{1,0:T(8,128)(2,1)}, u32[]{:S(2)}, u32[]{:S(2)}) collective-permute-start(bf16[192,1920]{1,0:T(8,128)(2,1)S(1)} %pad_maximum_fusion.5), channel_id=1, source_target_pairs={{0,0},{1,8},{2,2},{3,10},{4,4},{5,12},{6,6},{7,14},{8,1},{9,9},{10... | collective-permute-start | bytes 2211848 | tf_op jit(solution)/shard_map/ppermute | solution.py:660
  137.5 231.4 %all-gather.15.cloned.1.call-start = ((), (), s32[]{:S(2)}) async-start(), calls=%async_computation.9 | async-start | bytes 7962624 | tf_op jit(solution)/shard_map/all_gather | solution.py:698
  149.4 36.0 %collective-permute-start.19 = (bf16[512,768]{1,0:T(8,128)(2,1)S(1)}, bf16[512,768]{1,0:T(8,128)(2,1)}, u32[]{:S(2)}, u32[]{:S(2)}) collective-permute-start(bf16[512,768]{1,0:T(8,128)(2,1)S(1)} %get-tuple-element.193.refs_0_), channel_id=1, source_target_pairs={{0,4},{1,5},{2,6},{3,7},{4,0},{5,1},{6,2},{7,3},{8,12},{9,13},{10,... | collective-permute-start | bytes 2359304 | tf_op jit(solution)/shard_map/ppermute | solution.py:653
  151.0 35.4 %collective-permute-start.22 = (bf16[192,2240]{1,0:T(8,128)(2,1)S(1)}, bf16[192,2240]{1,0:T(8,128)(2,1)}, u32[]{:S(2)}, u32[]{:S(2)}) collective-permute-start(bf16[192,2240]{1,0:T(8,128)(2,1)S(1)} %copy-done.149), channel_id=1, source_target_pairs={{0,0},{1,8},{2,2},{3,10},{4,4},{5,12},{6,6},{7,14},{8,1},{9,9},{10... | collective-permute-start | bytes 2580488 | tf_op jit(solution)/shard_map/ppermute | solution.py:660
  152.6 32.8 %collective-permute-start.20 = (bf16[512,768]{1,0:T(8,128)(2,1)S(1)}, bf16[512,768]{1,0:T(8,128)(2,1)S(1)}, u32[]{:S(2)}, u32[]{:S(2)}) collective-permute-start(bf16[512,768]{1,0:T(8,128)(2,1)S(1)} %get-tuple-element.193.refs_0_), channel_id=1, source_target_pairs={{0,1},{1,0},{2,3},{3,2},{4,5},{5,4},{6,7},{7,6},{8,9},{9,8},{10,11... | collective-permute-start | bytes 2359304 | tf_op jit(solution)/shard_map/ppermute | solution.py:653
  188.1 200.9 %all-gather.13.cloned.1.call-start = ((), (), s32[]{:S(2)}) async-start(), calls=%async_computation.8 | async-start | bytes 8847360 | tf_op jit(solution)/shard_map/all_gather | solution.py:692
  190.8 37.0 %collective-permute-start.28 = (bf16[192,1120]{1,0:T(8,128)(2,1)}, bf16[192,1120]{1,0:T(8,128)(2,1)}, u32[]{:S(2)}, u32[]{:S(2)}) collective-permute-start(bf16[192,1120]{1,0:T(8,128)(2,1)} %get-tuple-element.442), channel_id=1, source_target_pairs={{0,16},{1,24},{2,18},{3,26},{4,20},{5,28},{6,22},{7,30},{8,17},{9,... | collective-permute-start | bytes 1290248 | tf_op jit(solution)/shard_map/ppermute | solution.py:667
  194.4 33.4 %collective-permute-start.27 = (bf16[192,1120]{1,0:T(8,128)(2,1)}, bf16[192,1120]{1,0:T(8,128)(2,1)}, u32[]{:S(2)}, u32[]{:S(2)}) collective-permute-start(bf16[192,1120]{1,0:T(8,128)(2,1)} %get-tuple-element.442), channel_id=1, source_target_pairs={{0,0},{1,8},{2,2},{3,10},{4,4},{5,12},{6,6},{7,14},{8,1},{9,9},{10... | collective-permute-start | bytes 1290248 | tf_op jit(solution)/shard_map/ppermute | solution.py:660
  230.5 22.0 %collective-permute-start.31 = (f32[1,384]{1,0:T(1,128)S(1)}, f32[1,384]{1,0:T(1,128)S(1)}, u32[]{:S(2)}, u32[]{:S(2)}) collective-permute-start(f32[1,384]{1,0:T(1,128)S(1)} %broadcast_in_dim.154), channel_id=1, source_target_pairs={{0,2},{1,3},{2,0},{3,1},{4,6},{5,7},{6,4},{7,5},{8,10},{9,11},{10,... | collective-permute-start | bytes 4616 | tf_op jit(solution)/shard_map/ppermute | solution.py:653
  250.0 18.8 %collective-permute-start.30 = (bf16[128,1536]{1,0:T(8,128)(2,1)S(1)}, bf16[128,1536]{1,0:T(8,128)(2,1)S(1)}, u32[]{:S(2)}, u32[]{:S(2)}) collective-permute-start(bf16[128,1536]{1,0:T(8,128)(2,1)S(1)} %get-tuple-element.213.refs_0_), channel_id=1, source_target_pairs={{0,8},{1,9},{2,10},{3,11},{4,12},{5,13},{6,14},{7,15},{8,0},{9,1},... | collective-permute-start | bytes 1179656 | tf_op jit(solution)/shard_map/ppermute | solution.py:653
  274.9 29.4 %collective-permute-start.40 = (bf16[384,768]{1,0:T(8,128)(2,1)}, bf16[384,768]{1,0:T(8,128)(2,1)}, u32[]{:S(2)}, u32[]{:S(2)}) collective-permute-start(bf16[384,768]{1,0:T(8,128)(2,1)} %pad_maximum_fusion.7.refs_0_), channel_id=1, source_target_pairs={{0,1},{1,0},{2,3},{3,2},{4,5},{5,4},{6,7},{7,6},{8,9},{9,8},{10,11... | collective-permute-start | bytes 1769480 | tf_op jit(solution)/shard_map/ppermute | solution.py:653
  279.0 25.2 %collective-permute-start.41 = (bf16[384,768]{1,0:T(8,128)(2,1)}, bf16[384,768]{1,0:T(8,128)(2,1)}, u32[]{:S(2)}, u32[]{:S(2)}) collective-permute-start(bf16[384,768]{1,0:T(8,128)(2,1)} %collective-permute-done.39.refs_1_), channel_id=1, source_target_pairs={{0,1},{1,0},{2,3},{3,2},{4,5},{5,4},{6,7},{7,6},{8,9},{9,8},{10,11... | collective-permute-start | bytes 1769480 | tf_op jit(solution)/shard_map/ppermute | solution.py:653
  285.7 42.2 %collective-permute-start.51 = (bf16[192,1120]{1,0:T(8,128)(2,1)}, bf16[192,1120]{1,0:T(8,128)(2,1)S(1)}, u32[]{:S(2)}, u32[]{:S(2)}) collective-permute-start(bf16[192,1120]{1,0:T(8,128)(2,1)} %get-tuple-element.237), channel_id=1, source_target_pairs={{0,16},{1,24},{2,18},{3,26},{4,20},{5,28},{6,22},{7,30},{8,17},{9,... | collective-permute-start | bytes 1290248 | tf_op jit(solution)/shard_map/ppermute | solution.py:667
  288.0 39.9 %collective-permute-start.50 = (bf16[192,1120]{1,0:T(8,128)(2,1)}, bf16[192,1120]{1,0:T(8,128)(2,1)S(1)}, u32[]{:S(2)}, u32[]{:S(2)}) collective-permute-start(bf16[192,1120]{1,0:T(8,128)(2,1)} %get-tuple-element.237), channel_id=1, source_target_pairs={{0,0},{1,8},{2,2},{3,10},{4,4},{5,12},{6,6},{7,14},{8,1},{9,9},{10... | collective-permute-start | bytes 1290248 | tf_op jit(solution)/shard_map/ppermute | solution.py:660
  338.8 257.6 %reduce-scatter.4.cloned.1.call-start = ((), (), s32[]{:S(2)}) async-start(), calls=%async_computation.3 | async-start | bytes 8847360 | tf_op jit(solution)/shard_map/reduce_scatter | solution.py:704
  386.6 339.9 %reduce-scatter.6.cloned.1.call-start = ((), (), s32[]{:S(2)}) async-start(), calls=%async_computation.4 | async-start | bytes 8847360 | tf_op jit(solution)/shard_map/reduce_scatter | solution.py:704
  406.1 407.3 %reduce-scatter.8.cloned.1.call-start = ((), (), s32[]{:S(2)}) async-start(), calls=%async_computation.5 | async-start | bytes 7372800 | tf_op jit(solution)/shard_map/reduce_scatter | solution.py:704
  468.6 23.5 %collective-permute-start.67 = (bf16[768,768]{1,0:T(8,128)(2,1)}, bf16[768,768]{1,0:T(8,128)(2,1)}, u32[]{:S(2)}, u32[]{:S(2)}) collective-permute-start(bf16[768,768]{1,0:T(8,128)(2,1)} %get-tuple-element.262), channel_id=1, source_target_pairs={{0,1},{1,0},{2,3},{3,2},{4,5},{5,4},{6,7},{7,6},{8,9},{9,8},{10,11... | collective-permute-start | bytes 3538952 | tf_op jit(solution)/shard_map/ppermute | solution.py:653
  494.1 28.1 %collective-permute-start.72 = (bf16[384,768]{1,0:T(8,128)(2,1)S(1)}, bf16[384,768]{1,0:T(8,128)(2,1)S(1)}, u32[]{:S(2)}, u32[]{:S(2)}) collective-permute-start(bf16[384,768]{1,0:T(8,128)(2,1)S(1)} %slice.799), channel_id=1, source_target_pairs={{0,4},{1,5},{2,6},{3,7},{4,0},{5,1},{6,2},{7,3},{8,12},{9,13},{10,... | collective-permute-start | bytes 1769480 | tf_op jit(solution)/shard_map/ppermute | solution.py:653
  525.9 22.5 %collective-permute-start.77 = (bf16[128,1536]{1,0:T(8,128)(2,1)}, bf16[128,1536]{1,0:T(8,128)(2,1)S(1)}, u32[]{:S(2)}, u32[]{:S(2)}) collective-permute-start(bf16[128,1536]{1,0:T(8,128)(2,1)} %get-tuple-element.290.refs_0_), channel_id=1, source_target_pairs={{0,2},{1,3},{2,0},{3,1},{4,6},{5,7},{6,4},{7,5},{8,10},{9,11},{10,... | collective-permute-start | bytes 1179656 | tf_op jit(solution)/shard_map/ppermute | solution.py:653
  527.4 21.0 %collective-permute-start.78 = (bf16[128,1536]{1,0:T(8,128)(2,1)}, bf16[128,1536]{1,0:T(8,128)(2,1)S(1)}, u32[]{:S(2)}, u32[]{:S(2)}) collective-permute-start(bf16[128,1536]{1,0:T(8,128)(2,1)} %get-tuple-element.290.refs_0_), channel_id=1, source_target_pairs={{0,8},{1,9},{2,10},{3,11},{4,12},{5,13},{6,14},{7,15},{8,0},{9,1},... | collective-permute-start | bytes 1179656 | tf_op jit(solution)/shard_map/ppermute | solution.py:653
  561.9 31.0 %collective-permute-start.97 = (bf16[2,64,1536]{2,1,0:T(8,128)(2,1)}, bf16[2,64,1536]{2,1,0:T(8,128)(2,1)}, u32[]{:S(2)}, u32[]{:S(2)}) collective-permute-start(bf16[2,64,1536]{2,1,0:T(8,128)(2,1)} %maximum_select_fusion.4), channel_id=1, source_target_pairs={{0,1},{1,0},{2,3},{3,2},{4,5},{5,4},{6,7},{7,6},{8,9},{9,8},{10,11... | collective-permute-start | bytes 1179656 | tf_op jit(solution)/shard_map/ppermute | solution.py:653
  588.4 19.0 %collective-permute-start.87 = (bf16[1024,768]{1,0:T(8,128)(2,1)}, bf16[1024,768]{1,0:T(8,128)(2,1)}, u32[]{:S(2)}, u32[]{:S(2)}) collective-permute-start(bf16[1024,768]{1,0:T(8,128)(2,1)} %get-tuple-element.304), channel_id=1, source_target_pairs={{0,1},{1,0},{2,3},{3,2},{4,5},{5,4},{6,7},{7,6},{8,9},{9,8},{10,11... | collective-permute-start | bytes 4718600 | tf_op jit(solution)/shard_map/ppermute | solution.py:653
  592.9 22.5 %collective-permute-start.98 = (bf16[2,64,1536]{2,1,0:T(8,128)(2,1)}, bf16[2,64,1536]{2,1,0:T(8,128)(2,1)S(1)}, u32[]{:S(2)}, u32[]{:S(2)}) collective-permute-start(bf16[2,64,1536]{2,1,0:T(8,128)(2,1)} %collective-permute-done.86), channel_id=1, source_target_pairs={{0,1},{1,0},{2,3},{3,2},{4,5},{5,4},{6,7},{7,6},{8,9},{9,8},{10,11... | collective-permute-start | bytes 1179656 | tf_op jit(solution)/shard_map/ppermute | solution.py:653
  600.2 32.7 %collective-permute-start.91 = (bf16[192,1120]{1,0:T(8,128)(2,1)}, bf16[192,1120]{1,0:T(8,128)(2,1)}, u32[]{:S(2)}, u32[]{:S(2)}) collective-permute-start(bf16[192,1120]{1,0:T(8,128)(2,1)} %get-tuple-element.440), channel_id=1, source_target_pairs={{0,0},{1,8},{2,2},{3,10},{4,4},{5,12},{6,6},{7,14},{8,1},{9,9},{10... | collective-permute-start | bytes 1290248 | tf_op jit(solution)/shard_map/ppermute | solution.py:660
  605.6 27.3 %collective-permute-start.92 = (bf16[192,1120]{1,0:T(8,128)(2,1)}, bf16[192,1120]{1,0:T(8,128)(2,1)}, u32[]{:S(2)}, u32[]{:S(2)}) collective-permute-start(bf16[192,1120]{1,0:T(8,128)(2,1)} %get-tuple-element.439), channel_id=1, source_target_pairs={{0,16},{1,24},{2,18},{3,26},{4,20},{5,28},{6,22},{7,30},{8,17},{9,... | collective-permute-start | bytes 1290248 | tf_op jit(solution)/shard_map/ppermute | solution.py:667
  610.3 31.7 %collective-permute-start.89 = (bf16[512,768]{1,0:T(8,128)(2,1)}, bf16[512,768]{1,0:T(8,128)(2,1)}, u32[]{:S(2)}, u32[]{:S(2)}) collective-permute-start(bf16[512,768]{1,0:T(8,128)(2,1)} %slice.810), channel_id=1, source_target_pairs={{0,4},{1,5},{2,6},{3,7},{4,0},{5,1},{6,2},{7,3},{8,12},{9,13},{10,... | collective-permute-start | bytes 2359304 | tf_op jit(solution)/shard_map/ppermute | solution.py:653
  654.0 25.0 %collective-permute-start.115 = (bf16[2,48,1536]{2,1,0:T(8,128)(2,1)S(1)}, bf16[2,48,1536]{2,1,0:T(8,128)(2,1)}, u32[]{:S(2)}, u32[]{:S(2)}) collective-permute-start(bf16[2,48,1536]{2,1,0:T(8,128)(2,1)S(1)} %maximum_select_fusion.6), channel_id=1, source_target_pairs={{0,1},{1,0},{2,3},{3,2},{4,5},{5,4},{6,7},{7,6},{8,9},{9,8},{10,11... | collective-permute-start | bytes 884744 | tf_op jit(solution)/shard_map/ppermute | solution.py:653
  657.4 32.8 %collective-permute-start.101 = (bf16[192,1120]{1,0:T(8,128)(2,1)}, bf16[192,1120]{1,0:T(8,128)(2,1)}, u32[]{:S(2)}, u32[]{:S(2)}) collective-permute-start(bf16[192,1120]{1,0:T(8,128)(2,1)} %get-tuple-element.438), channel_id=1, source_target_pairs={{0,0},{1,8},{2,2},{3,10},{4,4},{5,12},{6,6},{7,14},{8,1},{9,9},{10... | collective-permute-start | bytes 1290248 | tf_op jit(solution)/shard_map/ppermute | solution.py:660
  662.4 27.8 %collective-permute-start.102 = (bf16[192,1120]{1,0:T(8,128)(2,1)}, bf16[192,1120]{1,0:T(8,128)(2,1)}, u32[]{:S(2)}, u32[]{:S(2)}) collective-permute-start(bf16[192,1120]{1,0:T(8,128)(2,1)} %get-tuple-element.437), channel_id=1, source_target_pairs={{0,16},{1,24},{2,18},{3,26},{4,20},{5,28},{6,22},{7,30},{8,17},{9,... | collective-permute-start | bytes 1290248 | tf_op jit(solution)/shard_map/ppermute | solution.py:667
  679.0 20.9 %collective-permute-start.122 = (bf16[1,2,2,192,1152]{4,3,2,1,0:T(8,128)(2,1)}, bf16[1,2,2,192,1152]{4,3,2,1,0:T(8,128)(2,1)}, u32[]{:S(2)}, u32[]{:S(2)}) collective-permute-start(bf16[1,2,2,192,1152]{4,3,2,1,0:T(8,128)(2,1)} %constant_dynamic-slice_fusion.1), channel_id=1, source_target_pairs={{0,1},{1,0},{2,3},{3,2},{4,5},{5,4},{6,7},{7,6},{8,9},{9,8},{10,11... | collective-permute-start | bytes 5308424 | tf_op jit(solution)/shard_map/ppermute | solution.py:653
  693.3 56.0 %collective-permute-start.103 = (bf16[128,1536]{1,0:T(8,128)(2,1)S(1)}, bf16[128,1536]{1,0:T(8,128)(2,1)S(1)}, u32[]{:S(2)}, u32[]{:S(2)}) collective-permute-start(bf16[128,1536]{1,0:T(8,128)(2,1)S(1)} %get-tuple-element.331), channel_id=1, source_target_pairs={{0,2},{1,3},{2,0},{3,1},{4,6},{5,7},{6,4},{7,5},{8,10},{9,11},{10,... | collective-permute-start | bytes 1179656 | tf_op jit(solution)/shard_map/ppermute | solution.py:653
  694.7 54.6 %collective-permute-start.104 = (bf16[128,1536]{1,0:T(8,128)(2,1)S(1)}, bf16[128,1536]{1,0:T(8,128)(2,1)S(1)}, u32[]{:S(2)}, u32[]{:S(2)}) collective-permute-start(bf16[128,1536]{1,0:T(8,128)(2,1)S(1)} %get-tuple-element.332), channel_id=1, source_target_pairs={{0,8},{1,9},{2,10},{3,11},{4,12},{5,13},{6,14},{7,15},{8,0},{9,1},... | collective-permute-start | bytes 1179656 | tf_op jit(solution)/shard_map/ppermute | solution.py:653
  721.8 21.8 %collective-permute-start.125 = (bf16[192,1152]{1,0:T(8,128)(2,1)}, bf16[192,1152]{1,0:T(8,128)(2,1)S(1)}, u32[]{:S(2)}, u32[]{:S(2)}) collective-permute-start(bf16[192,1152]{1,0:T(8,128)(2,1)} %get-tuple-element.432), channel_id=1, source_target_pairs={{0,16},{1,24},{2,18},{3,26},{4,20},{5,28},{6,22},{7,30},{8,17},{9,... | collective-permute-start | bytes 1327112 | tf_op jit(solution)/shard_map/ppermute | solution.py:667
  730.3 19.0 %collective-permute-start.105 = (bf16[192,1120]{1,0:T(8,128)(2,1)}, bf16[192,1120]{1,0:T(8,128)(2,1)}, u32[]{:S(2)}, u32[]{:S(2)}) collective-permute-start(bf16[192,1120]{1,0:T(8,128)(2,1)} %get-tuple-element.436), channel_id=1, source_target_pairs={{0,0},{1,8},{2,2},{3,10},{4,4},{5,12},{6,6},{7,14},{8,1},{9,9},{10... | collective-permute-start | bytes 1290248 | tf_op jit(solution)/shard_map/ppermute | solution.py:660
  743.6 19.1 %collective-permute-start.106 = (bf16[192,1120]{1,0:T(8,128)(2,1)}, bf16[192,1120]{1,0:T(8,128)(2,1)}, u32[]{:S(2)}, u32[]{:S(2)}) collective-permute-start(bf16[192,1120]{1,0:T(8,128)(2,1)} %get-tuple-element.435), channel_id=1, source_target_pairs={{0,16},{1,24},{2,18},{3,26},{4,20},{5,28},{6,22},{7,30},{8,17},{9,... | collective-permute-start | bytes 1290248 | tf_op jit(solution)/shard_map/ppermute | solution.py:667
  779.2 31.1 %collective-permute-start.108 = (bf16[192,1120]{1,0:T(8,128)(2,1)}, bf16[192,1120]{1,0:T(8,128)(2,1)S(1)}, u32[]{:S(2)}, u32[]{:S(2)}) collective-permute-start(bf16[192,1120]{1,0:T(8,128)(2,1)} %get-tuple-element.434), channel_id=1, source_target_pairs={{0,0},{1,8},{2,2},{3,10},{4,4},{5,12},{6,6},{7,14},{8,1},{9,9},{10... | collective-permute-start | bytes 1290248 | tf_op jit(solution)/shard_map/ppermute | solution.py:660
  780.8 29.4 %collective-permute-start.109 = (bf16[192,1120]{1,0:T(8,128)(2,1)S(1)}, bf16[192,1120]{1,0:T(8,128)(2,1)S(1)}, u32[]{:S(2)}, u32[]{:S(2)}) collective-permute-start(bf16[192,1120]{1,0:T(8,128)(2,1)S(1)} %get-tuple-element.433), channel_id=1, source_target_pairs={{0,16},{1,24},{2,18},{3,26},{4,20},{5,28},{6,22},{7,30},{8,17},{9,... | collective-permute-start | bytes 1290248 | tf_op jit(solution)/shard_map/ppermute | solution.py:667
  783.5 23.8 %collective-permute-start.121 = (bf16[23,1536]{1,0:T(8,128)(2,1)S(1)}, bf16[23,1536]{1,0:T(8,128)(2,1)S(1)}, u32[]{:S(2)}, u32[]{:S(2)}) collective-permute-start(bf16[23,1536]{1,0:T(8,128)(2,1)S(1)} %concatenate.137), channel_id=1, source_target_pairs={{0,16},{1,17},{2,18},{3,19},{4,20},{5,21},{6,22},{7,23},{8,24},{9,... | collective-permute-start | bytes 211976 | tf_op jit(solution)/shard_map/ppermute | solution.py:653
  815.7 33.4 %collective-permute-start.113 = (bf16[192,1920]{1,0:T(8,128)(2,1)S(1)}, bf16[192,1920]{1,0:T(8,128)(2,1)S(1)}, u32[]{:S(2)}, u32[]{:S(2)}) collective-permute-start(bf16[192,1920]{1,0:T(8,128)(2,1)S(1)} %get-tuple-element.427), channel_id=1, source_target_pairs={{0,16},{1,24},{2,18},{3,26},{4,20},{5,28},{6,22},{7,30},{8,17},{9,... | collective-permute-start | bytes 2211848 | tf_op jit(solution)/shard_map/ppermute | solution.py:667
  (243 other events, 2168.5 us)
Sparse Core Ops, SparseCore 0:
  79.6 31.7 all-gather.8
  137.6 61.8 all-gather.10
  201.3 81.2 all-gather.14
  339.0 49.9 all-gather.12
  391.3 63.7 reduce-scatter.3
  457.6 76.2 reduce-scatter.5
  571.1 68.3 reduce-scatter.7

commit v3 on v2

--- a/solution.py
+++ b/solution.py
@@ -18,6 +18,7 @@
 SCALE = 1.0 / math.sqrt(HD)
 SCALE_TWO = SCALE * math.log2(math.e)
 STEP = 32
+HEAD_STEP = 128
 
 
 def nn(a, b):
@@ -109,16 +110,22 @@
     def three(refs, rows):
         return sum(ref[rows, :].astype(F32) for ref in refs)
 
-    def first(state_ref, grad_ref, ids_ref, vec_ref, act_ref, top_ref):
+    def first(state_ref, ids_ref, vec_ref, act_ref):
         def body(rows):
             choose = chooser(vec_ref, ids_ref[rows, :], latents)
             center, inverse = center_of(state_ref[rows, :].astype(F32))
             act_ref[rows, :] = (
                 center * inverse * (1.0 + choose(1)) + choose(0)
             ).astype(BF16)
+
+        by_rows(state_ref.shape[0], STEP, body)
+
+    def top(grad_ref, ids_ref, vec_ref, top_ref):
+        def body(rows):
+            choose = chooser(vec_ref, ids_ref[rows, :], latents)
             top_ref[rows, :] = (grad_ref[rows, :].astype(F32) * choose(5)).astype(BF16)
 
-        by_rows(state_ref.shape[0], STEP, body)
+        by_rows(grad_ref.shape[0], STEP, body)
 
     def middle(p0, p1, p2, state_ref, ids_ref, vec_ref, next_ref, branch_ref, act_ref):
         def body(rows):
@@ -233,7 +240,7 @@
 
         by_rows(state_ref.shape[0], STEP, body)
 
-    return first, middle, last, result, back_last, back_middle, back_first
+    return first, top, middle, last, result, back_last, back_middle, back_first
 
 
 def join_kernel(*refs):
@@ -298,17 +305,24 @@
     return jnp.concatenate([total] * (HD // 8), 0).T
 
 
-def squares(values, columns, count):
+def squares(values, columns, count, text=None):
     rows = values.shape[0]
-
-    def kernel(value_ref, out_ref):
+    args = (values,) if text is None else (values, text)
+
+    def kernel(*refs):
+        out_ref = refs[-1]
         parts = []
         for i in range(count):
-            part = value_ref[:, i * columns : (i + 1) * columns]
+            part = refs[0][:, i * columns : (i + 1) * columns]
             parts.append(jnp.sum(part * part, -1, keepdims=True))
+        if text is not None:
+            part = refs[1][:, :columns]
+            total = jnp.sum(part * part, -1, keepdims=True)
+            rest = jnp.zeros((rows - part.shape[0], 1), F32)
+            parts.append(jnp.concatenate((total, rest), 0))
         put_lines(out_ref, parts)
 
-    return vmem_call(kernel, [shape_of(8, rows)], (values,), "squares")[0]
+    return vmem_call(kernel, [shape_of(8, rows)], args, "squares")[0]
 
 
 def turn(values, cosine, signed):
@@ -338,7 +352,7 @@
                     ref[here, cols] = turn(value, cos, sin).astype(BF16)
             pair_ref[here, columns:] = value_ref[here, 2 * columns :].astype(BF16)
 
-        by_rows(rows, STEP, body)
+        by_rows(rows, HEAD_STEP, body)
 
     return vmem_call(
         kernel,
@@ -359,7 +373,7 @@
                 value_ref[here, :] * inv_ref[here, 0:1] * gain_ref[2:3, :]
             ).astype(BF16)
 
-        by_rows(rows, STEP, body)
+        by_rows(rows, HEAD_STEP, body)
 
     return vmem_call(
         kernel,
@@ -373,13 +387,13 @@
     rows, columns = dquery.shape
 
     def kernel(dq_ref, pair_ref, value_ref, gain_ref, cos_ref, sin_ref, gq_ref, gk_ref, line_ref, sum_ref):
-        lane = lax.broadcasted_iota(jnp.int32, (STEP, HD), 1)
+        lane = lax.broadcasted_iota(jnp.int32, (HEAD_STEP, HD), 1)
 
         def body(here):
             cos, sin = cos_ref[here, :], -sin_ref[here, :]
             totals = []
             for i, ref, out in ((0, dq_ref, gq_ref), (1, pair_ref, gk_ref)):
-                total = jnp.zeros((STEP, 1), F32)
+                total = jnp.zeros((HEAD_STEP, 1), F32)
                 for head in range(columns // HD):
                     cols = slice(head * HD, (head + 1) * HD)
                     at = i * columns + head * HD
@@ -395,7 +409,7 @@
                 lane == 0, totals[0], jnp.where(lane == 1, totals[1], 0.0)
             )
 
-        by_rows(rows, STEP, body)
+        by_rows(rows, HEAD_STEP, body)
         line_ref[...] = sum_ref[...].T[:8, :]
 
     return vmem_call(
@@ -432,7 +446,7 @@
             out_ref[here, cols] = value
             sums_ref[0:1, cols] += jnp.sum(value.astype(F32), 0, keepdims=True)
 
-        by_rows(rows, STEP, body)
+        by_rows(rows, HEAD_STEP, body)
 
     return vmem_call(
         kernel,
@@ -469,7 +483,7 @@
             sums_ref[0:1, :] += jnp.sum(low.astype(F32), 0, keepdims=True)
             sums_ref[1:2, :] += jnp.sum(grad * before * inv, 0, keepdims=True)
 
-        by_rows(rows, STEP, body)
+        by_rows(rows, HEAD_STEP, body)
 
     return vmem_call(
         kernel,
@@ -653,11 +667,10 @@
         return lax.ppermute(value, AXES, [(d, d ^ mask) for d in range(places)])
 
     def swap(value):
-        def other(d):
-            low, high = d & 1, (d // hop_w) & 1
-            return d if low == high else d ^ 1 ^ hop_w
-
-        return lax.ppermute(value, AXES, [(d, other(d)) for d in range(places)])
+        pairs_here = [
+            (d, d ^ 1 ^ hop_w) for d in range(places) if (d & 1) != (d // hop_w) & 1
+        ]
+        return jnp.where(c == w, value, lax.ppermute(value, AXES, pairs_here))
 
     def swap_far(value):
         def other(d):
@@ -708,6 +721,11 @@
             tiled=True,
             axis_index_groups=near_groups,
         ).reshape(2, slice_rows, grad.shape[1])
+
+    def scatter_far(grad):
+        return lax.psum_scatter(
+            grad, AXES, scatter_dimension=0, tiled=True, axis_index_groups=far_groups
+        )
 
     def home_parts(parts):
         own = lax.dynamic_index_in_dim(parts, k, 0, keepdims=False)
@@ -816,6 +834,13 @@
         own, far = share[:rows_each], hop(share[rows_each:], hop_k)
         return jnp.where(k == 0, jnp.stack((own, far)), jnp.stack((far, own)))
 
+    def give_far_two(one, two):
+        one, two = arrange(one, order_back), arrange(two, order_back)
+        size, size_two = one.shape[0] // 2, two.shape[0] // 2
+        far = hop(jnp.concatenate((one[size:], two[size_two:]), 0), hop_k)
+        own = jnp.concatenate((one[:size], two[:size_two]), 0)
+        return jnp.where(k == 0, jnp.stack((own, far)), jnp.stack((far, own)))
+
     def give_across(both):
         return both, hop(both, hop_x)
 
@@ -827,23 +852,16 @@
             out = lax.dynamic_update_index_in_dim(out, value, position(t ^ offset), 1)
         return out.reshape(micros, 4 * rows_each, width)
 
+    state_in = take_share(inputs)
     meta = jnp.stack((latent_ids, pad_mask, frame_pos, row_pos, col_pos))[None]
-    for mask in [hop_k, hop_w] + hop_rest:
-        meta = jnp.concatenate((meta, hop(meta, mask)), 0)
-    meta = lax.dynamic_index_in_dim(meta, k, 2, keepdims=False)
-    meta = meta.reshape((2,) * bits + (5, 2, 2, piece))
-    meta = jnp.where(x == 1, jnp.flip(meta, bits + 1), meta)
-    meta = jnp.where(c == 1, jnp.flip(meta, bits + 2), meta)
-    others = list(range(bits - 2))
-    meta = meta.transpose([bits, bits + 2] + others + [bits - 2, bits + 1, bits - 1, bits + 3])
-    meta = meta.reshape(5, -1)
-    ids_all = meta[0]
-    key_code = jnp.where(meta[1] == 1, ids_all, -1)
-    ids_here = ids_all[:group_rows]
-    ids_share = ids_here[:share_rows, None]
-    cosine, signed = rope_tables(*(meta[i, :group_rows] for i in (2, 3, 4)))
-
-    state_in = take_share(inputs)
+    meta = jnp.concatenate((meta, hop(meta, hop_k)), 0)
+
+    def by_own(value, axis):
+        value = jnp.where(x == 1, jnp.flip(value, axis), value)
+        return jnp.where(c == 1, jnp.flip(value, axis + 1), value)
+
+    ids_share = lax.dynamic_index_in_dim(meta[:, 0], k, 1, keepdims=False)
+    ids_share = by_own(ids_share.reshape(2, 2, 2, piece), 1)[:, 0, 0].reshape(-1)[:, None]
     table = modulation + lax.dynamic_index_in_dim(timestep_emb, k, 0, keepdims=False)
     vectors = arrange(
         jnp.concatenate(
@@ -857,12 +875,9 @@
         ),
         order,
     )
-
-    pack = lambda a: a.transpose(1, 0, 2).reshape(slice_rows, -1)
-    placed_attn = place_weight(pack(attn_in))
-    grad_top = take_share(cotangent)
     (
         share_first,
+        share_top,
         share_middle,
         share_last,
         share_result,
@@ -873,16 +888,31 @@
     share_low = shape_of(share_rows, width, BF16)
     share_full = shape_of(share_rows, width)
     sums_shape = lambda count: shape_of(count, width)
-    act_share, top_share = vmem_call(
-        share_first,
-        [share_low, share_low],
-        (state_in, grad_top, ids_share, vectors),
-        "share_first",
-    )
+    (act_share,) = vmem_call(
+        share_first, [share_low], (state_in, ids_share, vectors), "share_first"
+    )
+
+    pack = lambda a: a.transpose(1, 0, 2).reshape(slice_rows, -1)
+    placed_first = place_weight(pack(attn_in))
     act_low = spread(act_share)
-    w_attn = gather_weight(after(placed_attn, act_low))
-    mid_block = jnp.concatenate((pack(cross_in[1:]), attn_out.T, cross_in[0], cross_out.T), 1)
-    placed_mid = place_weight(after(mid_block, placed_attn))
+    w_first = gather_weight(placed_first)
+    grad_top = take_share(after(cotangent, act_low))
+    (top_share,) = vmem_call(share_top, [share_low], (grad_top, ids_share, vectors), "share_top")
+    second_block = jnp.concatenate((attn_out.T, pack(cross_in[1:])), 1)
+    placed_second = place_weight(after(second_block, act_low))
+    mid_block = jnp.concatenate((cross_in[0], cross_out.T), 1)
+    meta = after(meta, act_low)
+    for mask in [hop_w] + hop_rest:
+        meta = jnp.concatenate((meta, hop(meta, mask)), 0)
+    meta = lax.dynamic_index_in_dim(meta, k, 2, keepdims=False)
+    meta = by_own(meta.reshape((2,) * bits + (5, 2, 2, piece)), bits + 1)
+    others = list(range(bits - 2))
+    meta = meta.transpose([bits, bits + 2] + others + [bits - 2, bits + 1, bits - 1, bits + 3])
+    meta = meta.reshape(5, -1)
+    ids_all = meta[0]
+    key_code = jnp.where(meta[1] == 1, ids_all, -1)
+    ids_here = ids_all[:group_rows]
+    cosine, signed = rope_tables(*(meta[i, :group_rows] for i in (2, 3, 4)))
 
     flat = jnp.concatenate((in_bias.reshape(-1), norm_gains.reshape(-1), ffn_bias))
     flat = by_home(flat, hop(flat, hop_c)).astype(F32)
@@ -899,8 +929,9 @@
         )
         return arrange(own, order)
 
-    text_here = jnp.concatenate((text_of(k), hop(text_of(1 - k), hop_k)), 0)
-    text_here = jnp.concatenate((text_here, hop(text_here, hop_w)), 0)
+    text_here = jnp.concatenate(
+        (text_of(k), hop(after(text_of(1 - k), act_low), hop_k)), 0
+    )
     number = jnp.arange(4 * half * seq_size // 2, dtype=jnp.int32)
     row, chunk = number % half, number // half
     row_k, row_w, row_rest = chunk & 1, (chunk >> 1) & 1, chunk >> 2
@@ -910,35 +941,24 @@
     row_c = (row_rest >> len(rest)) ^ c
     text_code = (place * text_rows + row_c * half + row) // TXT
 
-    act_low, placed_mid, text_here = tie(act_low, placed_mid, text_here)
-    projected = nn(act_low, w_attn) + bias_in[0].reshape(1, -1)
-    w_mid = gather_weight(after(placed_mid, projected))
+    projected = nn(act_low, w_first) + bias_in[0].reshape(1, -1)
+    w_second = gather_weight(after(placed_second, projected))
+    w_attn_out, w_text = w_second[:, :columns], w_second[:, columns:]
+    placed_mid = place_weight(after(mid_block, projected))
     lines = lines_of(squares(projected, columns, 2))
-    swapped_up = swap(after(ffn_in, projected))
     query_low, pair, inverse = shape_heads(projected, lines, gains, cosine, signed, width)
+    grad_branch_three = spread(after(top_share, pair))
+    swapped_up = swap(after(ffn_in, pair))
+    text_near = after(text_here, pair)
+    text_here = jnp.concatenate((text_near, hop(text_near, hop_w)), 0)
     pairs = gather_pieces(pair)
-    pairs, swapped_up = tie(pairs, swapped_up)
-    w_up = gather_far(swapped_up)
-    attn_full, attn_low, attn_lines = attend(query_low, pairs, ids_here, key_code, True)
-    down_block = after(ffn_out.T, query_low)
-    hidden_half = hidden // 2
-    down_parts = [down_block[:, :hidden_half], down_block[:, hidden_half:]]
-    placed_down = [place_weight(down_parts[0])]
-    text_pre = nn(text_here, w_mid[:, : 2 * columns]) + bias_in[1, 1:].reshape(1, -1)
-    parts, text_pre, placed_first = collect(
-        attn_low, w_mid, 2 * columns, columns, (text_pre,), (placed_down[0],)
-    )
-    state_one, branch_one, cross_share = vmem_call(
-        share_middle,
-        [share_full, share_full, share_low],
-        (*parts, state_in, ids_share, vectors),
-        "share_middle",
-    )
-
+    pairs, placed_mid, swapped_up, grad_branch_three, text_here = tie(
+        pairs, placed_mid, swapped_up, grad_branch_three, text_here
+    )
+    text_pre = nn(text_here, w_text) + bias_in[1, 1:].reshape(1, -1)
     ckey_pre = text_pre[:, :columns]
-    inverse_ck = lax.rsqrt(
-        text_sum(jnp.sum(ckey_pre * ckey_pre, -1)[None])[0] / width + EPS
-    )[:, None]
+    text_squares = text_sum(jnp.sum(ckey_pre * ckey_pre, -1)[None])[0]
+    inverse_ck = lax.rsqrt(text_squares / width + EPS)[:, None]
     text_pair = jnp.concatenate(
         (
             (ckey_pre * inverse_ck * gains[3]).astype(BF16),
@@ -946,21 +966,28 @@
         ),
         1,
     )
-
-    cross_act, text_pair = spread(cross_share, (text_pair,))
-    text_pairs = gather_pieces(text_pair)
-    placed_second = place_weight(after(down_parts[1], placed_first))
-    cquery_pre = nn(cross_act, w_mid[:, 3 * columns : 4 * columns]) + bias_in[1, 0]
+    w_mid = gather_weight(placed_mid)
+    w_up = gather_far(swapped_up)
+    text_pairs = gather_pieces(after(text_pair, pairs))
+    attn_full, attn_low, attn_lines = attend(query_low, pairs, ids_here, key_code, True)
+    (parts,) = collect(attn_low, w_second, 0, columns)
+    swapped_down = swap(after(ffn_out.T, parts))
+    state_one, branch_one, cross_share = vmem_call(
+        share_middle,
+        [share_full, share_full, share_low],
+        (*parts, state_in, ids_share, vectors),
+        "share_middle",
+    )
+
+    cross_act, text_pairs, swapped_down = spread(cross_share, (text_pairs,), (swapped_down,))
+    w_down = gather_far(swapped_down)
+    cquery_pre = nn(cross_act, w_mid[:, :columns]) + bias_in[1, 0]
     cross_lines_here = lines_of(squares(cquery_pre, columns, 1))
-    cross_lines_here, text_pairs = tie(cross_lines_here, text_pairs)
     cquery_low, inverse_cq = shape_cross(cquery_pre, cross_lines_here, gains, width)
     cross_full, cross_low, total_lines = attend(
         cquery_low, text_pairs, ids_here, text_code, False
     )
-    parts, placed_second = collect(
-        cross_low, w_mid, 4 * columns, columns, (), (placed_second,)
-    )
-    w_down = gather_weight(jnp.concatenate((placed_first, placed_second), 2))
+    (parts,) = collect(cross_low, w_mid, columns, columns)
     state_two, ffn_share = vmem_call(
         share_last,
         [share_full, share_low],
@@ -971,13 +998,11 @@
     ffn_act = spread(ffn_share)
     hidden_pre = nn(ffn_act, w_up) + bias_ffn
     hidden_low = jax.nn.gelu(hidden_pre, approximate=True).astype(BF16)
-    grad_branch_three = spread(after(top_share, cross_act))
 
     gelu_pull = jax.vjp(lambda h: jax.nn.gelu(h, approximate=True), hidden_pre)[1]
     grad_hidden = gelu_pull(nn(grad_branch_three, w_down))[0].astype(BF16)
     part_down = weight_grad(grad_branch_three, hidden_low)
     part_up = weight_grad(ffn_act, grad_hidden)
-    half_down = scatter_weight(part_down)
     half_up = scatter_weight(part_up)
     parts, part_down, part_up = collect(
         grad_hidden, w_up, 0, hidden, (part_down,), (part_up,)
@@ -989,6 +1014,7 @@
         "share_back_last",
     )
 
+    half_down = scatter_far(after(part_down, gb2_share))
     grad_branch_two = spread(gb2_share)
     out_parts, = collect(after(hidden_low, gb2_share), w_down, 0, hidden)
     out_share, sums_three = vmem_call(
@@ -997,7 +1023,8 @@
         (*out_parts, state_two, grad_top, ids_share, vectors),
         "share_result",
     )
-    grad_cross = nn(grad_branch_two, w_mid[:, 4 * columns :]).astype(BF16)
+    grad_cross = nn(grad_branch_two, w_mid[:, columns:]).astype(BF16)
+    hidden_half = hidden // 2
     grad_cquery, text_near, text_far = attend_back(
         cquery_low,
         grad_cross,
@@ -1018,9 +1045,7 @@
     for mask in hop_rest[::-1]:
         rows_left = gpair.shape[0] // 2
         gpair = add_low(gpair[:rows_left], hop(gpair[rows_left:], mask))
-    parts, gpair, out_share = collect(
-        gcq_low, w_mid, 3 * columns, columns, (), (gpair, out_share)
-    )
+    parts, gpair, out_share = collect(gcq_low, w_mid, 0, columns, (gpair,), (out_share,))
     grad_one, gb1_share, sums_one = vmem_call(
         share_back_middle,
         [share_full, share_low, sums_shape(latents + 3)],
@@ -1032,13 +1057,14 @@
     sums_ck = text_sum(jnp.sum(gains[3] * gckey * ckey_pre, -1)[None])[0]
     out_both = give_far(out_share)
     grad_branch_one, sums_ck, out_both = spread(gb1_share, (sums_ck,), (out_both,))
+    home_up = home_parts(after(half_up, out_both))
     out_both, out_across = give_across(out_both)
     gck_low = rms_pull(ckey_pre, inverse_ck, gains[3], gckey, sums_ck[:, None], width)
     gtext = jnp.concatenate((gck_low, gpair[:, columns:]), 1)
-    text_part = nt(gtext, w_mid[:, : 2 * columns]).astype(BF16)
+    text_part = nt(gtext, w_text).astype(BF16)
     text_back = hop(text_part[2 * half :], hop_w)
 
-    grad_attn = nn(grad_branch_one, w_mid[:, 2 * columns : 3 * columns]).astype(BF16)
+    grad_attn = nn(grad_branch_one, w_attn_out).astype(BF16)
     part_mid = jnp.concatenate(
         (
             weight_grad(text_here, gtext),
@@ -1050,75 +1076,55 @@
     )
     half_mid = scatter_weight(part_mid)
     grad_attn, text_back, out_across = tie(grad_attn, text_back, out_across)
-    block_out = give_back(out_both, out_across, lambda place_here: place_here)
     grad_query, near, far = attend_back(
         query_low, grad_attn, attn_full, attn_lines, pairs, ids_here, key_code, True
     )
+    far = hop(far, hop_c)
+    kv_back = add_low(near, far)
+    for mask in hop_rest[::-1]:
+        rows_left = kv_back.shape[0] // 2
+        kv_back = add_low(kv_back[:rows_left], hop(kv_back[rows_left:], mask))
+    kv_back, home_up = tie(kv_back, home_up)
+    gquery, gkey, head_lines = turn_back(
+        grad_query, kv_back, projected, gains, cosine, signed
+    )
+    head_lines = lines_of(head_lines)
     text_sub = half // 2
     text_part = text_part[: 2 * half].astype(F32) + text_back.astype(F32)
     text_part = text_part.reshape(2, 2, text_sub, width)
     text_share = lax.dynamic_index_in_dim(text_part, x, 1, keepdims=False)
     text_given = lax.dynamic_index_in_dim(text_part, 1 - x, 1, keepdims=False)
     text_got = hop(text_given.astype(BF16), hop_x)
-    far = hop(far, hop_c)
-    far, text_got = tie(far, text_got)
-    kv_back = add_low(near, far)
+    block_out = give_back(out_both, out_across, lambda place_here: place_here)
+    head_lines, text_got, block_out = tie(head_lines, text_got, block_out)
     text_share = (text_share + text_got.astype(F32)).astype(BF16)
-    text_both = give_far(text_share.reshape(2 * text_sub, width))
-    home_down = [home_parts(half_down[:, :, :hidden_half])]
-    for mask in hop_rest[::-1]:
-        rows_left = kv_back.shape[0] // 2
-        given = hop(kv_back[rows_left:], mask)
-        if mask == hop_rest[0]:
-            given, text_both, home_down[0] = tie(given, text_both, home_down[0])
-        kv_back = add_low(kv_back[:rows_left], given)
-    text_both, text_across = give_across(text_both)
-    gquery, gkey, head_lines = turn_back(
-        grad_query, kv_back, projected, gains, cosine, signed
-    )
-    head_lines = lines_of(head_lines)
-    head_lines, text_across, block_out = tie(head_lines, text_across, block_out)
     grad_proj, sums_heads = back_heads(
         gquery, gkey, projected, inverse, kv_back, head_lines, gains, width
     )
-    grad_text = give_back(
-        text_both,
-        text_across,
-        lambda place_here: ((place_here & 1) << 1) | (place_here >> 1),
-    ).astype(F32)
     part_attn = weight_grad(act_low, grad_proj)
+    part_whole = part_attn
     part_attn = part_attn.reshape((2,) * (bits - 1) + (2, slice_rows, 3 * columns))
     steps = [(0, hop_c, c)] + [
         (1 + i, tensor_size << b, seq_bit(b)) for i, b in enumerate(rest[::-1])
     ]
-    for axis, mask, mine in steps:
+    given = hop(lax.dynamic_index_in_dim(part_attn, 1 - c, 0, keepdims=True), hop_c)
+    part_attn = add_low(lax.dynamic_index_in_dim(part_attn, c, 0, keepdims=True), given)
+    part_near = part_attn
+    for axis, mask, mine in steps[1:]:
         kept = lax.dynamic_index_in_dim(part_attn, mine, axis, keepdims=True)
         given = lax.dynamic_index_in_dim(part_attn, 1 - mine, axis, keepdims=True)
         part_attn = add_low(kept, hop(given, mask))
     part_attn = part_attn.reshape(2, slice_rows, 3 * columns)
-    home_down.append(home_parts(after(half_down[:, :, hidden_half:], home_down[0])))
-    home_up = [home_parts(half_up[:, :, :hidden_half])]
-    parts, home_down[1], home_up[0] = collect(
-        grad_proj, w_attn, 0, 3 * columns, (home_down[1],), (home_up[0],)
-    )
+    parts, part_near, part_attn = collect(
+        after(grad_proj, part_whole), w_first, 0, 3 * columns, (part_near,), (part_attn,)
+    )
+    home_down = swap(after(half_down, parts))
     grad_share, sums_zero = vmem_call(
         share_back_first,
         [share_low, sums_shape(2 * latents)],
         (*parts, state_in, grad_one, ids_share, vectors),
         "share_back_first",
     )
-    home_up.append(home_parts(after(half_up[:, :, hidden_half:], home_up[0])))
-    in_both = give_far(grad_share)
-    in_both, home_up[1] = tie(in_both, home_up[1])
-    in_both, in_across = give_across(in_both)
-    home_mid = home_parts(half_mid)
-    in_across, home_mid = tie(in_across, home_mid)
-    grad_inputs = give_back(in_both, in_across, lambda place_here: place_here).astype(F32)
-    grad_attn_in = whole_of(home_parts(part_attn))
-    grad_mid = whole_of(home_mid)
-    grad_up = jnp.concatenate([whole_of(h) for h in home_up], 1)
-    grad_down = jnp.concatenate([whole_of(h) for h in home_down], 1)
-
     rows_sum = lambda a: jnp.sum(a.astype(F32), 0)
     extra = -hidden % columns
     column_sums = jnp.concatenate(
@@ -1133,13 +1139,6 @@
         ),
         0,
     )
-    column_sums = all_sum(column_sums, [hop_c] + hop_rest + [hop_k])
-    low_sums = column_sums.astype(BF16)
-    column_sums = by_home(low_sums, hop(low_sums, hop_w)).astype(F32)
-    grad_in_bias = column_sums[:6].reshape(2, 3, columns)
-    grad_gains = column_sums[6:10]
-    grad_ffn_bias = column_sums[10:].reshape(-1)[:hidden]
-
     count = latents
     feature_sums = jnp.concatenate(
         (
@@ -1153,10 +1152,53 @@
         ),
         0,
     )
-    feature_sums = all_sum(feature_sums, [hop_c, hop_x, hop_w] + hop_rest)
-    low_features = arrange(feature_sums.astype(BF16), order_back)
-    far_features = hop(low_features, hop_k).astype(F32)
-    near_features = low_features.astype(F32)
+    marks = column_sums.shape[0]
+    lanes = width // columns
+    column_sums = jnp.pad(column_sums, ((0, -marks % lanes), (0, 0))).reshape(-1, width)
+    features = feature_sums.shape[0]
+    near_sums = jnp.concatenate((feature_sums, column_sums), 0).astype(BF16)
+    far_sums = hop(near_sums, hop_k)
+    text_share = text_share.reshape(2 * text_sub, width)
+    both = give_far_two(grad_share, text_share)
+    home_attn = home_parts(after(part_attn, both, far_sums))
+    home_mid = home_parts(after(half_mid, both, far_sums))
+    across = hop(both, hop_x)
+    returned = ((0, both), (1, hop(both, hop_c)), (2, across), (3, hop(across, hop_c)))
+
+    def put_back(first, rows_each, position):
+        out = jnp.zeros((micros, 4, rows_each, width), BF16)
+        for offset, value in returned:
+            out = lax.dynamic_update_index_in_dim(
+                out, value[:, first : first + rows_each], position(t ^ offset), 1
+            )
+        return out.reshape(micros, 4 * rows_each, width).astype(F32)
+
+    grad_inputs = put_back(0, piece, lambda place_here: place_here)
+    grad_text = put_back(
+        piece, text_sub, lambda place_here: ((place_here & 1) << 1) | (place_here >> 1)
+    )
+    grad_attn_in = whole_of(home_attn)
+    grad_mid = whole_of(home_mid)
+    grad_up = whole_of(home_up)
+    grad_down = home_down.astype(F32)
+
+    column_sums = near_sums[features:].astype(F32) + far_sums[features:].astype(F32)
+    sums = jnp.concatenate(
+        (near_sums[:features].astype(F32), far_sums[:features].astype(F32), column_sums), 0
+    )
+    sums = all_sum(sums, [hop_c])
+    feature_sums = all_sum(sums[: 2 * features], [hop_x, hop_w])
+    sums = all_sum(jnp.concatenate((feature_sums, sums[2 * features :]), 0), hop_rest)
+    sums = sums.astype(BF16)
+    column_sums = sums[2 * features :]
+    column_sums = by_home(column_sums, hop(column_sums, hop_w)).astype(F32)
+    column_sums = column_sums.reshape(-1, columns)[:marks]
+    grad_in_bias = column_sums[:6].reshape(2, 3, columns)
+    grad_gains = column_sums[6:10]
+    grad_ffn_bias = column_sums[10:].reshape(-1)[:hidden]
+
+    near_features = arrange(sums[:features], order_back).astype(F32)
+    far_features = arrange(sums[features : 2 * features], order_back).astype(F32)
     both_sums = near_features + far_features
     count = 6 * latents
     near_temb = near_features[:count].reshape(6, latents, width).transpose(1, 0, 2)

time: 873 us -> 845 us (0.968)
  starting transfers between devices: 169 us -> 133 us
    ppermute x11 -> x9, starting transfers between devices: 31.6 us -> 10.7 us  [swap(): return jnp.where(c == w, value, lax.ppermute(value, AXES, pairs_here))]
    ppermute x10 -> x6, starting transfers between devices: 23.1 us -> 9.87 us  [swap_far(): return lax.ppermute(value, AXES, [(d, other(d)) for d in range(places)])]
    dynamic_update_slice x0 -> x9, local copies, waits for them, and re-layouts: none -> 9.08 us  [put_back(): lax.dynamic_update_index_in_dim(out, value[:, first:first + rows_each], p...]
    ppermute x109 -> x102, waiting for transfers between devices: 297 us -> 302 us  [hop(): return lax.ppermute(value, AXES, [(d, d ^ mask) for d in range(places)])]
    pallas_call x37 -> x38, Pallas kernels: 79.2 us -> 75 us  [vmem_call(): pl.pallas_call(kernel, out_shape=outs, in_specs=[whole] * len(args), out_...]
    ppermute x109 -> x102, starting transfers between devices: 114 us -> 111 us  [hop(): return lax.ppermute(value, AXES, [(d, d ^ mask) for d in range(places)])]
    unnamed x319 -> x361, local copies, waits for them, and re-layouts: 56.1 us -> 53.6 us
    ppermute x10 -> x6, waiting for transfers between devices: 65.7 us -> 67.7 us  [swap_far(): return lax.ppermute(value, AXES, [(d, other(d)) for d in range(places)])]
  transfers between devices with their start and end apart: 137 -> 125, of which waited for: 60 -> 54; matrix products, arithmetic and copies ran while one was open for 20% -> 19% of each run, Pallas kernels for 9% -> 9%
where the time goes in v3:
time: 845 us; the launch traced here: 835 us
  waiting for transfers between devices  370 us (44%)
  starting transfers between devices  133 us (16%)
  local copies, waits for them, and re-layouts  128 us (15%)
  Pallas kernels  75 us (9%)
  matrix products  57.4 us (7%)
  other arithmetic  53.9 us (6%)
  between operations  17.3 us (2%)
    ppermute x102, waiting for transfers between devices, hop(): return lax.ppermute(value, AXES, [(d, d ^ mask) for d in range(places)])  302 us
    ppermute x102, starting transfers between devices, hop(): return lax.ppermute(value, AXES, [(d, d ^ mask) for d in range(places)])  111 us
    pallas_call x38, Pallas kernels, vmem_call(): pl.pallas_call(kernel, out_shape=outs, in_specs=[whole] * len(args), out_...  75 us
    ppermute x6, waiting for transfers between devices, swap_far(): return lax.ppermute(value, AXES, [(d, other(d)) for d in range(places)])  67.7 us
    unnamed x361, local copies, waits for them, and re-layouts  53.6 us
    dot_general x7, matrix products, nn(): lax.dot_general(a, b, (((1,), (0,)), ((), ())), preferred_element_type=F32)  34.2 us
    dot_general x7, matrix products, tn(): lax.dot_general(a, b, (((0,), (0,)), ((), ())), preferred_element_type=F32)  21 us
  transfers between devices with their start and end apart: 125, of which 54 were waited for; matrix products, arithmetic and copies ran while one was open for 19% of the time, Pallas kernels for 9%

profile of v3, /device:TPU:0, one launch (start us, length us, event | category | flops | bytes accessed | tf_op | source)
XLA Modules:
  0.0 834.9 jit_solution(5963740332886263288)
XLA Ops:
  9.1 4.1 collective-permute-start.7
  13.2 20.1 %collective-permute-done.7 = bf16[192,1152]{1,0:T(8,128)(2,1)S(1)} collective-permute-done((bf16[192,1152]{1,0:T(8,128)(2,1)S(1)}, bf16[192,1152]{1,0:T(8,128)(2,1)S(1)}, u32[]{:S(2)}, u32[]{:S(2)}) %collective-permute-start.7) | collective-permute-done | bytes 442400 | tf_op jit(solution)/shard_map/ppermute | solution.py:680
  40.0 6.8 collective-permute-done.1
  50.0 9.0 %collective-permute-done.3.refs_2_ = bf16[128,1536]{1,0:T(8,128)(2,1)S(1)} collective-permute-done((bf16[128,1536]{1,0:T(8,128)(2,1)S(1)}, bf16[128,1536]{1,0:T(8,128)(2,1)S(1)}, u32[]{:S(2)}, u32[]{:S(2)}) %collective-permute-start.3) | collective-permute-done | bytes 393248 | tf_op jit(solution)/shard_map/ppermute | solution.py:667
  60.9 3.9 collective-permute-done.4.refs_3_
  73.8 19.9 %collective-permute-done.28 = bf16[192,1152]{1,0:T(8,128)(2,1)S(1)} collective-permute-done((bf16[192,1152]{1,0:T(8,128)(2,1)S(1)}, bf16[192,1152]{1,0:T(8,128)(2,1)S(1)}, u32[]{:S(2)}, u32[]{:S(2)}) %collective-permute-start.28) | collective-permute-done | bytes 442400 | tf_op jit(solution)/shard_map/ppermute | solution.py:680
  94.8 4.7 convolution_add_fusion.1.refs_0_.value_ref
  128.5 3.6 shape_heads.1
  135.1 8.6 %collective-permute-done.25 = bf16[96,1536]{1,0:T(8,128)(2,1)} collective-permute-done((bf16[96,1536]{1,0:T(8,128)(2,1)}, bf16[96,1536]{1,0:T(8,128)(2,1)}, u32[]{:S(2)}, u32[]{:S(2)}) %collective-permute-start.25) | collective-permute-done | bytes 294944 | tf_op jit(solution)/shard_map/ppermute | solution.py:667
  153.1 26.2 %collective-permute-done.22.refs_2_ = bf16[128,1536]{1,0:T(8,128)(2,1)} collective-permute-done((bf16[128,1536]{1,0:T(8,128)(2,1)S(1)}, bf16[128,1536]{1,0:T(8,128)(2,1)}, u32[]{:S(2)}, u32[]{:S(2)}) %collective-permute-start.22) | collective-permute-done | bytes 393248 | tf_op jit(solution)/shard_map/ppermute | solution.py:667
  201.6 8.5 %attend.1 = (f32[512,384]{1,0:T(8,128)S(1)}, bf16[512,384]{1,0:T(8,128)(2,1)S(1)}, f32[8,512]{1,0:T(8,128)S(1)}) custom-call(bf16[512,384]{1,0:T(8,128)(2,1)S(1)} %copy-done.63, s32[512,1]{1,0:T(8,128)S(1)} %copy.136.qcode_ref, s32[1,2048]{1,0:T(1,128)S(1)} %select_n.393.kcode_ref, bf16[512,768]{1,0:T(8,128)(2,1)} %get-tuple-element.181.refs_0_, ...), custom_call_target="tpu_custom_call" | custom-call | flops 1024 | bytes 1024 | tf_op jit(solution)/shard_map/attend/pallas_call | solution.py:49
  224.6 5.7 collective-permute-done.31.p1
  233.2 9.3 %collective-permute-done.38.refs_1_ = bf16[384,768]{1,0:T(8,128)(2,1)S(1)} collective-permute-done((bf16[384,768]{1,0:T(8,128)(2,1)S(1)}, bf16[384,768]{1,0:T(8,128)(2,1)S(1)}, u32[]{:S(2)}, u32[]{:S(2)}) %collective-permute-start.38) | collective-permute-done | bytes 589856 | tf_op jit(solution)/shard_map/ppermute | solution.py:667
  250.5 6.6 collective-permute-done.33.refs_1_
  257.0 5.7 collective-permute-done.34.refs_2_
  267.2 4.0 collective-permute-done.41.refs_3_
  271.2 4.4 collective-permute-done.42.refs_4_
  286.4 11.7 %collective-permute-done.45.l2 = f32[8,512]{1,0:T(8,128)S(1)} collective-permute-done((f32[8,512]{1,0:T(8,128)S(1)}, f32[8,512]{1,0:T(8,128)S(1)}, u32[]{:S(2)}, u32[]{:S(2)}) %collective-permute-start.45) | collective-permute-done | bytes 16416 | tf_op jit(solution)/shard_map/ppermute | solution.py:667
  302.8 4.7 attend_text.1
  309.2 6.3 collective-permute-done.47.from_x
  321.9 6.4 collective-permute-done.49.p1
  328.3 7.9 collective-permute-done.50.p2
  339.2 16.1 %collective-permute-done.52.refs_2_ = bf16[128,1536]{1,0:T(8,128)(2,1)S(1)} collective-permute-done((bf16[128,1536]{1,0:T(8,128)(2,1)S(1)}, bf16[128,1536]{1,0:T(8,128)(2,1)S(1)}, u32[]{:S(2)}, u32[]{:S(2)}) %collective-permute-start.52) | collective-permute-done | bytes 393248 | tf_op jit(solution)/shard_map/ppermute | solution.py:667
  361.4 6.2 collective-permute-done.54.refs_4_
  368.8 11.1 %multiply_convert_fusion = (bf16[512,2240]{1,0:T(8,128)(2,1)}, f32[512,2240]{1,0:T(8,128)}) fusion(f32[2240]{0:T(1024)S(1)} %slice.883, bf16[512,1536]{1,0:T(8,128)(2,1)} %copy-done.58, bf16[1536,2240]{1,0:T(8,128)(2,1)} %all-gather.18.cloned.1.call-done.weight_ref), kind=kOutput, calls=%fused_computation.14 | convolution fusion | flops 3534684160 | bytes 15344384 | tf_op jit(solution)/shard_map/dot_general | solution.py:25
  379.9 10.6 %fusion.59 = (bf16[2240]{0:T(1024)(128)(2,1)}, bf16[512,2240]{1,0:T(8,128)(2,1)S(1)}) fusion(f32[512,2240]{1,0:T(8,128)} %get-tuple-element.525, bf16[512,1536]{1,0:T(8,128)(2,1)} %copy-done.54, bf16[1536,2240]{1,0:T(8,128)(2,1)} %all-gather.16.cloned.1.call-done.weight_ref), kind=kOutput, calls=%fused_computation.221 | convolution fusion | flops 3547297536 | bytes 15339904 | tf_op jit(solution)/shard_map/dot_general | solution.py:25
  390.5 5.9 convolution_convert_fusion
  403.3 4.6 project_out.8
  413.1 6.3 convolution_convert_fusion.1
  423.7 6.9 collective-permute-done.57.p1
  441.3 5.7 collective-permute-done.60.refs_2_
  452.7 3.6 collective-permute-done.62.refs_4_
  458.9 7.2 attend_text_back.1
  469.4 3.8 project_out.10
  493.4 5.8 collective-permute-done.75.p2
  514.5 15.3 %collective-permute-done.68.from_w = bf16[64,1536]{1,0:T(8,128)(2,1)S(1)} collective-permute-done((bf16[64,1536]{1,0:T(8,128)(2,1)S(1)}, bf16[64,1536]{1,0:T(8,128)(2,1)S(1)}, u32[]{:S(2)}, u32[]{:S(2)}) %collective-permute-start.68) | collective-permute-done | bytes 196640 | tf_op jit(solution)/shard_map/ppermute | solution.py:667
  531.3 3.4 collective-permute-start.80
  550.1 15.6 %collective-permute-done.83 = bf16[64,1536]{1,0:T(8,128)(2,1)S(1)} collective-permute-done((bf16[64,1536]{1,0:T(8,128)(2,1)S(1)}, bf16[64,1536]{1,0:T(8,128)(2,1)S(1)}, u32[]{:S(2)}, u32[]{:S(2)}) %collective-permute-start.83) | collective-permute-done | bytes 196640 | tf_op jit(solution)/shard_map/ppermute | solution.py:667
  580.0 6.4 collective-permute-done.84
  587.3 12.4 %attend_back.1 = (f32[512,384]{1,0:T(8,128)S(1)}, bf16[1024,768]{1,0:T(8,128)(2,1)S(1)}, bf16[1024,768]{1,0:T(8,128)(2,1)}) custom-call(bf16[512,384]{1,0:T(8,128)(2,1)S(1)} %copy-done.64, bf16[512,384]{1,0:T(8,128)(2,1)S(1)} %convolution_convert_fusion.8.grad_ref, f32[512,384]{1,0:T(8,128)S(1)} %copy-done.74, f32[8,512]{1,0:T(8,128)S(1)} %get-tuple-element.280.line_ref, ...), custom_call_target="tpu_custom_call" | custom-call | flops 1024 | bytes 1024 | tf_op jit(solution)/shard_map/attend_back/pallas_call | solution.py:49
  620.6 22.3 %collective-permute-done.87 = bf16[512,768]{1,0:T(8,128)(2,1)} collective-permute-done((bf16[512,768]{1,0:T(8,128)(2,1)}, bf16[512,768]{1,0:T(8,128)(2,1)}, u32[]{:S(2)}, u32[]{:S(2)}) %collective-permute-start.87) | collective-permute-done | bytes 786464 | tf_op jit(solution)/shard_map/ppermute | solution.py:667
  645.3 16.5 %collective-permute-done.89 = bf16[192,2240]{1,0:T(8,128)(2,1)S(1)} collective-permute-done((bf16[192,2240]{1,0:T(8,128)(2,1)S(1)}, bf16[192,2240]{1,0:T(8,128)(2,1)S(1)}, u32[]{:S(2)}, u32[]{:S(2)}) %collective-permute-start.89) | collective-permute-done | bytes 860192 | tf_op jit(solution)/shard_map/ppermute | solution.py:680
  701.3 16.8 %collective-permute-done.101 = bf16[1,1,2,192,1152]{4,3,2,1,0:T(8,128)(2,1)} collective-permute-done((bf16[1,1,2,192,1152]{4,3,2,1,0:T(8,128)(2,1)}, bf16[1,1,2,192,1152]{4,3,2,1,0:T(8,128)(2,1)}, u32[]{:S(2)}, u32[]{:S(2)}) %collective-permute-start.101) | collective-permute-done | bytes 884768 | tf_op jit(solution)/shard_map/ppermute | solution.py:667
  728.5 9.9 %collective-permute-done.106 = bf16[27,1536]{1,0:T(8,128)(2,1)S(1)} collective-permute-done((bf16[27,1536]{1,0:T(8,128)(2,1)S(1)}, bf16[27,1536]{1,0:T(8,128)(2,1)S(1)}, u32[]{:S(2)}, u32[]{:S(2)}) %collective-permute-start.106) | collective-permute-done | bytes 82976 | tf_op jit(solution)/shard_map/ppermute | solution.py:667
  752.4 10.8 %collective-permute-done.109 = bf16[46,1536]{1,0:T(8,128)(2,1)S(1)} collective-permute-done((bf16[46,1536]{1,0:T(8,128)(2,1)S(1)}, bf16[46,1536]{1,0:T(8,128)(2,1)S(1)}, u32[]{:S(2)}, u32[]{:S(2)}) %collective-permute-start.109) | collective-permute-done | bytes 141344 | tf_op jit(solution)/shard_map/ppermute | solution.py:667
  766.3 3.6 collective-permute-done.110
  793.3 10.6 %collective-permute-start.105 = (bf16[2,112,1536]{2,1,0:T(8,128)(2,1)}, bf16[2,112,1536]{2,1,0:T(8,128)(2,1)S(1)}, u32[]{:S(2)}, u32[]{:S(2)}) collective-permute-start(bf16[2,112,1536]{2,1,0:T(8,128)(2,1)} %collective-permute-done.104), channel_id=1, source_target_pairs={{0,1},{1,0},{2,3},{3,2},{4,5},{5,4},{6,7},{7,6},{8,9},{9,8},{10,11... | collective-permute-start | bytes 2064392 | tf_op jit(solution)/shard_map/ppermute | solution.py:667
  807.4 11.2 %collective-permute-done.115 = bf16[192,1920]{1,0:T(8,128)(2,1)} collective-permute-done((bf16[192,1920]{1,0:T(8,128)(2,1)}, bf16[192,1920]{1,0:T(8,128)(2,1)}, u32[]{:S(2)}, u32[]{:S(2)}) %collective-permute-start.115) | collective-permute-done | bytes 737312 | tf_op jit(solution)/shard_map/ppermute | solution.py:680
  (858 shorter events, 381.1 us)
Async XLA Ops:
  7.2 87.6 %all-gather.10.cloned.1.call-start = ((), (), s32[]{:S(2)}) async-start(), calls=%async_computation.3 | async-start | bytes 4423680 | tf_op jit(solution)/shard_map/all_gather | solution.py:705
  9.1 24.3 %collective-permute-start.7 = (bf16[192,1152]{1,0:T(8,128)(2,1)S(1)}, bf16[192,1152]{1,0:T(8,128)(2,1)S(1)}, u32[]{:S(2)}, u32[]{:S(2)}) collective-permute-start(bf16[192,1152]{1,0:T(8,128)(2,1)S(1)} %bitcast.220), channel_id=1, source_target_pairs={{0,16},{1,24},{2,18},{3,26},{4,20},{5,28},{6,22},{7,30},{8,17},{9,... | collective-permute-start | bytes 1327112 | tf_op jit(solution)/shard_map/ppermute | solution.py:680
  34.5 159.9 %all-gather.12.cloned.1.call-start = ((), (), s32[]{:S(2)}) async-start(), calls=%async_computation.7 | async-start | bytes 4423680 | tf_op jit(solution)/shard_map/all_gather | solution.py:705
  70.5 23.2 %collective-permute-start.28 = (bf16[192,1152]{1,0:T(8,128)(2,1)S(1)}, bf16[192,1152]{1,0:T(8,128)(2,1)S(1)}, u32[]{:S(2)}, u32[]{:S(2)}) collective-permute-start(bf16[192,1152]{1,0:T(8,128)(2,1)S(1)} %pad_maximum_fusion.6), channel_id=1, source_target_pairs={{0,16},{1,24},{2,18},{3,26},{4,20},{5,28},{6,22},{7,30},{8,17},{9,... | collective-permute-start | bytes 1327112 | tf_op jit(solution)/shard_map/ppermute | solution.py:680
  99.5 180.0 %all-gather.14.cloned.1.call-start = ((), (), s32[]{:S(2)}) async-start(), calls=%async_computation.8 | async-start | bytes 2949120 | tf_op jit(solution)/shard_map/all_gather | solution.py:705
  112.8 34.5 %collective-permute-start.20 = (bf16[64,1536]{1,0:T(8,128)(2,1)}, bf16[64,1536]{1,0:T(8,128)(2,1)}, u32[]{:S(2)}, u32[]{:S(2)}) collective-permute-start(bf16[64,1536]{1,0:T(8,128)(2,1)} %concatenate.144), channel_id=1, source_target_pairs={{0,16},{1,17},{2,18},{3,19},{4,20},{5,21},{6,22},{7,23},{8,24},{9,... | collective-permute-start | bytes 589832 | tf_op jit(solution)/shard_map/ppermute | solution.py:667
  114.5 29.2 %collective-permute-start.25 = (bf16[96,1536]{1,0:T(8,128)(2,1)}, bf16[96,1536]{1,0:T(8,128)(2,1)}, u32[]{:S(2)}, u32[]{:S(2)}) collective-permute-start(bf16[96,1536]{1,0:T(8,128)(2,1)} %concatenate.147), channel_id=1, source_target_pairs={{0,16},{1,17},{2,18},{3,19},{4,20},{5,21},{6,22},{7,23},{8,24},{9,... | collective-permute-start | bytes 884744 | tf_op jit(solution)/shard_map/ppermute | solution.py:667
  125.3 24.2 %collective-permute-start.18 = (bf16[192,768]{1,0:T(8,128)(2,1)S(1)}, bf16[192,768]{1,0:T(8,128)(2,1)S(1)}, u32[]{:S(2)}, u32[]{:S(2)}) collective-permute-start(bf16[192,768]{1,0:T(8,128)(2,1)S(1)} %copy-done.115), channel_id=1, source_target_pairs={{0,16},{1,24},{2,18},{3,26},{4,20},{5,28},{6,22},{7,30},{8,17},{9,... | collective-permute-start | bytes 884744 | tf_op jit(solution)/shard_map/ppermute | solution.py:680
  127.8 23.7 %collective-permute-start.17 = (bf16[192,768]{1,0:T(8,128)(2,1)S(1)}, bf16[192,768]{1,0:T(8,128)(2,1)S(1)}, u32[]{:S(2)}, u32[]{:S(2)}) collective-permute-start(bf16[192,768]{1,0:T(8,128)(2,1)S(1)} %copy-done.115), channel_id=1, source_target_pairs={{1,8},{3,10},{5,12},{7,14},{8,1},{10,3},{12,5},{14,7},{17,24},{19,... | collective-permute-start | bytes 884744 | tf_op jit(solution)/shard_map/ppermute | solution.py:673
  133.6 49.5 %collective-permute-start.14 = (bf16[512,768]{1,0:T(8,128)(2,1)}, bf16[512,768]{1,0:T(8,128)(2,1)}, u32[]{:S(2)}, u32[]{:S(2)}) collective-permute-start(bf16[512,768]{1,0:T(8,128)(2,1)} %get-tuple-element.181.refs_0_), channel_id=1, source_target_pairs={{0,4},{1,5},{2,6},{3,7},{4,0},{5,1},{6,2},{7,3},{8,12},{9,13},{10,... | collective-permute-start | bytes 2359304 | tf_op jit(solution)/shard_map/ppermute | solution.py:667
  145.5 46.0 %collective-permute-start.19 = (bf16[192,2240]{1,0:T(8,128)(2,1)}, bf16[192,2240]{1,0:T(8,128)(2,1)}, u32[]{:S(2)}, u32[]{:S(2)}) collective-permute-start(bf16[192,2240]{1,0:T(8,128)(2,1)} %param.34), channel_id=1, source_target_pairs={{1,8},{3,10},{5,12},{7,14},{8,1},{10,3},{12,5},{14,7},{17,24},{19,... | collective-permute-start | bytes 2580488 | tf_op jit(solution)/shard_map/ppermute | solution.py:673
  147.3 34.7 %collective-permute-start.26 = (bf16[192,1536]{1,0:T(8,128)(2,1)}, bf16[192,1536]{1,0:T(8,128)(2,1)}, u32[]{:S(2)}, u32[]{:S(2)}) collective-permute-start(bf16[192,1536]{1,0:T(8,128)(2,1)} %pad_maximum_fusion.3), channel_id=1, source_target_pairs={{0,8},{1,9},{2,10},{3,11},{4,12},{5,13},{6,14},{7,15},{8,0},{9,1},... | collective-permute-start | bytes 1769480 | tf_op jit(solution)/shard_map/ppermute | solution.py:667
  149.5 29.8 %collective-permute-start.22 = (bf16[128,1536]{1,0:T(8,128)(2,1)S(1)}, bf16[128,1536]{1,0:T(8,128)(2,1)}, u32[]{:S(2)}, u32[]{:S(2)}) collective-permute-start(bf16[128,1536]{1,0:T(8,128)(2,1)S(1)} %share_top.1.refs_0_.top_ref), channel_id=1, source_target_pairs={{0,8},{1,9},{2,10},{3,11},{4,12},{5,13},{6,14},{7,15},{8,0},{9,1},... | collective-permute-start | bytes 1179656 | tf_op jit(solution)/shard_map/ppermute | solution.py:667
  151.5 28.8 %collective-permute-start.21 = (bf16[128,1536]{1,0:T(8,128)(2,1)S(1)}, bf16[128,1536]{1,0:T(8,128)(2,1)}, u32[]{:S(2)}, u32[]{:S(2)}) collective-permute-start(bf16[128,1536]{1,0:T(8,128)(2,1)S(1)} %share_top.1.refs_0_.top_ref), channel_id=1, source_target_pairs={{0,2},{1,3},{2,0},{3,1},{4,6},{5,7},{6,4},{7,5},{8,10},{9,11},{10,... | collective-permute-start | bytes 1179656 | tf_op jit(solution)/shard_map/ppermute | solution.py:667
  193.7 175.1 %all-gather.18.cloned.1.call-start = ((), (), s32[]{:S(2)}) async-start(), calls=%async_computation.10 | async-start | bytes 7962624 | tf_op jit(solution)/shard_map/all_gather | solution.py:711
  194.2 185.6 %all-gather.16.cloned.1.call-start = ((), (), s32[]{:S(2)}) async-start(), calls=%async_computation.9 | async-start | bytes 7962624 | tf_op jit(solution)/shard_map/all_gather | solution.py:711
  198.7 18.2 %collective-permute-start.37 = (f32[1,384]{1,0:T(1,128)S(1)}, f32[1,384]{1,0:T(1,128)S(1)}, u32[]{:S(2)}, u32[]{:S(2)}) collective-permute-start(f32[1,384]{1,0:T(1,128)S(1)} %broadcast_in_dim.150), channel_id=1, source_target_pairs={{0,10},{1,11},{2,8},{3,9},{4,14},{5,15},{6,12},{7,13},{8,2},{9,3},... | collective-permute-start | bytes 4616 | tf_op jit(solution)/shard_map/ppermute | solution.py:667
  223.1 19.3 %collective-permute-start.38 = (bf16[384,768]{1,0:T(8,128)(2,1)S(1)}, bf16[384,768]{1,0:T(8,128)(2,1)S(1)}, u32[]{:S(2)}, u32[]{:S(2)}) collective-permute-start(bf16[384,768]{1,0:T(8,128)(2,1)S(1)} %pad_maximum_fusion.4.refs_0_), channel_id=1, source_target_pairs={{0,4},{1,5},{2,6},{3,7},{4,0},{5,1},{6,2},{7,3},{8,12},{9,13},{10,... | collective-permute-start | bytes 1769480 | tf_op jit(solution)/shard_map/ppermute | solution.py:667
  230.4 35.8 %collective-permute-start.43 = (bf16[192,2240]{1,0:T(8,128)(2,1)S(1)}, bf16[192,2240]{1,0:T(8,128)(2,1)S(1)}, u32[]{:S(2)}, u32[]{:S(2)}) collective-permute-start(bf16[192,2240]{1,0:T(8,128)(2,1)S(1)} %bitcast.227), channel_id=1, source_target_pairs={{1,8},{3,10},{5,12},{7,14},{8,1},{10,3},{12,5},{14,7},{17,24},{19,... | collective-permute-start | bytes 2580488 | tf_op jit(solution)/shard_map/ppermute | solution.py:673
  231.1 18.5 %collective-permute-start.39 = (bf16[384,768]{1,0:T(8,128)(2,1)S(1)}, bf16[384,768]{1,0:T(8,128)(2,1)S(1)}, u32[]{:S(2)}, u32[]{:S(2)}) collective-permute-start(bf16[384,768]{1,0:T(8,128)(2,1)S(1)} %pad_maximum_fusion.4.refs_0_), channel_id=1, source_target_pairs={{0,1},{1,0},{2,3},{3,2},{4,5},{5,4},{6,7},{7,6},{8,9},{9,8},{10,11... | collective-permute-start | bytes 1769480 | tf_op jit(solution)/shard_map/ppermute | solution.py:667
  242.5 20.3 %collective-permute-start.40 = (bf16[384,768]{1,0:T(8,128)(2,1)S(1)}, bf16[384,768]{1,0:T(8,128)(2,1)S(1)}, u32[]{:S(2)}, u32[]{:S(2)}) collective-permute-start(bf16[384,768]{1,0:T(8,128)(2,1)S(1)} %collective-permute-done.38.refs_1_), channel_id=1, source_target_pairs={{0,1},{1,0},{2,3},{3,2},{4,5},{5,4},{6,7},{7,6},{8,9},{9,8},{10,11... | collective-permute-start | bytes 1769480 | tf_op jit(solution)/shard_map/ppermute | solution.py:667
  275.6 339.0 %reduce-scatter.4.cloned.1.call-start = ((), (), s32[]{:S(2)}) async-start(), calls=%async_computation.4 | async-start | bytes 8847360 | tf_op jit(solution)/shard_map/reduce_scatter | solution.py:717
  338.2 17.0 %collective-permute-start.52 = (bf16[128,1536]{1,0:T(8,128)(2,1)S(1)}, bf16[128,1536]{1,0:T(8,128)(2,1)S(1)}, u32[]{:S(2)}, u32[]{:S(2)}) collective-permute-start(bf16[128,1536]{1,0:T(8,128)(2,1)S(1)} %get-tuple-element.220.refs_0_), channel_id=1, source_target_pairs={{0,8},{1,9},{2,10},{3,11},{4,12},{5,13},{6,14},{7,15},{8,0},{9,1},... | collective-permute-start | bytes 1179656 | tf_op jit(solution)/shard_map/ppermute | solution.py:667
  338.2 18.8 %collective-permute-start.51 = (bf16[128,1536]{1,0:T(8,128)(2,1)S(1)}, bf16[128,1536]{1,0:T(8,128)(2,1)S(1)}, u32[]{:S(2)}, u32[]{:S(2)}) collective-permute-start(bf16[128,1536]{1,0:T(8,128)(2,1)S(1)} %get-tuple-element.220.refs_0_), channel_id=1, source_target_pairs={{0,2},{1,3},{2,0},{3,1},{4,6},{5,7},{6,4},{7,5},{8,10},{9,11},{10,... | collective-permute-start | bytes 1179656 | tf_op jit(solution)/shard_map/ppermute | solution.py:667
  397.8 329.1 %reduce-scatter.8.cloned.1.call-start = ((), (), s32[]{:S(2)}) async-start(), calls=%async_computation.6 | async-start | bytes 7962624 | tf_op jit(solution)/shard_map/reduce_scatter | solution.py:726
  438.2 314.2 %reduce-scatter.6.cloned.1.call-start = ((), (), s32[]{:S(2)}) async-start(), calls=%async_computation.5 | async-start | bytes 7372800 | tf_op jit(solution)/shard_map/reduce_scatter | solution.py:717
  466.1 19.2 %collective-permute-start.66 = (bf16[768,768]{1,0:T(8,128)(2,1)S(1)}, bf16[768,768]{1,0:T(8,128)(2,1)S(1)}, u32[]{:S(2)}, u32[]{:S(2)}) collective-permute-start(bf16[768,768]{1,0:T(8,128)(2,1)S(1)} %get-tuple-element.239), channel_id=1, source_target_pairs={{0,1},{1,0},{2,3},{3,2},{4,5},{5,4},{6,7},{7,6},{8,9},{9,8},{10,11... | collective-permute-start | bytes 3538952 | tf_op jit(solution)/shard_map/ppermute | solution.py:667
  486.9 26.4 %collective-permute-start.69 = (bf16[384,768]{1,0:T(8,128)(2,1)}, bf16[384,768]{1,0:T(8,128)(2,1)}, u32[]{:S(2)}, u32[]{:S(2)}) collective-permute-start(bf16[384,768]{1,0:T(8,128)(2,1)} %slice.888), channel_id=1, source_target_pairs={{0,4},{1,5},{2,6},{3,7},{4,0},{5,1},{6,2},{7,3},{8,12},{9,13},{10,... | collective-permute-start | bytes 1769480 | tf_op jit(solution)/shard_map/ppermute | solution.py:667
  509.1 20.6 %collective-permute-start.68 = (bf16[64,1536]{1,0:T(8,128)(2,1)S(1)}, bf16[64,1536]{1,0:T(8,128)(2,1)S(1)}, u32[]{:S(2)}, u32[]{:S(2)}) collective-permute-start(bf16[64,1536]{1,0:T(8,128)(2,1)S(1)} %get-tuple-element.249), channel_id=1, source_target_pairs={{0,8},{1,9},{2,10},{3,11},{4,12},{5,13},{6,14},{7,15},{8,0},{9,1},... | collective-permute-start | bytes 589832 | tf_op jit(solution)/shard_map/ppermute | solution.py:667
  542.8 23.7 %collective-permute-start.76 = (bf16[128,1536]{1,0:T(8,128)(2,1)}, bf16[128,1536]{1,0:T(8,128)(2,1)S(1)}, u32[]{:S(2)}, u32[]{:S(2)}) collective-permute-start(bf16[128,1536]{1,0:T(8,128)(2,1)} %get-tuple-element.269.refs_0_), channel_id=1, source_target_pairs={{0,2},{1,3},{2,0},{3,1},{4,6},{5,7},{6,4},{7,5},{8,10},{9,11},{10,... | collective-permute-start | bytes 1179656 | tf_op jit(solution)/shard_map/ppermute | solution.py:667
  543.2 23.3 %collective-permute-start.77 = (bf16[128,1536]{1,0:T(8,128)(2,1)}, bf16[128,1536]{1,0:T(8,128)(2,1)S(1)}, u32[]{:S(2)}, u32[]{:S(2)}) collective-permute-start(bf16[128,1536]{1,0:T(8,128)(2,1)} %get-tuple-element.269.refs_0_), channel_id=1, source_target_pairs={{0,8},{1,9},{2,10},{3,11},{4,12},{5,13},{6,14},{7,15},{8,0},{9,1},... | collective-permute-start | bytes 1179656 | tf_op jit(solution)/shard_map/ppermute | solution.py:667
  576.9 40.2 %collective-permute-start.94 = (bf16[2,64,1536]{2,1,0:T(8,128)(2,1)}, bf16[2,64,1536]{2,1,0:T(8,128)(2,1)}, u32[]{:S(2)}, u32[]{:S(2)}) collective-permute-start(bf16[2,64,1536]{2,1,0:T(8,128)(2,1)} %maximum_select_fusion.4), channel_id=1, source_target_pairs={{0,1},{1,0},{2,3},{3,2},{4,5},{5,4},{6,7},{7,6},{8,9},{9,8},{10,11... | collective-permute-start | bytes 1179656 | tf_op jit(solution)/shard_map/ppermute | solution.py:667
  607.8 65.1 %collective-permute-start.93 = (bf16[2,48,1536]{2,1,0:T(8,128)(2,1)}, bf16[2,48,1536]{2,1,0:T(8,128)(2,1)}, u32[]{:S(2)}, u32[]{:S(2)}) collective-permute-start(bf16[2,48,1536]{2,1,0:T(8,128)(2,1)} %fusion.38), channel_id=1, source_target_pairs={{0,2},{1,3},{2,0},{3,1},{4,6},{5,7},{6,4},{7,5},{8,10},{9,11},{10,... | collective-permute-start | bytes 884744 | tf_op jit(solution)/shard_map/ppermute | solution.py:667
  608.3 60.0 %collective-permute-start.95 = (bf16[2,64,1536]{2,1,0:T(8,128)(2,1)}, bf16[2,64,1536]{2,1,0:T(8,128)(2,1)}, u32[]{:S(2)}, u32[]{:S(2)}) collective-permute-start(bf16[2,64,1536]{2,1,0:T(8,128)(2,1)} %collective-permute-done.85), channel_id=1, source_target_pairs={{0,1},{1,0},{2,3},{3,2},{4,5},{5,4},{6,7},{7,6},{8,9},{9,8},{10,11... | collective-permute-start | bytes 1179656 | tf_op jit(solution)/shard_map/ppermute | solution.py:667
  613.4 29.6 %collective-permute-start.87 = (bf16[512,768]{1,0:T(8,128)(2,1)}, bf16[512,768]{1,0:T(8,128)(2,1)}, u32[]{:S(2)}, u32[]{:S(2)}) collective-permute-start(bf16[512,768]{1,0:T(8,128)(2,1)} %slice.898), channel_id=1, source_target_pairs={{0,4},{1,5},{2,6},{3,7},{4,0},{5,1},{6,2},{7,3},{8,12},{9,13},{10,... | collective-permute-start | bytes 2359304 | tf_op jit(solution)/shard_map/ppermute | solution.py:667
  616.2 28.1 %collective-permute-start.88 = (bf16[192,2240]{1,0:T(8,128)(2,1)S(1)}, bf16[192,2240]{1,0:T(8,128)(2,1)S(1)}, u32[]{:S(2)}, u32[]{:S(2)}) collective-permute-start(bf16[192,2240]{1,0:T(8,128)(2,1)S(1)} %get-tuple-element.387), channel_id=1, source_target_pairs={{1,8},{3,10},{5,12},{7,14},{8,1},{10,3},{12,5},{14,7},{17,24},{19,... | collective-permute-start | bytes 2580488 | tf_op jit(solution)/shard_map/ppermute | solution.py:673
  620.6 41.2 %collective-permute-start.89 = (bf16[192,2240]{1,0:T(8,128)(2,1)S(1)}, bf16[192,2240]{1,0:T(8,128)(2,1)S(1)}, u32[]{:S(2)}, u32[]{:S(2)}) collective-permute-start(bf16[192,2240]{1,0:T(8,128)(2,1)S(1)} %get-tuple-element.386), channel_id=1, source_target_pairs={{0,16},{1,24},{2,18},{3,26},{4,20},{5,28},{6,22},{7,30},{8,17},{9,... | collective-permute-start | bytes 2580488 | tf_op jit(solution)/shard_map/ppermute | solution.py:680
  696.3 21.8 %collective-permute-start.101 = (bf16[1,1,2,192,1152]{4,3,2,1,0:T(8,128)(2,1)}, bf16[1,1,2,192,1152]{4,3,2,1,0:T(8,128)(2,1)}, u32[]{:S(2)}, u32[]{:S(2)}) collective-permute-start(bf16[1,1,2,192,1152]{4,3,2,1,0:T(8,128)(2,1)} %constant_dynamic-slice_fusion.1), channel_id=1, source_target_pairs={{0,4},{1,5},{2,6},{3,7},{4,0},{5,1},{6,2},{7,3},{8,12},{9,13},{10,... | collective-permute-start | bytes 2654216 | tf_op jit(solution)/shard_map/ppermute | solution.py:667
  699.1 21.6 %collective-permute-start.99 = (bf16[128,1536]{1,0:T(8,128)(2,1)S(1)}, bf16[128,1536]{1,0:T(8,128)(2,1)S(1)}, u32[]{:S(2)}, u32[]{:S(2)}) collective-permute-start(bf16[128,1536]{1,0:T(8,128)(2,1)S(1)} %get-tuple-element.306), channel_id=1, source_target_pairs={{0,2},{1,3},{2,0},{3,1},{4,6},{5,7},{6,4},{7,5},{8,10},{9,11},{10,... | collective-permute-start | bytes 1179656 | tf_op jit(solution)/shard_map/ppermute | solution.py:667
  700.2 20.5 %collective-permute-start.100 = (bf16[128,1536]{1,0:T(8,128)(2,1)S(1)}, bf16[128,1536]{1,0:T(8,128)(2,1)S(1)}, u32[]{:S(2)}, u32[]{:S(2)}) collective-permute-start(bf16[128,1536]{1,0:T(8,128)(2,1)S(1)} %get-tuple-element.307), channel_id=1, source_target_pairs={{0,8},{1,9},{2,10},{3,11},{4,12},{5,13},{6,14},{7,15},{8,0},{9,1},... | collective-permute-start | bytes 1179656 | tf_op jit(solution)/shard_map/ppermute | solution.py:667
  724.0 21.2 %collective-permute-start.102 = (bf16[112,1536]{1,0:T(8,128)(2,1)S(1)}, bf16[112,1536]{1,0:T(8,128)(2,1)S(1)}, u32[]{:S(2)}, u32[]{:S(2)}) collective-permute-start(bf16[112,1536]{1,0:T(8,128)(2,1)S(1)} %pad_maximum_fusion.9), channel_id=1, source_target_pairs={{0,16},{1,17},{2,18},{3,19},{4,20},{5,21},{6,22},{7,23},{8,24},{9,... | collective-permute-start | bytes 1032200 | tf_op jit(solution)/shard_map/ppermute | solution.py:667
  726.9 62.9 %collective-permute-start.116 = (bf16[192,2240]{1,0:T(8,128)(2,1)}, bf16[192,2240]{1,0:T(8,128)(2,1)}, u32[]{:S(2)}, u32[]{:S(2)}) collective-permute-start(bf16[192,2240]{1,0:T(8,128)(2,1)} %reduce-scatter.8.cloned.1.call-done), channel_id=1, source_target_pairs={{1,8},{3,10},{5,12},{7,14},{8,1},{10,3},{12,5},{14,7},{17,24},{19,... | collective-permute-start | bytes 2580488 | tf_op jit(solution)/shard_map/ppermute | solution.py:673
  746.1 45.1 %collective-permute-start.103 = (bf16[2,112,1536]{2,1,0:T(8,128)(2,1)}, bf16[2,112,1536]{2,1,0:T(8,128)(2,1)}, u32[]{:S(2)}, u32[]{:S(2)}) collective-permute-start(bf16[2,112,1536]{2,1,0:T(8,128)(2,1)} %maximum_select_fusion.2), channel_id=1, source_target_pairs={{0,1},{1,0},{2,3},{3,2},{4,5},{5,4},{6,7},{7,6},{8,9},{9,8},{10,11... | collective-permute-start | bytes 2064392 | tf_op jit(solution)/shard_map/ppermute | solution.py:667
  746.1 46.1 %collective-permute-start.104 = (bf16[2,112,1536]{2,1,0:T(8,128)(2,1)}, bf16[2,112,1536]{2,1,0:T(8,128)(2,1)}, u32[]{:S(2)}, u32[]{:S(2)}) collective-permute-start(bf16[2,112,1536]{2,1,0:T(8,128)(2,1)} %maximum_select_fusion.2), channel_id=1, source_target_pairs={{0,2},{1,3},{2,0},{3,1},{4,6},{5,7},{6,4},{7,5},{8,10},{9,11},{10,... | collective-permute-start | bytes 2064392 | tf_op jit(solution)/shard_map/ppermute | solution.py:667
  749.4 33.9 %collective-permute-start.112 = (bf16[192,1152]{1,0:T(8,128)(2,1)}, bf16[192,1152]{1,0:T(8,128)(2,1)}, u32[]{:S(2)}, u32[]{:S(2)}) collective-permute-start(bf16[192,1152]{1,0:T(8,128)(2,1)} %get-tuple-element.402), channel_id=1, source_target_pairs={{0,16},{1,24},{2,18},{3,26},{4,20},{5,28},{6,22},{7,30},{8,17},{9,... | collective-permute-start | bytes 1327112 | tf_op jit(solution)/shard_map/ppermute | solution.py:680
  783.3 35.2 %collective-permute-start.115 = (bf16[192,1920]{1,0:T(8,128)(2,1)}, bf16[192,1920]{1,0:T(8,128)(2,1)}, u32[]{:S(2)}, u32[]{:S(2)}) collective-permute-start(bf16[192,1920]{1,0:T(8,128)(2,1)} %get-tuple-element.398), channel_id=1, source_target_pairs={{0,16},{1,24},{2,18},{3,26},{4,20},{5,28},{6,22},{7,30},{8,17},{9,... | collective-permute-start | bytes 2211848 | tf_op jit(solution)/shard_map/ppermute | solution.py:680
  783.3 35.2 %collective-permute-start.114 = (bf16[192,1920]{1,0:T(8,128)(2,1)S(1)}, bf16[192,1920]{1,0:T(8,128)(2,1)}, u32[]{:S(2)}, u32[]{:S(2)}) collective-permute-start(bf16[192,1920]{1,0:T(8,128)(2,1)S(1)} %get-tuple-element.397), channel_id=1, source_target_pairs={{1,8},{3,10},{5,12},{7,14},{8,1},{10,3},{12,5},{14,7},{17,24},{19,... | collective-permute-start | bytes 2211848 | tf_op jit(solution)/shard_map/ppermute | solution.py:673
  793.3 28.4 %collective-permute-start.105 = (bf16[2,112,1536]{2,1,0:T(8,128)(2,1)}, bf16[2,112,1536]{2,1,0:T(8,128)(2,1)S(1)}, u32[]{:S(2)}, u32[]{:S(2)}) collective-permute-start(bf16[2,112,1536]{2,1,0:T(8,128)(2,1)} %collective-permute-done.104), channel_id=1, source_target_pairs={{0,1},{1,0},{2,3},{3,2},{4,5},{5,4},{6,7},{7,6},{8,9},{9,8},{10,11... | collective-permute-start | bytes 2064392 | tf_op jit(solution)/shard_map/ppermute | solution.py:667
  (253 other events, 2686.3 us)
Sparse Core Ops, SparseCore 0:
  34.6 30.0 all-gather.9
  99.6 29.3 all-gather.11
  193.8 25.1 all-gather.13
  221.3 78.4 all-gather.17
  302.0 77.2 all-gather.15
  397.9 62.0 reduce-scatter.3
  464.0 102.7 reduce-scatter.7
  603.9 62.5 reduce-scatter.5
